TPU v7x, 32 devices: a whole 2x2x4 slice. The times are simulated.
32 devices in a mesh: row: 8 (over z, x), col: 4 (over y, core).
Axes of the slice: x: 2, y: 2, z: 4, core: 2. Of those that a mesh axis runs over, the one named last changes fastest.
Arguments:
- tokens: bfloat16 [2048, 8192], P('row', 'col'), may hold values from -6 to 6
- weight: bfloat16 [8192, 16384], P('col', 'row'), may hold values from -0.0625 to 0.0625
- grad: bfloat16 [8192, 16384], P('col', 'row'), may hold values from -0.0625 to 0.0625
- roots: bfloat16 [2, 8, 2, 16, 1024, 1024], P(None, 'col', None, 'row')
- owner: int32 [8, 16], replicated, may hold values from 0 to 7, as said below
Outputs:
- new_weight: bfloat16 [8192, 16384], P('col', 'row')
- output: bfloat16 [2048, 16384], P('col', 'row')
Inputs may be any that keep to these rules, and one draw needn't show every extreme that they name: owner[p, q] is the block's home q // 2 or the next index (q // 2 + 1) mod 8; in every draw some index along row keeps the roots of all blocks of its own home and of the previous home.
All inputs are finite; a program needn't handle non-finite values.
Results may differ from a plain program's by a relative error of at most 0.013.
Values may be sent and summed in bfloat16 or wider, within the bound.
No kernel may reach another device: no remote copies, remote signals or barrier semaphores. Data moves between devices by JAX's collectives and lax.ppermute only.
A program may use at most 256 MiB of HBM per device.

v0:
```python
import jax
import jax.numpy as jnp
from jax import lax
from jax.sharding import PartitionSpec as P

step_size = 0.5


def from_behind(block, axis, distance):
    devices = range(lax.axis_size(axis))
    route = [((i - distance) % len(devices), i) for i in devices]
    return lax.ppermute(block, axis, route)


def to_blocks(matrix, block_width):
    blocks_down = matrix.shape[0] // block_width
    blocks_across = matrix.shape[1] // block_width
    return matrix.reshape(blocks_down, block_width, blocks_across, block_width).transpose(
        0, 2, 1, 3
    )


def from_blocks(blocks):
    blocks_down, blocks_across, block_width, block_height = blocks.shape
    return blocks.transpose(0, 2, 1, 3).reshape(
        blocks_down * block_width, blocks_across * block_height
    )


def precondition(left_root, grad_block, right_root):
    mixed_rows = jnp.einsum(
        "...ab,...bc->...ac", left_root, grad_block, preferred_element_type=jnp.float32
    ).astype(jnp.bfloat16)
    return jnp.einsum(
        "...ab,...bc->...ac", mixed_rows, right_root, preferred_element_type=jnp.float32
    )


def on_device(tokens, weight, grad, roots, owner):
    block_width = roots.shape[-1]
    blocks_down = weight.shape[0] // block_width
    blocks_across = weight.shape[1] // block_width
    row_place = lax.axis_index("row")
    col_place = lax.axis_index("col")
    row_count = lax.axis_size("row")
    previous = jnp.mod(row_place - 1 + row_count, row_count)
    own_owner = lax.dynamic_slice(
        owner, (col_place * blocks_down, row_place * blocks_across), (blocks_down, blocks_across)
    )
    prior_owner = lax.dynamic_slice(
        owner, (col_place * blocks_down, previous * blocks_across), (blocks_down, blocks_across)
    )
    kept_home = own_owner == row_place
    taken_over = prior_owner == row_place
    grad_blocks = to_blocks(grad, block_width)

    def when_owned(flag, left_root, grad_block, right_root):
        return lax.cond(
            flag,
            lambda: precondition(left_root, grad_block, right_root),
            lambda: jnp.zeros((block_width, block_width), jnp.float32),
        )

    from_prior = from_behind(grad_blocks, "row", 1)
    home_list = []
    lent_list = []
    for down_index in range(blocks_down):
        for across_index in range(blocks_across):
            home_list.append(
                when_owned(
                    kept_home[down_index, across_index],
                    roots[0, down_index, 0, across_index],
                    grad_blocks[down_index, across_index],
                    roots[1, down_index, 0, across_index],
                )
            )
            lent_list.append(
                when_owned(
                    taken_over[down_index, across_index],
                    roots[0, down_index, 1, across_index],
                    from_prior[down_index, across_index],
                    roots[1, down_index, 1, across_index],
                )
            )
    home_part = jnp.stack(home_list).reshape(blocks_down, blocks_across, block_width, block_width)
    lent_part = jnp.stack(lent_list).reshape(blocks_down, blocks_across, block_width, block_width)
    returned = from_behind(lent_part.astype(jnp.bfloat16), "row", -1).astype(lent_part.dtype)
    update = jnp.where(kept_home[:, :, None, None], home_part, returned)
    new_weight = (weight.astype(jnp.float32) - step_size * from_blocks(update)).astype(jnp.bfloat16)
    gathered = lax.all_gather(tokens, "row", axis=0, tiled=True)
    output = lax.psum_scatter(
        jnp.dot(gathered, new_weight, preferred_element_type=jnp.float32).astype(jnp.bfloat16),
        "col",
        scatter_dimension=0,
        tiled=True,
    )
    return (new_weight, output)


def solution(mesh):
    placed = (
        P("row", "col"),
        P("col", "row"),
        P("col", "row"),
        P(None, "col", None, "row", None, None),
        P(),
    )
    return jax.shard_map(
        on_device,
        mesh=mesh,
        in_specs=placed,
        out_specs=(P("col", "row"), P("col", "row")),
        check_vma=False,
    )
```

profile of v0, /device:TPU:0, one launch (start us, length us, event | category | flops | bytes accessed | tf_op | source)
XLA Modules:
  0.0 725.8 jit_solution(13600053533474247549)
XLA Ops:
  7.2 0.0 copy-start
  7.2 0.0 all-gather.2.cloned.1.call-start
  7.2 14.4 %reshape.32 = bf16[2,1024,2,1024]{3,2,1,0:T(2,128)(2,1)} reshape(bf16[2048,2048]{1,0:T(8,128)(2,1)} %param.23) | data formatting | bytes 16777216 | tf_op jit(solution)/shard_map/reshape | solution.py:18
  21.6 2.9 collective-permute-start
  24.6 0.0 all-gather.2.cloned.1.call-update
  24.6 0.0 reduce-scatter.2.cloned.1.call-start
  24.7 0.0 copy-done
  24.7 0.1 dynamic-slice_compare_fusion
  24.8 0.7 fusion.129
  27.9 281.7 %collective-permute-done = bf16[2,2,1024,1024]{3,1,2,0:T(2,128)(2,1)} collective-permute-done((bf16[2,2,1024,1024]{3,1,2,0:T(2,128)(2,1)}, bf16[2,2,1024,1024]{3,1,2,0:T(2,128)(2,1)}, u32[]{:S(2)}, u32[]{:S(2)}) %collective-permute-start) | collective-permute-done | bytes 8388640 | tf_op jit(solution)/shard_map/ppermute | solution.py:12
  309.6 9.4 %copy.14 = bf16[2,2,1024,1024]{3,2,1,0:T(8,128)(2,1)} copy(bf16[2,2,1024,1024]{3,1,2,0:T(2,128)(2,1)} %collective-permute-done) | data formatting | bytes 16777216 | tf_op jit(solution)/shard_map/cond | solution.py:58
  318.9 0.3 conditional.12
  318.9 0.3 stack.53
  319.2 1.6 conditional.13
  319.2 1.6 stack.55
  320.8 1.7 conditional.14
  320.8 1.6 stack.57
  322.6 1.6 conditional.15
  322.6 1.6 stack.59
  324.2 3.8 pad_maximum_fusion.1
  328.0 29.4 %copy.18 = bf16[2,2,1024,1024]{3,1,2,0:T(2,128)(2,1)} copy(bf16[2,2,1024,1024]{3,2,1,0:T(8,128)(2,1)S(1)} %bitcast.176) | data formatting | bytes 16777216 | tf_op jit(solution)/shard_map/convert_element_type | solution.py:87
  357.4 27.9 %collective-permute-start.1 = (bf16[2,2,1024,1024]{3,1,2,0:T(2,128)(2,1)}, bf16[2,2,1024,1024]{3,1,2,0:T(2,128)(2,1)}, u32[]{:S(2)}, u32[]{:S(2)}) collective-permute-start(bf16[2,2,1024,1024]{3,1,2,0:T(2,128)(2,1)} %copy.18), channel_id=1, source_target_pairs={{4,0},{8,4},{12,8},{16,12},{20,16},{24,20},{28,24},{0,28},{5,1},{9... | collective-permute-start | bytes 25165832 | tf_op jit(solution)/shard_map/ppermute | solution.py:12
  385.3 9.4 %copy.10 = bf16[2,2,1024,1024]{3,2,1,0:T(8,128)(2,1)} copy(bf16[2,2,1024,1024]{3,1,2,0:T(2,128)(2,1)} %bitcast.175) | data formatting | bytes 16777216 | tf_op jit(solution)/shard_map/cond | solution.py:58
  397.1 2.7 conditional.10
  397.1 2.5 stack.49
  399.8 9.4 %conditional.11 = (f32[1,1024,1024]{2,1,0:T(8,128)}) conditional(s32[]{:T(128)} %bitcast.36, () %tuple.76, (bf16[2,2,2,2,1024,1024]{5,4,3,2,1,0:T(8,128)(2,1)}, bf16[2,2,1024,1024]{3,2,1,0:T(8,128)(2,1)}) %tuple.84), branch_computations={%region_6.7_spmd, %region_7.8_spmd} | conditional | flops 4296015872 | bytes 10485768 | solution.py:58
  399.8 9.4 %convolution_bitcast_fusion.3 = f32[1,1024,1024]{2,1,0:T(8,128)} fusion(bf16[2,2,2,2,1024,1024]{5,4,3,2,1,0:T(8,128)(2,1)} %get-tuple-element.126, bf16[2,2,1024,1024]{3,2,1,0:T(8,128)(2,1)} %get-tuple-element.127), kind=kOutput, calls=%fused_computation.27 | convolution fusion | flops 4296015872 | bytes 10485760 | tf_op jit(solution)/shard_map/cond/branch_1_fun/...ab,...bc->...ac/dot_general | solution.py:34
  409.2 2.6 conditional.8
  409.2 2.6 stack.45
  411.8 9.6 %conditional.9 = (f32[1,1024,1024]{2,1,0:T(8,128)}) conditional(s32[]{:T(128)} %bitcast.34, () %tuple.74, (bf16[2,2,2,2,1024,1024]{5,4,3,2,1,0:T(8,128)(2,1)}, bf16[2,2,1024,1024]{3,2,1,0:T(8,128)(2,1)}) %tuple.84), branch_computations={%region_2.3_spmd, %region_3.4_spmd} | conditional | flops 4296015872 | bytes 10485768 | solution.py:58
  411.8 9.4 %convolution_bitcast_fusion.1 = f32[1,1024,1024]{2,1,0:T(8,128)} fusion(bf16[2,2,2,2,1024,1024]{5,4,3,2,1,0:T(8,128)(2,1)} %get-tuple-element.122, bf16[2,2,1024,1024]{3,2,1,0:T(8,128)(2,1)} %get-tuple-element.123), kind=kOutput, calls=%fused_computation.9 | convolution fusion | flops 4296015872 | bytes 10485760 | tf_op jit(solution)/shard_map/cond/branch_1_fun/...ab,...bc->...ac/dot_general | solution.py:34
  421.4 6.4 pad_maximum_fusion
  427.8 136.9 %collective-permute-done.1 = bf16[2,2,1024,1024]{3,1,2,0:T(2,128)(2,1)} collective-permute-done((bf16[2,2,1024,1024]{3,1,2,0:T(2,128)(2,1)}, bf16[2,2,1024,1024]{3,1,2,0:T(2,128)(2,1)}, u32[]{:S(2)}, u32[]{:S(2)}) %collective-permute-start.1) | collective-permute-done | bytes 8388640 | tf_op jit(solution)/shard_map/ppermute | solution.py:12
  564.8 33.0 %fusion.128 = f32[2,2,1024,1024]{3,1,2,0:T(2,128)} fusion(f32[2,2,1024,1024]{3,2,1,0:T(8,128)S(1)} %bitcast.171, bf16[2,2,1024,1024]{3,1,2,0:T(2,128)(2,1)} %collective-permute-done.1, pred[2,2]{1,0:T(4,128)(4,1)S(1)} %get-tuple-element.159), kind=kLoop, calls=%fused_computation.74 | loop fusion | flops 12582912 | bytes 41943044 | tf_op jit(solution)/shard_map/mul | solution.py:89
  597.8 11.0 %copy.21 = f32[256,8,2,1024]{3,1,2,0:T(8,128)S(1)} copy(f32[256,8,2,1024]{3,2,1,0:T(2,128)} %bitcast.172) | data formatting | bytes 33554432
  608.8 8.4 %subtract_convert_fusion = bf16[2048,2048]{1,0:T(8,128)(2,1)} fusion(f32[2048,2048]{1,0:T(8,128)S(1)} %bitcast.173, bf16[2048,2048]{1,0:T(8,128)(2,1)} %param.22), kind=kLoop, calls=%fused_computation.75 | loop fusion | flops 12582912 | bytes 33554432 | tf_op jit(solution)/shard_map/convert_element_type | solution.py:89
  617.2 0.0 all-gather.2.cloned.1.call-done
  617.2 23.9 %convert_bitcast_fusion = bf16[2048,2048]{0,1:T(8,128)(2,1)} fusion(bf16[2048,2048]{1,0:T(8,128)(2,1)} %subtract_convert_fusion, bf16[2048,2048]{1,0:T(8,128)(2,1)} %all-gather.2.cloned.1.call-done), kind=kOutput, calls=%fused_computation.77 | convolution fusion | flops 17184063488 | bytes 25165824 | tf_op jit(solution)/shard_map/dot_general | solution.py:92
  641.1 0.0 reduce-scatter.2.cloned.1.call-update
  641.1 73.5 %reduce-scatter.2.cloned.1.call-done = bf16[512,2048]{0,1:T(8,128)(2,1)} async-done(((bf16[2048,2048]{0,1:T(8,128)(2,1)}), bf16[512,2048]{0,1:T(8,128)(2,1)}) %reduce-scatter.2.cloned.1.call-update) | async-done | bytes 2097168 | tf_op jit(solution)/shard_map/reduce_scatter | solution.py:91
  714.6 3.9 copy.20
Async XLA Ops:
  7.2 17.5 %copy-start = (s32[8,16]{1,0:T(8,128)S(1)}, s32[8,16]{1,0:T(8,128)}, u32[]{:S(2)}) copy-start(s32[8,16]{1,0:T(8,128)} %param.25) | copy-start | bytes 1540
  7.2 610.0 %all-gather.2.cloned.1.call-start = ((), (), s32[]{:S(2)}) async-start(), calls=%async_computation.1 | async-start | bytes 9437184 | tf_op jit(solution)/shard_map/all_gather | solution.py:90
  21.6 287.9 %collective-permute-start = (bf16[2,2,1024,1024]{3,1,2,0:T(2,128)(2,1)}, bf16[2,2,1024,1024]{3,1,2,0:T(2,128)(2,1)}, u32[]{:S(2)}, u32[]{:S(2)}) collective-permute-start(bf16[2,2,1024,1024]{3,1,2,0:T(2,128)(2,1)} %bitcast.174), channel_id=1, source_target_pairs={{28,0},{0,4},{4,8},{8,12},{12,16},{16,20},{20,24},{24,28},{29,1},{... | collective-permute-start | bytes 25165832 | tf_op jit(solution)/shard_map/ppermute | solution.py:12
  24.6 690.0 %reduce-scatter.2.cloned.1.call-start = ((), (), s32[]{:S(2)}) async-start(), calls=%async_computation.2 | async-start | bytes 10485760 | tf_op jit(solution)/shard_map/reduce_scatter | solution.py:91
  357.4 207.4 %collective-permute-start.1 = (bf16[2,2,1024,1024]{3,1,2,0:T(2,128)(2,1)}, bf16[2,2,1024,1024]{3,1,2,0:T(2,128)(2,1)}, u32[]{:S(2)}, u32[]{:S(2)}) collective-permute-start(bf16[2,2,1024,1024]{3,1,2,0:T(2,128)(2,1)} %copy.18), channel_id=1, source_target_pairs={{4,0},{8,4},{12,8},{16,12},{20,16},{24,20},{28,24},{0,28},{5,1},{9... | collective-permute-start | bytes 25165832 | tf_op jit(solution)/shard_map/ppermute | solution.py:12
Sparse Core Ops, SparseCore 0:
  24.7 203.7 all-gather.1
  641.2 73.3 reduce-scatter.1
where the time goes:
time: 734 us; the launch traced here: 726 us
  waiting for transfers between devices  492 us (67%)
  local copies, waits for them, and re-layouts  88.2 us (12%)
  other arithmetic  51.7 us (7%)
  matrix products  42.6 us (6%)
  starting transfers between devices  30.9 us (4%)
  between operations  19.5 us (3%)
    ppermute x2, waiting for transfers between devices, from_behind(): return lax.ppermute(block, axis, route)  419 us
    reduce_scatter x1, waiting for transfers between devices, on_device(): lax.psum_scatter(jnp.dot(gathered, new_weight, preferred_element_type=jnp...  73.5 us
    mul x1, other arithmetic, on_device(): step_size * from_blocks(update)  33 us
    ppermute x2, starting transfers between devices, from_behind(): return lax.ppermute(block, axis, route)  30.8 us
    convert_element_type x1, local copies, waits for them, and re-layouts, on_device(): lent_part.astype(jnp.bfloat16)  29.4 us
    dot_general x1, matrix products, on_device(): jnp.dot(gathered, new_weight, preferred_element_type=jnp.float32)  23.9 us
    dot_general x2, matrix products, precondition(): jnp.einsum('...ab,...bc->...ac', mixed_rows, right_root, preferred_elemen...  18.7 us
    cond x2, local copies, waits for them, and re-layouts, when_owned(): lax.cond(flag, lambda: precondition(left_root, grad_block, right_root), l...  18.7 us
  transfers between devices with their start and end apart: 4, of which 3 were waited for; matrix products, arithmetic and copies ran while one was open for 19% of the time, Pallas kernels for 0%

commit v1 on v0

v1 whole, which is shorter than its diff:
```python
import jax
import jax.numpy as jnp
from jax import lax
from jax.experimental import pallas as pl
from jax.experimental.pallas import tpu as pltpu
from jax.sharding import PartitionSpec as P

step_size = 0.5


def shift_route(count, distance):
    return [(i, (i + distance) % count) for i in range(count)]


def pair_route(count):
    return [(i, i ^ 1) for i in range(count)]


def after(value, *others):
    return lax.optimization_barrier((value,) + others)[0]


def precondition(flags, roots, slot, q, grads, grads_q, kind):
    width = roots.shape[-1]
    down = grads.shape[0] // width
    tile = min(width, 256)

    def kernel(flag_ref, left_ref, grad_ref, right_ref, out_ref):
        @pl.when(flag_ref[pl.program_id(0)] != 0)
        def _():
            @pl.loop(0, width // tile)
            def _(i):
                rows = pl.ds(pl.multiple_of(i * tile, tile), tile)
                mixed = jnp.dot(left_ref[rows, :], grad_ref[...], preferred_element_type=jnp.float32)
                update = jnp.dot(mixed.astype(jnp.bfloat16), right_ref[...], preferred_element_type=jnp.float32)
                out_ref[rows, :] = update.astype(kind)

        @pl.when(flag_ref[pl.program_id(0)] == 0)
        def _():
            out_ref[...] = jnp.zeros_like(out_ref)

    def root_spec(side):
        return pl.BlockSpec((None, None, None, None, width, width), lambda p, f: (side, p, slot, q, 0, 0))

    size = 2 if kind == jnp.bfloat16 else 4
    return pl.pallas_call(
        kernel,
        out_shape=jax.ShapeDtypeStruct((down * width, width), kind),
        grid_spec=pltpu.PrefetchScalarGridSpec(
            num_scalar_prefetch=1,
            grid=(down,),
            in_specs=[root_spec(0), pl.BlockSpec((width, width), lambda p, f: (p, grads_q)), root_spec(1)],
            out_specs=pl.BlockSpec((width, width), lambda p, f: (p, 0)),
        ),
        compiler_params=pltpu.CompilerParams(vmem_limit_bytes=40 << 20),
        cost_estimate=pl.CostEstimate(
            flops=down * 4 * width**3, bytes_accessed=down * width * width * (6 + size), transcendentals=0
        ),
        name="precondition",
    )(flags, roots, grads, roots)


def gather_tokens(tokens, row_count, row_place):
    rows = tokens.shape[0]
    other = lax.ppermute(tokens, "row", pair_route(row_count))
    low = jnp.mod(row_place, 2) == 0
    pair = jnp.concatenate([jnp.where(low, tokens, other), jnp.where(low, other, tokens)], axis=0)
    pairs = row_count // 2
    place = row_place // 2
    gathered = jnp.zeros((rows * row_count, tokens.shape[1]), tokens.dtype)

    def put(whole, piece, index):
        return lax.dynamic_update_slice(whole, piece, (jnp.mod(index, pairs) * (2 * rows), 0))

    gathered = put(gathered, pair, place)
    up = below = pair
    for step in range(1, pairs // 2 + 1):
        up = lax.ppermute(up, "row", shift_route(row_count, 2))
        gathered = put(gathered, up, place - step)
        if step <= (pairs - 1) // 2:
            below = lax.ppermute(below, "row", shift_route(row_count, -2))
            gathered = put(gathered, below, place + step)
    return gathered


def pair_sum(terms, col_count, col_place):
    rows = terms.shape[0] // col_count
    terms = terms.reshape(col_count // 2, 2, rows, terms.shape[1])
    core = jnp.mod(col_place, 2)
    mine = lax.dynamic_index_in_dim(terms, core, 1, keepdims=False)
    others = lax.dynamic_index_in_dim(terms, 1 - core, 1, keepdims=False)
    came = lax.ppermute(others, "col", pair_route(col_count))
    return mine.astype(jnp.float32) + came.astype(jnp.float32)


def far_sum(halves, col_count, col_place):
    groups = col_count // 2
    place = col_place // 2
    total = lax.dynamic_index_in_dim(halves, place, 0, keepdims=False)
    sent = halves.astype(jnp.bfloat16)
    for step in range(1, groups):
        piece = lax.dynamic_index_in_dim(sent, jnp.mod(place + step, groups), 0, keepdims=False)
        total = total + lax.ppermute(piece, "col", shift_route(col_count, 2 * step)).astype(jnp.float32)
    return total.astype(jnp.bfloat16)


def on_device(tokens, weight, grad, roots, owner):
    width = roots.shape[-1]
    down = weight.shape[0] // width
    across = weight.shape[1] // width
    row_place = lax.axis_index("row")
    col_place = lax.axis_index("col")
    row_count = lax.axis_size("row")
    col_count = lax.axis_size("col")
    previous = jnp.mod(row_place - 1 + row_count, row_count)
    own_owner = lax.dynamic_slice(owner, (col_place * down, row_place * across), (down, across))
    prior_owner = lax.dynamic_slice(owner, (col_place * down, previous * across), (down, across))
    kept = (own_owner == row_place).astype(jnp.int32)
    taken = (prior_owner == row_place).astype(jnp.int32)
    forth = shift_route(row_count, 1)
    back = shift_route(row_count, -1)

    came = []
    for q in range(across):
        column = grad[:, q * width:(q + 1) * width]
        came.append(lax.ppermute(column if q == 0 else after(column, came[q - 1]), "row", forth))
    all_tokens = gather_tokens(tokens, row_count, row_place)

    new_weight = jnp.zeros_like(weight)
    output = jnp.zeros((all_tokens.shape[0] // col_count, weight.shape[1]), jnp.bfloat16)
    returned = []
    homes = []
    for q in range(across):
        flags = kept[:, q] if q == 0 else after(kept[:, q], lent)
        homes.append(precondition(flags, roots, 0, q, grad, q, jnp.float32))
        lent = precondition(taken[:, q], roots, 1, q, after(came[q], homes[q]) if q == 0 else came[q], 0, jnp.bfloat16)
        cuts = [0, width] if q < across - 1 else [0, width // 2, width * 3 // 4, width]
        last = None
        for start, stop in zip(cuts[:-1], cuts[1:]):
            piece = lent[:, start:stop]
            if last is not None:
                piece = after(piece, last)
            last = lax.ppermute(piece, "row", back)
            returned.append((q, start, stop, last))
    gate = None
    for q, start, stop, piece in returned:
        if gate is not None:
            piece = after(piece, gate)
        at = q * width + start
        flags = jnp.repeat(kept[:, q] != 0, width)[:, None]
        update = jnp.where(flags, homes[q][:, start:stop], piece.astype(jnp.float32))
        fresh = (weight[:, at:at + stop - start].astype(jnp.float32) - step_size * update).astype(jnp.bfloat16)
        new_weight = lax.dynamic_update_slice(new_weight, fresh, (0, at))
        terms = jnp.dot(all_tokens, fresh, preferred_element_type=jnp.float32).astype(jnp.bfloat16)
        halves = pair_sum(terms, col_count, col_place)
        gate = halves
        output = lax.dynamic_update_slice(output, far_sum(halves, col_count, col_place), (0, at))
    return new_weight, output


def solution(mesh):
    placed = (
        P("row", "col"),
        P("col", "row"),
        P("col", "row"),
        P(None, "col", None, "row", None, None),
        P(),
    )
    return jax.shard_map(
        on_device,
        mesh=mesh,
        in_specs=placed,
        out_specs=(P("col", "row"), P("col", "row")),
        check_vma=False,
    )
```

time: 734 us -> 512 us (0.70)
  waiting for transfers between devices: 492 us -> 339 us
  local copies, waits for them, and re-layouts: 88.2 us -> 45.8 us
  Pallas kernels: 0 us -> 41.9 us
  other arithmetic: 51.7 us -> 25.6 us
  matrix products: 42.6 us -> 21.9 us
  between operations: 19.5 us -> 1.05 us
    ppermute x2 -> x18, waiting for transfers between devices: 419 us -> 339 us  [the longest x1 131 us: gather_tokens(): below = lax.ppermute(below, 'row', shift_route(row_count, -2))]
    reduce_scatter x1 -> x0, waiting for transfers between devices: 73.5 us -> none  [on_device(): lax.psum_scatter(jnp.dot(gathered, new_weight, preferred_element_type=jnp...]
    pallas_call x0 -> x4, Pallas kernels: none -> 41.9 us  [precondition(): pl.pallas_call(kernel, out_shape=jax.ShapeDtypeStruct((down * width, widt...]
    mul x1 -> x0, other arithmetic: 33 us -> none  [on_device(): step_size * from_blocks(update)]
    convert_element_type x1 -> x0, local copies, waits for them, and re-layouts: 29.4 us -> none  [on_device(): lent_part.astype(jnp.bfloat16)]
    dot_general x3 -> x4, matrix products: 42.6 us -> 21.9 us  [on_device(): jnp.dot(all_tokens, fresh, preferred_element_type=jnp.float32)]
    dynamic_update_slice x0 -> x5, local copies, waits for them, and re-layouts: none -> 19.5 us  [the longest x1 9.72 us: on_device(): new_weight = lax.dynamic_update_slice(new_weight, fresh, (0, at))]
    cond x2 -> x0, local copies, waits for them, and re-layouts: 18.7 us -> none  [when_owned(): lax.cond(flag, lambda: precondition(left_root, grad_block, right_root), l...]
  transfers between devices with their start and end apart: 4 -> 18, of which waited for: 3 -> 11; matrix products, arithmetic and copies ran while one was open for 19% -> 14% of each run, Pallas kernels for 0% -> 8%
where the time goes in v1:
time: 512 us; the launch traced here: 510 us
  waiting for transfers between devices  339 us (66%)
  local copies, waits for them, and re-layouts  45.8 us (9%)
  Pallas kernels  41.9 us (8%)
  starting transfers between devices  34 us (7%)
  other arithmetic  25.6 us (5%)
  matrix products  21.9 us (4%)
    ppermute x1, waiting for transfers between devices, gather_tokens(): below = lax.ppermute(below, 'row', shift_route(row_count, -2))  131 us
    ppermute x1, waiting for transfers between devices, gather_tokens(): other = lax.ppermute(tokens, 'row', pair_route(row_count))  113 us
    ppermute x2, waiting for transfers between devices, gather_tokens(): up = lax.ppermute(up, 'row', shift_route(row_count, 2))  52.5 us
    pallas_call x4, Pallas kernels, precondition(): pl.pallas_call(kernel, out_shape=jax.ShapeDtypeStruct((down * width, widt...  41.9 us
    ppermute x4, waiting for transfers between devices, on_device(): last = lax.ppermute(piece, 'row', back)  25.5 us
    dot_general x4, matrix products, on_device(): jnp.dot(all_tokens, fresh, preferred_element_type=jnp.float32)  21.9 us
    ppermute x4, waiting for transfers between devices, far_sum(): lax.ppermute(piece, 'col', shift_route(col_count, 2 * step))  17.6 us
    ppermute x4, starting transfers between devices, on_device(): last = lax.ppermute(piece, 'row', back)  11.1 us
  transfers between devices with their start and end apart: 18, of which 11 were waited for; matrix products, arithmetic and copies ran while one was open for 14% of the time, Pallas kernels for 8%

profile of v1, /device:TPU:0, one launch (start us, length us, event | category | flops | bytes accessed | tf_op | source)
XLA Modules:
  0.0 509.7 jit_solution(4646207372344393474)
XLA Ops:
  0.6 6.1 %fusion.23 = (bf16[2048,1024]{1,0:T(8,128)(2,1)}, bf16[2048,1024]{1,0:T(8,128)(2,1)}) fusion(bf16[2048,2048]{1,0:T(8,128)(2,1)} %grad_ref.3), kind=kLoop, calls=%fused_computation.62 | loop fusion | bytes 16777216 | tf_op jit(solution)/shard_map/slice | solution.py:125
  6.7 2.9 collective-permute-start
  9.7 1.5 collective-permute-start.4
  11.3 0.2 slice_reduce_fusion.1
  11.5 112.7 %collective-permute-done.4 = bf16[256,2048]{1,0:T(8,128)(2,1)S(1)} collective-permute-done((bf16[256,2048]{1,0:T(8,128)(2,1)S(1)}, bf16[256,2048]{1,0:T(8,128)(2,1)S(1)}, u32[]{:S(2)}, u32[]{:S(2)}) %collective-permute-start.4) | collective-permute-done | bytes 1048608 | tf_op jit(solution)/shard_map/ppermute | solution.py:65
  124.2 0.1 broadcast_select_fusion.1
  124.3 1.1 broadcast.24
  125.4 0.4 pad_maximum_fusion
  125.7 1.5 collective-permute-start.5
  127.3 1.7 copy-done.5
  129.0 10.3 %precondition.4 = f32[2048,1024]{1,0:T(8,128)S(1)} custom-call(s32[2]{0:T(128)S(1)} %get-tuple-element.21.flag_ref, bf16[2,2,2,2,1024,1024]{5,4,3,2,1,0:T(8,128)(2,1)} %right_ref.7, bf16[2048,2048]{1,0:T(8,128)(2,1)} %grad_ref.3, bf16[2,2,2,2,1024,1024]{5,4,3,2,1,0:T(8,128)(2,1)} %right_ref.7), custom_call_target="tpu_custom_call" | custom-call | flops 8589934592 | bytes 20971520 | tf_op jit(solution)/shard_map/precondition/pallas_call | solution.py:46
  139.3 3.4 copy-done
  142.7 0.2 slice_reduce_fusion
  142.8 3.8 collective-permute-start.2
  146.6 12.4 %precondition.5 = bf16[2048,1024]{1,0:T(8,128)(2,1)} custom-call(s32[2]{0:T(128)S(1)} %get-tuple-element.19.flag_ref, bf16[2,2,2,2,1024,1024]{5,4,3,2,1,0:T(8,128)(2,1)} %right_ref.7, bf16[2048,1024]{1,0:T(8,128)(2,1)} %collective-permute-done.grad_ref, bf16[2,2,2,2,1024,1024]{5,4,3,2,1,0:T(8,128)(2,1)} %right_ref.7), custom_call_target="tpu_custom_call" | custom-call | flops 8589934592 | bytes 16777216 | tf_op jit(solution)/shard_map/precondition/pallas_call | solution.py:46
  159.0 5.9 %collective-permute-start.6 = (bf16[512,2048]{1,0:T(8,128)(2,1)S(1)}, bf16[512,2048]{1,0:T(8,128)(2,1)}, u32[]{:S(2)}, u32[]{:S(2)}) collective-permute-start(bf16[512,2048]{1,0:T(8,128)(2,1)S(1)} %get-tuple-element.32), channel_id=1, source_target_pairs={{0,24},{4,28},{8,0},{12,4},{16,8},{20,12},{24,16},{28,20},{1,25},{... | collective-permute-start | bytes 6291464 | tf_op jit(solution)/shard_map/ppermute | solution.py:81
  164.9 11.4 %collective-permute-done.5 = bf16[512,2048]{1,0:T(8,128)(2,1)} collective-permute-done((bf16[512,2048]{1,0:T(8,128)(2,1)S(1)}, bf16[512,2048]{1,0:T(8,128)(2,1)}, u32[]{:S(2)}, u32[]{:S(2)}) %collective-permute-start.5) | collective-permute-done | bytes 2097184 | tf_op jit(solution)/shard_map/ppermute | solution.py:78
  176.4 3.1 constant_dynamic-update-slice_fusion.5
  179.6 131.2 %collective-permute-done.6 = bf16[512,2048]{1,0:T(8,128)(2,1)} collective-permute-done((bf16[512,2048]{1,0:T(8,128)(2,1)S(1)}, bf16[512,2048]{1,0:T(8,128)(2,1)}, u32[]{:S(2)}, u32[]{:S(2)}) %collective-permute-start.6) | collective-permute-done | bytes 2097184 | tf_op jit(solution)/shard_map/ppermute | solution.py:81
  310.8 3.2 constant_dynamic-update-slice_fusion.4
  314.0 41.1 %collective-permute-done.7 = bf16[512,2048]{1,0:T(8,128)(2,1)} collective-permute-done((bf16[512,2048]{1,0:T(8,128)(2,1)}, bf16[512,2048]{1,0:T(8,128)(2,1)}, u32[]{:S(2)}, u32[]{:S(2)}) %collective-permute-start.7) | collective-permute-done | bytes 2097184 | tf_op jit(solution)/shard_map/ppermute | solution.py:78
  355.1 3.1 constant_dynamic-update-slice_fusion.3
  358.3 13.7 %precondition.7 = bf16[2048,1024]{1,0:T(8,128)(2,1)S(1)} custom-call(s32[2]{0:T(128)S(1)} %get-tuple-element.18.flag_ref, bf16[2,2,2,2,1024,1024]{5,4,3,2,1,0:T(8,128)(2,1)} %right_ref.7, bf16[2048,1024]{1,0:T(8,128)(2,1)} %collective-permute-done.2.grad_ref, bf16[2,2,2,2,1024,1024]{5,4,3,2,1,0:T(8,128)(2,1)} %right_ref.7), custom_call_target="tpu_custom_call" | custom-call | flops 8589934592 | bytes 16777216 | tf_op jit(solution)/shard_map/precondition/pallas_call | solution.py:46
  372.0 1.6 slice.69
  373.6 0.7 collective-permute-start.3
  374.3 5.7 %subtract_convert_fusion = bf16[2048,1024]{1,0:T(8,128)(2,1)S(1)} fusion(f32[2048,1024]{1,0:T(8,128)S(1)} %bitcast.63, bf16[2048,1024]{1,0:T(8,128)(2,1)} %collective-permute-done.1, bf16[2048,2048]{1,0:T(8,128)(2,1)} %param.6, pred[2048]{0:T(1024)(128)(4,1)S(1)} %broadcast_in_dim.41), kind=kLoop, calls=%fused_computation | loop fusion | flops 12582912 | bytes 20973568 | tf_op jit(solution)/shard_map/convert_element_type | solution.py:152
  380.1 0.1 slice-done.3
  380.2 9.1 %convolution_convert_fusion = bf16[2048,1024]{1,0:T(8,128)(2,1)S(1)} fusion(bf16[2048,2048]{1,0:T(8,128)(2,1)S(1)} %bitcast.65, bf16[2048,1024]{1,0:T(8,128)(2,1)S(1)} %subtract_convert_fusion), kind=kOutput, calls=%fused_computation.6 | convolution fusion | flops 8592031744 | bytes 16777216 | tf_op jit(solution)/shard_map/dot_general | solution.py:154
  389.3 2.0 copy-done.6
  391.2 1.5 dynamic-slice_bitcast_fusion
  392.8 5.5 %precondition.6 = f32[2048,1024]{1,0:T(8,128)S(1)} custom-call(s32[2]{0:T(128)S(1)} %get-tuple-element.11.flag_ref, bf16[2,2,2,2,1024,1024]{5,4,3,2,1,0:T(8,128)(2,1)} %right_ref.7, bf16[2048,2048]{1,0:T(8,128)(2,1)} %grad_ref.3, bf16[2,2,2,2,1024,1024]{5,4,3,2,1,0:T(8,128)(2,1)} %right_ref.7), custom_call_target="tpu_custom_call" | custom-call | flops 8589934592 | bytes 20971520 | tf_op jit(solution)/shard_map/precondition/pallas_call | solution.py:46
  398.4 9.7 %dynamic_update_slice.36 = bf16[2048,2048]{1,0:T(8,128)(2,1)} pad(bf16[2048,1024]{1,0:T(8,128)(2,1)} %copy-done.4, bf16[]{:T(256)} %constant.165.clone.1), padding=0_0x0_1024 | pad | bytes 12582914 | tf_op jit(solution)/shard_map/dynamic_update_slice | solution.py:153
  408.1 1.1 fusion.24
  409.2 5.3 %collective-permute-done.3 = bf16[2048,512]{1,0:T(8,128)(2,1)} collective-permute-done((bf16[2048,512]{1,0:T(8,128)(2,1)}, bf16[2048,512]{1,0:T(8,128)(2,1)}, u32[]{:S(2)}, u32[]{:S(2)}) %collective-permute-start.3) | collective-permute-done | bytes 2097184 | tf_op jit(solution)/shard_map/ppermute | solution.py:143
  414.5 4.6 convert_add_fusion
  419.1 5.2 %collective-permute-start.9 = (bf16[2048,256]{1,0:T(8,128)(2,1)S(1)}, bf16[2048,256]{1,0:T(8,128)(2,1)S(1)}, u32[]{:S(2)}, u32[]{:S(2)}) collective-permute-start(bf16[2048,256]{1,0:T(8,128)(2,1)S(1)} %get-tuple-element.14), channel_id=1, source_target_pairs={{0,28},{4,0},{8,4},{12,8},{16,12},{20,16},{24,20},{28,24},{1,29},{... | collective-permute-start | bytes 3145736 | tf_op jit(solution)/shard_map/ppermute | solution.py:143
  424.3 3.6 constant_dynamic-update-slice_fusion.2
  427.9 4.7 convolution_convert_fusion.1
  432.8 11.9 %collective-permute-done.9 = bf16[2048,256]{1,0:T(8,128)(2,1)S(1)} collective-permute-done((bf16[2048,256]{1,0:T(8,128)(2,1)S(1)}, bf16[2048,256]{1,0:T(8,128)(2,1)S(1)}, u32[]{:S(2)}, u32[]{:S(2)}) %collective-permute-start.9) | collective-permute-done | bytes 1048608 | tf_op jit(solution)/shard_map/ppermute | solution.py:143
  444.7 5.2 %collective-permute-start.11 = (bf16[2048,256]{1,0:T(8,128)(2,1)}, bf16[2048,256]{1,0:T(8,128)(2,1)}, u32[]{:S(2)}, u32[]{:S(2)}) collective-permute-start(bf16[2048,256]{1,0:T(8,128)(2,1)} %get-tuple-element.16), channel_id=1, source_target_pairs={{0,28},{4,0},{8,4},{12,8},{16,12},{20,16},{24,20},{28,24},{1,29},{... | collective-permute-start | bytes 3145736 | tf_op jit(solution)/shard_map/ppermute | solution.py:143
  449.9 0.3 convert_add_fusion.1
  450.2 2.4 constant_dynamic-update-slice_fusion.1
  452.6 2.4 convolution_convert_fusion.3
  455.1 1.1 copy-done.10
  456.3 2.7 fusion.10
  459.1 1.0 collective-permute-start.13
  460.0 1.3 convert_add_fusion.3
  461.4 8.3 %collective-permute-done.11 = bf16[2048,256]{1,0:T(8,128)(2,1)} collective-permute-done((bf16[2048,256]{1,0:T(8,128)(2,1)}, bf16[2048,256]{1,0:T(8,128)(2,1)}, u32[]{:S(2)}, u32[]{:S(2)}) %collective-permute-start.11) | collective-permute-done | bytes 1048608 | tf_op jit(solution)/shard_map/ppermute | solution.py:143
  469.6 3.2 constant_dynamic-update-slice_fusion
  472.9 5.7 %convolution_convert_fusion.2 = bf16[2048,256]{1,0:T(8,128)(2,1)S(1)} fusion(bf16[2048,2048]{1,0:T(8,128)(2,1)} %constant_dynamic-update-slice_fusion.3, bf16[2048,256]{1,0:T(8,128)(2,1)S(1)} %get-tuple-element.23), kind=kOutput, calls=%fused_computation.8 | convolution fusion | flops 2148007936 | bytes 10485760 | tf_op jit(solution)/shard_map/dot_general | solution.py:154
  478.6 1.0 copy-done.11
  479.6 0.9 dynamic-slice_bitcast_fusion.2
  480.6 3.9 collective-permute-start.14
  484.5 0.4 collective-permute-done.13
  484.9 2.3 fusion.9
  487.2 0.2 dynamic_update_slice.44
  487.4 1.1 collective-permute-start.15
  488.5 1.2 convert_add_fusion.2
  489.7 1.1 collective-permute-start.17
  490.8 6.4 %collective-permute-done.14 = bf16[512,512]{1,0:T(8,128)(2,1)S(1)} collective-permute-done((bf16[512,512]{1,0:T(8,128)(2,1)S(1)}, bf16[512,512]{1,0:T(8,128)(2,1)S(1)}, u32[]{:S(2)}, u32[]{:S(2)}) %collective-permute-start.14) | collective-permute-done | bytes 524320 | tf_op jit(solution)/shard_map/ppermute | solution.py:103
  497.2 0.2 fusion.12
  497.4 5.4 %collective-permute-done.15 = bf16[512,256]{1,0:T(8,128)(2,1)S(1)} collective-permute-done((bf16[512,256]{1,0:T(8,128)(2,1)S(1)}, bf16[512,256]{1,0:T(8,128)(2,1)S(1)}, u32[]{:S(2)}, u32[]{:S(2)}) %collective-permute-start.15) | collective-permute-done | bytes 262176 | tf_op jit(solution)/shard_map/ppermute | solution.py:103
  502.9 5.4 %collective-permute-done.17 = bf16[512,256]{1,0:T(8,128)(2,1)S(1)} collective-permute-done((bf16[512,256]{1,0:T(8,128)(2,1)S(1)}, bf16[512,256]{1,0:T(8,128)(2,1)S(1)}, u32[]{:S(2)}, u32[]{:S(2)}) %collective-permute-start.17) | collective-permute-done | bytes 262176 | tf_op jit(solution)/shard_map/ppermute | solution.py:103
  508.4 1.3 copy-done.8
  (62 shorter events, 0.9 us)
Async XLA Ops:
  0.6 9.0 %copy-start.9 = (bf16[256,2048]{1,0:T(8,128)(2,1)S(1)}, bf16[256,2048]{1,0:T(8,128)(2,1)}, u32[]{:S(2)}) copy-start(bf16[256,2048]{1,0:T(8,128)(2,1)} %param.5) | copy-start | bytes 3145732
  0.6 10.6 %copy-start.13 = (s32[8,16]{1,0:T(8,128)S(1)}, s32[8,16]{1,0:T(8,128)}, u32[]{:S(2)}) copy-start(s32[8,16]{1,0:T(8,128)} %param.9) | copy-start | bytes 1540
  6.7 136.1 %collective-permute-start = (bf16[2048,1024]{1,0:T(8,128)(2,1)}, bf16[2048,1024]{1,0:T(8,128)(2,1)}, u32[]{:S(2)}, u32[]{:S(2)}) collective-permute-start(bf16[2048,1024]{1,0:T(8,128)(2,1)} %get-tuple-element.29), channel_id=1, source_target_pairs={{0,4},{4,8},{8,12},{12,16},{16,20},{20,24},{24,28},{28,0},{1,5},{5... | collective-permute-start | bytes 12582920 | tf_op jit(solution)/shard_map/ppermute | solution.py:126
  9.7 114.5 %collective-permute-start.4 = (bf16[256,2048]{1,0:T(8,128)(2,1)S(1)}, bf16[256,2048]{1,0:T(8,128)(2,1)S(1)}, u32[]{:S(2)}, u32[]{:S(2)}) collective-permute-start(bf16[256,2048]{1,0:T(8,128)(2,1)S(1)} %copy-done.9), channel_id=1, source_target_pairs={{0,4},{4,0},{8,12},{12,8},{16,20},{20,16},{24,28},{28,24},{1,5},{5... | collective-permute-start | bytes 3145736 | tf_op jit(solution)/shard_map/ppermute | solution.py:65
  125.7 3.2 copy-start.5
  125.7 50.5 %collective-permute-start.5 = (bf16[512,2048]{1,0:T(8,128)(2,1)S(1)}, bf16[512,2048]{1,0:T(8,128)(2,1)}, u32[]{:S(2)}, u32[]{:S(2)}) collective-permute-start(bf16[512,2048]{1,0:T(8,128)(2,1)S(1)} %get-tuple-element.32), channel_id=1, source_target_pairs={{0,8},{4,12},{8,16},{12,20},{16,24},{20,28},{24,0},{28,4},{1,9},{5... | collective-permute-start | bytes 6291464 | tf_op jit(solution)/shard_map/ppermute | solution.py:78
  139.3 3.4 copy-start
  142.8 215.4 %collective-permute-start.2 = (bf16[2048,1024]{1,0:T(8,128)(2,1)}, bf16[2048,1024]{1,0:T(8,128)(2,1)}, u32[]{:S(2)}, u32[]{:S(2)}) collective-permute-start(bf16[2048,1024]{1,0:T(8,128)(2,1)} %get-tuple-element.12), channel_id=1, source_target_pairs={{0,4},{4,8},{8,12},{12,16},{16,20},{20,24},{24,28},{28,0},{1,5},{5... | collective-permute-start | bytes 12582920 | tf_op jit(solution)/shard_map/ppermute | solution.py:126
  159.0 215.3 %collective-permute-start.1 = (bf16[2048,1024]{1,0:T(8,128)(2,1)}, bf16[2048,1024]{1,0:T(8,128)(2,1)}, u32[]{:S(2)}, u32[]{:S(2)}) collective-permute-start(bf16[2048,1024]{1,0:T(8,128)(2,1)} %precondition.5), channel_id=1, source_target_pairs={{0,28},{4,0},{8,4},{12,8},{16,12},{20,16},{24,20},{28,24},{1,29},{... | collective-permute-start | bytes 12582920 | tf_op jit(solution)/shard_map/ppermute | solution.py:143
  159.0 151.8 %collective-permute-start.6 = (bf16[512,2048]{1,0:T(8,128)(2,1)S(1)}, bf16[512,2048]{1,0:T(8,128)(2,1)}, u32[]{:S(2)}, u32[]{:S(2)}) collective-permute-start(bf16[512,2048]{1,0:T(8,128)(2,1)S(1)} %get-tuple-element.32), channel_id=1, source_target_pairs={{0,24},{4,28},{8,0},{12,4},{16,8},{20,12},{24,16},{28,20},{1,25},{... | collective-permute-start | bytes 6291464 | tf_op jit(solution)/shard_map/ppermute | solution.py:81
  176.3 178.8 %collective-permute-start.7 = (bf16[512,2048]{1,0:T(8,128)(2,1)}, bf16[512,2048]{1,0:T(8,128)(2,1)}, u32[]{:S(2)}, u32[]{:S(2)}) collective-permute-start(bf16[512,2048]{1,0:T(8,128)(2,1)} %collective-permute-done.5), channel_id=1, source_target_pairs={{0,8},{4,12},{8,16},{12,20},{16,24},{20,28},{24,0},{28,4},{1,9},{5... | collective-permute-start | bytes 6291464 | tf_op jit(solution)/shard_map/ppermute | solution.py:78
  358.3 16.1 %slice-start = ((s8[8388608]{0:T(1024)(128)(4,1)}), s8[4194304]{0:T(1024)(128)(4,1)S(1)}, s32[]{:S(2)}) async-start(s8[8388608]{0:T(1024)(128)(4,1)} %bitcast.62), calls=%async_computation | async-start | bytes 8388608
  358.3 16.1 %slice-start.1 = ((s8[8388608]{0:T(1024)(128)(4,1)}), s8[4194304]{0:T(1024)(128)(4,1)S(1)}, s32[]{:S(2)}) async-start(s8[8388608]{0:T(1024)(128)(4,1)} %bitcast.62), calls=%async_computation.1 | async-start | bytes 8388608
  372.0 8.0 %copy-start.2 = (bf16[2048,1024]{1,0:T(8,128)(2,1)}, bf16[2048,1024]{1,0:T(8,128)(2,1)S(1)}, u32[]{:S(2)}) copy-start(bf16[2048,1024]{1,0:T(8,128)(2,1)S(1)} %precondition.7) | copy-start | bytes 12582916
  372.0 8.0 %slice-start.2 = ((s8[8388608]{0:T(1024)(128)(4,1)}), s8[4194304]{0:T(1024)(128)(4,1)S(1)}, s32[]{:S(2)}) async-start(s8[8388608]{0:T(1024)(128)(4,1)} %bitcast.64), calls=%async_computation.2 | async-start | bytes 8388608
  373.6 6.6 %slice-start.3 = ((s8[8388608]{0:T(1024)(128)(4,1)}), s8[4194304]{0:T(1024)(128)(4,1)S(1)}, s32[]{:S(2)}) async-start(s8[8388608]{0:T(1024)(128)(4,1)} %bitcast.64), calls=%async_computation.3 | async-start | bytes 8388608
  373.6 40.9 %collective-permute-start.3 = (bf16[2048,512]{1,0:T(8,128)(2,1)}, bf16[2048,512]{1,0:T(8,128)(2,1)}, u32[]{:S(2)}, u32[]{:S(2)}) collective-permute-start(bf16[2048,512]{1,0:T(8,128)(2,1)} %slice.69), channel_id=1, source_target_pairs={{0,28},{4,0},{8,4},{12,8},{16,12},{20,16},{24,20},{28,24},{1,29},{... | collective-permute-start | bytes 6291464 | tf_op jit(solution)/shard_map/ppermute | solution.py:143
  380.2 9.1 %copy-start.4 = (bf16[2048,1024]{1,0:T(8,128)(2,1)}, bf16[2048,1024]{1,0:T(8,128)(2,1)S(1)}, u32[]{:S(2)}) copy-start(bf16[2048,1024]{1,0:T(8,128)(2,1)S(1)} %subtract_convert_fusion) | copy-start | bytes 12582916
  389.2 2.0 copy-start.6
  392.7 21.8 %collective-permute-start.8 = (bf16[2,512,1024]{2,1,0:T(8,128)(2,1)}, bf16[2,512,1024]{2,1,0:T(8,128)(2,1)}, u32[]{:S(2)}, u32[]{:S(2)}) collective-permute-start(bf16[2,512,1024]{2,1,0:T(8,128)(2,1)} %dynamic-slice_bitcast_fusion), channel_id=1, source_target_pairs={{0,1},{1,0},{2,3},{3,2},{4,5},{5,4},{6,7},{7,6},{8,9},{9,8},{10,11... | collective-permute-start | bytes 6291464 | tf_op jit(solution)/shard_map/ppermute | solution.py:92
  398.4 51.8 %copy-start.1 = (f32[2048,1024]{1,0:T(8,128)}, f32[2048,1024]{1,0:T(8,128)S(1)}, u32[]{:S(2)}) copy-start(f32[2048,1024]{1,0:T(8,128)S(1)} %precondition.6) | copy-start | bytes 25165828
  398.4 9.7 %copy-start.3 = (bf16[2048,1024]{1,0:T(8,128)(2,1)S(1)}, bf16[2048,1024]{1,0:T(8,128)(2,1)}, u32[]{:S(2)}) copy-start(bf16[2048,1024]{1,0:T(8,128)(2,1)} %copy-done.2) | copy-start | bytes 12582916
  408.1 6.4 %copy-start.7 = (bf16[2048,1024]{1,0:T(8,128)(2,1)S(1)}, bf16[2048,1024]{1,0:T(8,128)(2,1)}, u32[]{:S(2)}) copy-start(bf16[2048,1024]{1,0:T(8,128)(2,1)} %copy-done.6) | copy-start | bytes 12582916
  414.5 13.4 %slice-start.4 = ((s8[8388608]{0:T(1024)(128)(4,1)}), s8[4194304]{0:T(1024)(128)(4,1)S(1)}, s32[]{:S(2)}) async-start(s8[8388608]{0:T(1024)(128)(4,1)} %bitcast.66), calls=%async_computation.4 | async-start | bytes 8388608
  419.1 8.8 %slice-start.5 = ((s8[8388608]{0:T(1024)(128)(4,1)}), s8[4194304]{0:T(1024)(128)(4,1)S(1)}, s32[]{:S(2)}) async-start(s8[8388608]{0:T(1024)(128)(4,1)} %bitcast.66), calls=%async_computation.5 | async-start | bytes 8388608
  419.1 25.6 %collective-permute-start.9 = (bf16[2048,256]{1,0:T(8,128)(2,1)S(1)}, bf16[2048,256]{1,0:T(8,128)(2,1)S(1)}, u32[]{:S(2)}, u32[]{:S(2)}) collective-permute-start(bf16[2048,256]{1,0:T(8,128)(2,1)S(1)} %get-tuple-element.14), channel_id=1, source_target_pairs={{0,28},{4,0},{8,4},{12,8},{16,12},{20,16},{24,20},{28,24},{1,29},{... | collective-permute-start | bytes 3145736 | tf_op jit(solution)/shard_map/ppermute | solution.py:143
  432.7 17.2 %collective-permute-start.10 = (bf16[2,512,512]{2,1,0:T(8,128)(2,1)S(1)}, bf16[2,512,512]{2,1,0:T(8,128)(2,1)S(1)}, u32[]{:S(2)}, u32[]{:S(2)}) collective-permute-start(bf16[2,512,512]{2,1,0:T(8,128)(2,1)S(1)} %dynamic-slice_bitcast_fusion.1), channel_id=1, source_target_pairs={{0,1},{1,0},{2,3},{3,2},{4,5},{5,4},{6,7},{7,6},{8,9},{9,8},{10,11... | collective-permute-start | bytes 3145736 | tf_op jit(solution)/shard_map/ppermute | solution.py:92
  444.7 25.0 %collective-permute-start.11 = (bf16[2048,256]{1,0:T(8,128)(2,1)}, bf16[2048,256]{1,0:T(8,128)(2,1)}, u32[]{:S(2)}, u32[]{:S(2)}) collective-permute-start(bf16[2048,256]{1,0:T(8,128)(2,1)} %get-tuple-element.16), channel_id=1, source_target_pairs={{0,28},{4,0},{8,4},{12,8},{16,12},{20,16},{24,20},{28,24},{1,29},{... | collective-permute-start | bytes 3145736 | tf_op jit(solution)/shard_map/ppermute | solution.py:143
  455.1 1.1 copy-start.10
  456.2 3.8 collective-permute-start.12
  459.1 25.8 %collective-permute-start.13 = (bf16[512,1024]{1,0:T(8,128)(2,1)}, bf16[512,1024]{1,0:T(8,128)(2,1)}, u32[]{:S(2)}, u32[]{:S(2)}) collective-permute-start(bf16[512,1024]{1,0:T(8,128)(2,1)} %fusion.10), channel_id=1, source_target_pairs={{0,2},{1,3},{2,0},{3,1},{4,6},{5,7},{6,4},{7,5},{8,10},{9,11},{10,... | collective-permute-start | bytes 3145736 | tf_op jit(solution)/shard_map/ppermute | solution.py:103
  478.6 1.0 copy-start.11
  480.5 8.0 %collective-permute-start.16 = (bf16[2,512,256]{2,1,0:T(8,128)(2,1)}, bf16[2,512,256]{2,1,0:T(8,128)(2,1)}, u32[]{:S(2)}, u32[]{:S(2)}) collective-permute-start(bf16[2,512,256]{2,1,0:T(8,128)(2,1)} %dynamic-slice_bitcast_fusion.2), channel_id=1, source_target_pairs={{0,1},{1,0},{2,3},{3,2},{4,5},{5,4},{6,7},{7,6},{8,9},{9,8},{10,11... | collective-permute-start | bytes 1572872 | tf_op jit(solution)/shard_map/ppermute | solution.py:92
  480.5 7.9 %copy-start.12 = (bf16[2048,256]{1,0:T(8,128)(2,1)S(1)}, bf16[2048,256]{1,0:T(8,128)(2,1)}, u32[]{:S(2)}) copy-start(bf16[2048,256]{1,0:T(8,128)(2,1)} %copy-done.11) | copy-start | bytes 3145732
  480.6 16.7 %collective-permute-start.14 = (bf16[512,512]{1,0:T(8,128)(2,1)S(1)}, bf16[512,512]{1,0:T(8,128)(2,1)S(1)}, u32[]{:S(2)}, u32[]{:S(2)}) collective-permute-start(bf16[512,512]{1,0:T(8,128)(2,1)S(1)} %fusion.13), channel_id=1, source_target_pairs={{0,2},{1,3},{2,0},{3,1},{4,6},{5,7},{6,4},{7,5},{8,10},{9,11},{10,... | collective-permute-start | bytes 1572872 | tf_op jit(solution)/shard_map/ppermute | solution.py:103
  487.4 15.4 %collective-permute-start.15 = (bf16[512,256]{1,0:T(8,128)(2,1)S(1)}, bf16[512,256]{1,0:T(8,128)(2,1)S(1)}, u32[]{:S(2)}, u32[]{:S(2)}) collective-permute-start(bf16[512,256]{1,0:T(8,128)(2,1)S(1)} %fusion.18), channel_id=1, source_target_pairs={{0,2},{1,3},{2,0},{3,1},{4,6},{5,7},{6,4},{7,5},{8,10},{9,11},{10,... | collective-permute-start | bytes 786440 | tf_op jit(solution)/shard_map/ppermute | solution.py:103
  489.7 18.6 %collective-permute-start.17 = (bf16[512,256]{1,0:T(8,128)(2,1)S(1)}, bf16[512,256]{1,0:T(8,128)(2,1)S(1)}, u32[]{:S(2)}, u32[]{:S(2)}) collective-permute-start(bf16[512,256]{1,0:T(8,128)(2,1)S(1)} %fusion.19), channel_id=1, source_target_pairs={{0,2},{1,3},{2,0},{3,1},{4,6},{5,7},{6,4},{7,5},{8,10},{9,11},{10,... | collective-permute-start | bytes 786440 | tf_op jit(solution)/shard_map/ppermute | solution.py:103
  508.4 1.3 copy-start.8

commit v2 on v1

v2 whole, which is shorter than its diff:
```python
import jax
import jax.numpy as jnp
from jax import lax
from jax.experimental import pallas as pl
from jax.experimental.pallas import tpu as pltpu
from jax.sharding import PartitionSpec as P

step_size = 0.5


def shift_route(count, distance):
    return [(i, (i + distance) % count) for i in range(count)]


def pair_route(count):
    return [(i, i ^ 1) for i in range(count)]


def together(*values):
    return lax.optimization_barrier(values)


def root_spec(roots, side, slot, block):
    width = roots.shape[-1]
    return pl.BlockSpec((None, None, None, None, width, width), lambda *at: (side, block(*at)[0], slot, block(*at)[1], 0, 0))


def update_rows(left_ref, grad_ref, right_ref, rows):
    mixed = jnp.dot(left_ref[rows, :], grad_ref[...], preferred_element_type=jnp.float32)
    return jnp.dot(mixed.astype(jnp.bfloat16), right_ref[...], preferred_element_type=jnp.float32)


def cost(blocks, width, arrays):
    return pl.CostEstimate(
        flops=blocks * 4 * width**3, bytes_accessed=blocks * 2 * arrays * width * width, transcendentals=0
    )


def precondition_lent(flags, roots, q, came, cuts, later_than):
    width = roots.shape[-1]
    down = came.shape[0] // width
    tile = min(width, 256)
    pieces = list(zip(cuts[:-1], cuts[1:]))

    def kernel(flag_ref, left_ref, grad_ref, right_ref, *rest):
        *out_refs, mark_ref = rest[-len(pieces) - 1:]
        mark_ref[...] = jnp.zeros_like(mark_ref)

        @pl.when(flag_ref[pl.program_id(0)] != 0)
        def _():
            @pl.loop(0, width // tile)
            def _(i):
                rows = pl.ds(pl.multiple_of(i * tile, tile), tile)
                update = update_rows(left_ref, grad_ref, right_ref, rows).astype(jnp.bfloat16)
                for (start, stop), out_ref in zip(pieces, out_refs):
                    out_ref[rows, :] = update[:, start:stop]

        @pl.when(flag_ref[pl.program_id(0)] == 0)
        def _():
            for out_ref in out_refs:
                out_ref[...] = jnp.zeros_like(out_ref)

    return pl.pallas_call(
        kernel,
        out_shape=[jax.ShapeDtypeStruct((down * width, stop - start), jnp.bfloat16) for start, stop in pieces]
        + [jax.ShapeDtypeStruct((8, 128), jnp.float32)],
        grid_spec=pltpu.PrefetchScalarGridSpec(
            num_scalar_prefetch=1,
            grid=(down,),
            in_specs=[
                root_spec(roots, 0, 1, lambda p, f: (p, q)),
                pl.BlockSpec((width, width), lambda p, f: (p, q)),
                root_spec(roots, 1, 1, lambda p, f: (p, q)),
            ]
            + [pl.BlockSpec(memory_space=pl.ANY)] * len(later_than),
            out_specs=[pl.BlockSpec((width, stop - start), lambda p, f: (p, 0)) for start, stop in pieces]
            + [pl.BlockSpec((8, 128), lambda p, f: (0, 0))],
        ),
        compiler_params=pltpu.CompilerParams(vmem_limit_bytes=40 << 20),
        cost_estimate=cost(down, width, 4),
        name="precondition_lent",
    )(flags, roots, came, roots, *later_than)


def precondition_home(kept_column, roots, grad, weight, q, new_weight, later_than):
    width = roots.shape[-1]
    down = kept_column.shape[0]
    tile = min(width, 256)

    def kernel(flag_ref, left_ref, grad_ref, right_ref, weight_ref, *rest):
        out_ref = rest[-1]

        @pl.when(flag_ref[pl.program_id(0)] != 0)
        def _():
            @pl.loop(0, width // tile)
            def _(i):
                rows = pl.ds(pl.multiple_of(i * tile, tile), tile)
                update = update_rows(left_ref, grad_ref, right_ref, rows)
                out_ref[rows, :] = (weight_ref[rows, :].astype(jnp.float32) - step_size * update).astype(jnp.bfloat16)

        @pl.when(flag_ref[pl.program_id(0)] == 0)
        def _():
            out_ref[...] = weight_ref[...]

    tiles = pl.BlockSpec((width, width), lambda p, f: (p, q))
    extra = ([] if new_weight is None else [new_weight]) + list(later_than)
    return pl.pallas_call(
        kernel,
        out_shape=jax.ShapeDtypeStruct(weight.shape, jnp.bfloat16),
        grid_spec=pltpu.PrefetchScalarGridSpec(
            num_scalar_prefetch=1,
            grid=(down,),
            in_specs=[
                root_spec(roots, 0, 0, lambda p, f: (p, q)),
                tiles,
                root_spec(roots, 1, 0, lambda p, f: (p, q)),
                tiles,
            ]
            + [pl.BlockSpec(memory_space=pl.ANY)] * len(extra),
            out_specs=tiles,
        ),
        input_output_aliases={} if new_weight is None else {5: 0},
        compiler_params=pltpu.CompilerParams(vmem_limit_bytes=48 << 20),
        cost_estimate=cost(down, width, 5),
        name="precondition_home",
    )(kept_column, roots, grad, roots, weight, *extra)


def finish_columns(flags, down, across, q, col_count, new_weight, piece, tokens, start, width, later_than):
    depth = piece.shape[0]
    at = (q * piece.shape[1] + start) // width
    height = depth // down
    rows = tokens.shape[0] // col_count
    half = col_count // 2
    tile = min(width, 256)

    def kernel(flag_ref, weight_ref, piece_ref, token_ref, *rest):
        new_ref, others_ref, mine_ref = rest[-3:]
        step = pl.program_id(0)

        @pl.when(step == 0)
        def _():
            for p in range(down):
                own = slice(p * height, (p + 1) * height)

                @pl.when(flag_ref[p * across + q] != 0)
                def _():
                    new_ref[own, :] = weight_ref[own, :]

                @pl.when(flag_ref[p * across + q] == 0)
                def _():
                    update = step_size * piece_ref[own, :].astype(jnp.float32)
                    new_ref[own, :] = (weight_ref[own, :].astype(jnp.float32) - update).astype(jnp.bfloat16)

        def product(out_ref):
            @pl.loop(0, width // tile)
            def _(i):
                some = pl.ds(pl.multiple_of(i * tile, tile), tile)
                term = jnp.dot(token_ref[...], new_ref[:, some], preferred_element_type=jnp.float32)
                out_ref[:, some] = term.astype(jnp.bfloat16)

        @pl.when(step < half)
        def _():
            product(others_ref)

        @pl.when(step >= half)
        def _():
            product(mine_ref)

    def chunk(t, f):
        core = f[down * across]
        return jnp.where(t < half, 2 * t + 1 - core, 2 * (t - half) + core)

    columns = pl.BlockSpec((depth, width), lambda t, f: (0, at))
    terms = jax.ShapeDtypeStruct((half, rows, width), jnp.bfloat16)
    return pl.pallas_call(
        kernel,
        out_shape=(jax.ShapeDtypeStruct(new_weight.shape, jnp.bfloat16), terms, terms),
        grid_spec=pltpu.PrefetchScalarGridSpec(
            num_scalar_prefetch=1,
            grid=(col_count,),
            in_specs=[
                columns,
                pl.BlockSpec((depth, width), lambda t, f: (0, start // width)),
                pl.BlockSpec((rows, depth), lambda t, f: (chunk(t, f), 0)),
            ]
            + [pl.BlockSpec(memory_space=pl.ANY)] * len(later_than),
            out_specs=(
                columns,
                pl.BlockSpec((None, rows, width), lambda t, f: (jnp.minimum(t, half - 1), 0, 0)),
                pl.BlockSpec((None, rows, width), lambda t, f: (jnp.maximum(t - half, 0), 0, 0)),
            ),
        ),
        input_output_aliases={1: 0},
        compiler_params=pltpu.CompilerParams(vmem_limit_bytes=56 << 20),
        cost_estimate=pl.CostEstimate(flops=1000, bytes_accessed=1000, transcendentals=0),
        name="finish_columns",
    )(flags, new_weight, piece, tokens, *later_than)


def swap_tokens(tokens, row_count, row_place):
    other = lax.ppermute(tokens, "row", pair_route(row_count))
    low = jnp.mod(row_place, 2) == 0
    return jnp.concatenate([jnp.where(low, tokens, other), jnp.where(low, other, tokens)], axis=0)


def ring_direct(pair, row_count, side):
    sides = range(side, row_count, 2)
    return [
        lax.ppermute(pair, "row", [(i, (i + 2 * step) % row_count) for i in sides])
        for step in range(1, row_count // 2)
    ]


def line_step(up, down, row_count, side):
    ups = lax.ppermute(up, "row", [(i, i + 2) for i in range(side, row_count - 2, 2)])
    downs = lax.ppermute(down, "row", [(i + 2, i) for i in range(side, row_count - 2, 2)])
    return ups, downs


def put_pairs(pair, early, late, row_place):
    pairs = len(early) + 1
    rows, depth = pair.shape
    ups = [up for up, _ in late]
    downs = [below for _, below in late]

    def kernel(place_ref, *refs):
        pair_ref, *others, out_ref, sem = refs
        early_refs, up_refs, down_refs = (others[i * (pairs - 1):(i + 1) * (pairs - 1)] for i in range(3))
        t = pl.program_id(0)
        apart = place_ref[0] - t
        odd = place_ref[1] == 1
        cases = [(apart == 0, pair_ref)]
        for step in range(1, pairs):
            cases.append((jnp.logical_and(odd, apart == step), up_refs[step - 1]))
            cases.append((jnp.logical_and(odd, apart == -step), down_refs[step - 1]))
            around = jnp.logical_or(apart == step, apart == step - pairs)
            cases.append((jnp.logical_and(jnp.logical_not(odd), around), early_refs[step - 1]))
        for case, source in cases:
            @pl.when(case)
            def _():
                copy = pltpu.make_async_copy(source, out_ref, sem)
                copy.start()
                copy.wait()

    count = 1 + 3 * (pairs - 1)
    return pl.pallas_call(
        kernel,
        out_shape=jax.ShapeDtypeStruct((rows * pairs, depth), pair.dtype),
        grid_spec=pltpu.PrefetchScalarGridSpec(
            num_scalar_prefetch=1,
            grid=(pairs,),
            in_specs=[pl.BlockSpec(memory_space=pl.ANY)] * count,
            out_specs=pl.BlockSpec((rows, depth), lambda t, f: (t, 0)),
            scratch_shapes=[pltpu.SemaphoreType.DMA],
        ),
        cost_estimate=pl.CostEstimate(flops=1000, bytes_accessed=1000, transcendentals=0),
        name="put_pairs",
    )(jnp.stack([row_place // 2, row_place % 2]), pair, *early, *ups, *downs)


def far_sum(mine, came, col_count, col_place):
    halves = mine.astype(jnp.float32) + came.astype(jnp.float32)
    groups = col_count // 2
    place = col_place // 2
    total = lax.dynamic_index_in_dim(halves, place, 0, keepdims=False)
    sent = halves.astype(jnp.bfloat16)
    for step in range(1, groups):
        piece = lax.dynamic_index_in_dim(sent, jnp.mod(place + step, groups), 0, keepdims=False)
        total = total + lax.ppermute(piece, "col", shift_route(col_count, 2 * step)).astype(jnp.float32)
    return total.astype(jnp.bfloat16)


def on_device(tokens, weight, grad, roots, owner):
    width = roots.shape[-1]
    down = weight.shape[0] // width
    across = weight.shape[1] // width
    row_place = lax.axis_index("row")
    col_place = lax.axis_index("col")
    row_count = lax.axis_size("row")
    col_count = lax.axis_size("col")
    previous = jnp.mod(row_place - 1 + row_count, row_count)
    own_owner = lax.dynamic_slice(owner, (col_place * down, row_place * across), (down, across))
    prior_owner = lax.dynamic_slice(owner, (col_place * down, previous * across), (down, across))
    kept = (own_owner == row_place).astype(jnp.int32)
    taken = (prior_owner == row_place).astype(jnp.int32)
    forth = shift_route(row_count, 1)
    back = shift_route(row_count, -1)

    swapped = swap_tokens(tokens, row_count, row_place)
    swapped, grad = together(swapped, grad)
    came = lax.ppermute(grad, "row", forth)
    early = ring_direct(swapped, row_count, 0)
    came, late_pair, *early = together(came, swapped, *early)

    returned = []
    new_weight = None
    for q in range(across):
        later_than = () if new_weight is None else (new_weight,)
        lent, mark = precondition_lent(taken[:, q], roots, q, came, (0, width), later_than)
        returned.append(lax.ppermute(lent, "row", back))
        new_weight = precondition_home(kept[:, q], roots, grad, weight, q, new_weight, (mark,))

    late = []
    up = down_piece = late_pair
    first_piece = returned[0]
    for step in range(1, row_count // 2):
        if step == row_count // 2 - 1:
            up, down_piece, first_piece, new_weight = together(up, down_piece, first_piece, new_weight)
        up, down_piece = line_step(up, down_piece, row_count, 1)
        late.append((up, down_piece))
    returned[0] = first_piece
    all_tokens = put_pairs(swapped, early, late, row_place)
    output = jnp.zeros((all_tokens.shape[0] // col_count, weight.shape[1]), jnp.bfloat16)

    flags = jnp.concatenate([kept.reshape(-1), jnp.mod(col_place, 2).reshape(1)])

    half = width // 2
    parts = [(q, 0, width) for q in range(across - 1)] + [(across - 1, 0, half), (across - 1, half, half)]
    later_than = ()
    ahead = ()
    for k, (q, start, size) in enumerate(parts):
        if k == len(parts) - 1:
            later_than = later_than + ahead
        new_weight, others, mine = finish_columns(
            flags, down, across, q, col_count, new_weight, returned[q], all_tokens, start, size, later_than
        )
        other = lax.ppermute(others, "col", pair_route(col_count))
        total = far_sum(mine, other, col_count, col_place)
        output = lax.dynamic_update_slice(output, total, (0, q * width + start))
        later_than = (mine,)
        if q < across - 1:
            ahead = ahead + (total,)
    return new_weight, output


def solution(mesh):
    placed = (
        P("row", "col"),
        P("col", "row"),
        P("col", "row"),
        P(None, "col", None, "row", None, None),
        P(),
    )
    return jax.shard_map(
        on_device,
        mesh=mesh,
        in_specs=placed,
        out_specs=(P("col", "row"), P("col", "row")),
        check_vma=False,
    )
```

time: 512 us -> 485 us (0.947)
  Pallas kernels: 41.9 us -> 97.1 us
  local copies, waits for them, and re-layouts: 45.8 us -> 6.18 us
  waiting for transfers between devices: 339 us -> 316 us
  matrix products: 21.9 us -> 0 us
  other arithmetic: 25.6 us -> 9.26 us
  starting transfers between devices: 34 us -> 48.9 us
    pallas_call x4 -> x8, Pallas kernels: 41.9 us -> 97.1 us  [the longest x3 44 us: finish_columns(): pl.pallas_call(kernel, out_shape=(jax.ShapeDtypeStruct(new_weight.shape,...]
    ppermute x14 -> x16, waiting for transfers between devices: 322 us -> 296 us  [the longest x3 173 us: ring_direct(): lax.ppermute(pair, 'row', [(i, (i + 2 * step) % row_count) for i in sides])]
    dot_general x4 -> x0, matrix products: 21.9 us -> none  [on_device(): jnp.dot(all_tokens, fresh, preferred_element_type=jnp.float32)]
    dynamic_update_slice x5 -> x1, local copies, waits for them, and re-layouts: 19.5 us -> 0.23 us  [on_device(): output = lax.dynamic_update_slice(output, total, (0, q * width + start))]
    ppermute x14 -> x16, starting transfers between devices: 26.9 us -> 44.5 us  [the longest x2 18.1 us: on_device(): returned.append(lax.ppermute(lent, 'row', back))]
    dynamic_update_slice x6 -> x2, other arithmetic: 9.61 us -> 0.34 us  [on_device(): output = lax.dynamic_update_slice(output, total, (0, q * width + start))]
    slice x4 -> x1, local copies, waits for them, and re-layouts: 8.95 us -> 0.17 us  [on_device(): kept[:, q]]
    convert_element_type x1 -> x0, other arithmetic: 5.7 us -> none  [on_device(): (weight[:, at:at + stop - start].astype(jnp.float32) - step_size * update...]
  transfers between devices with their start and end apart: 18 -> 19, of which waited for: 11 -> 9; matrix products, arithmetic and copies ran while one was open for 14% -> 2% of each run, Pallas kernels for 8% -> 20%
where the time goes in v2:
time: 485 us; the launch traced here: 479 us
  waiting for transfers between devices  316 us (65%)
  Pallas kernels  97.1 us (20%)
  starting transfers between devices  48.9 us (10%)
  other arithmetic  9.26 us (2%)
  local copies, waits for them, and re-layouts  6.18 us (1%)
    ppermute x3, waiting for transfers between devices, ring_direct(): lax.ppermute(pair, 'row', [(i, (i + 2 * step) % row_count) for i in sides])  173 us
    ppermute x2, waiting for transfers between devices, on_device(): returned.append(lax.ppermute(lent, 'row', back))  93.8 us
    pallas_call x3, Pallas kernels, finish_columns(): pl.pallas_call(kernel, out_shape=(jax.ShapeDtypeStruct(new_weight.shape,...  44 us
    pallas_call x2, Pallas kernels, precondition_home(): pl.pallas_call(kernel, out_shape=jax.ShapeDtypeStruct(weight.shape, jnp.b...  24.6 us
    ppermute x1, waiting for transfers between devices, swap_tokens(): other = lax.ppermute(tokens, 'row', pair_route(row_count))  23.4 us
    ppermute x3, waiting for transfers between devices, far_sum(): lax.ppermute(piece, 'col', shift_route(col_count, 2 * step))  20.8 us
    ppermute x2, starting transfers between devices, on_device(): returned.append(lax.ppermute(lent, 'row', back))  18.1 us
    pallas_call x2, Pallas kernels, precondition_lent(): pl.pallas_call(kernel, out_shape=[jax.ShapeDtypeStruct((down * width, sto...  17.7 us
  transfers between devices with their start and end apart: 19, of which 9 were waited for; matrix products, arithmetic and copies ran while one was open for 2% of the time, Pallas kernels for 20%

profile of v2, /device:TPU:0, one launch (start us, length us, event | category | flops | bytes accessed | tf_op | source)
XLA Modules:
  0.0 478.7 jit_solution(3153263278053729911)
XLA Ops:
  0.6 3.0 collective-permute-start
  3.6 23.4 %collective-permute-done = bf16[256,2048]{1,0:T(8,128)(2,1)S(1)} collective-permute-done((bf16[256,2048]{1,0:T(8,128)(2,1)}, bf16[256,2048]{1,0:T(8,128)(2,1)S(1)}, u32[]{:S(2)}, u32[]{:S(2)}) %collective-permute-start) | collective-permute-done | bytes 1048608 | tf_op jit(solution)/shard_map/ppermute | solution.py:202
  27.0 1.4 broadcast_select_fusion.1
  28.4 0.0 copy-start.8
  28.4 0.1 pad_maximum_fusion.refs_0_
  28.5 0.0 copy-start.2
  28.5 1.8 collective-permute-start.1
  30.3 5.5 %collective-permute-start.4 = (bf16[512,2048]{1,0:T(8,128)(2,1)S(1)}, bf16[512,2048]{1,0:T(8,128)(2,1)}, u32[]{:S(2)}, u32[]{:S(2)}) collective-permute-start(bf16[512,2048]{1,0:T(8,128)(2,1)S(1)} %pad_maximum_fusion.refs_0_), channel_id=1, source_target_pairs={{0,24},{8,0},{16,8},{24,16},{1,25},{9,1},{17,9},{25,17},{2,26},{10... | collective-permute-start | bytes 6291464 | tf_op jit(solution)/shard_map/ppermute | solution.py:210
  35.8 1.9 collective-permute-start.3
  37.8 2.9 collective-permute-start.2
  40.7 0.1 compare_convert_fusion
  40.8 0.2 slice_reduce_fusion
  41.0 41.0 %collective-permute-done.4.refs_3_ = bf16[512,2048]{1,0:T(8,128)(2,1)} collective-permute-done((bf16[512,2048]{1,0:T(8,128)(2,1)S(1)}, bf16[512,2048]{1,0:T(8,128)(2,1)}, u32[]{:S(2)}, u32[]{:S(2)}) %collective-permute-start.4) | collective-permute-done | bytes 2097184 | tf_op jit(solution)/shard_map/ppermute | solution.py:210
  82.0 132.4 %collective-permute-done.3.refs_2_ = bf16[512,2048]{1,0:T(8,128)(2,1)} collective-permute-done((bf16[512,2048]{1,0:T(8,128)(2,1)S(1)}, bf16[512,2048]{1,0:T(8,128)(2,1)}, u32[]{:S(2)}, u32[]{:S(2)}) %collective-permute-start.3) | collective-permute-done | bytes 2097184 | tf_op jit(solution)/shard_map/ppermute | solution.py:210
  214.4 0.0 collective-permute-done.2.refs_1_
  214.4 0.0 collective-permute-done.1.grad_ref
  214.4 2.0 collective-permute-start.7
  216.4 2.0 collective-permute-start.5
  218.4 5.4 %precondition_lent.2 = (bf16[2048,1024]{1,0:T(8,128)(2,1)S(1)}, f32[8,128]{1,0:T(8,128)S(1)}) custom-call(s32[2]{0:T(128)S(1)} %get-tuple-element.51.flag_ref, bf16[2,2,2,2,1024,1024]{5,4,3,2,1,0:T(8,128)(2,1)} %right_ref.7, bf16[2048,2048]{1,0:T(8,128)(2,1)} %collective-permute-done.1.grad_ref, bf16[2,2,2,2,1024,1024]{5,4,3,2,1,0:T(8,128)(2,1)} %right_ref.7), custom_call_target="tpu_custom_call" | custom-call | flops 8589934592 | bytes 16777216 | tf_op jit(solution)/shard_map/precondition_lent/pallas_call | solution.py:63
  223.7 9.8 %collective-permute-start.9 = (bf16[2048,1024]{1,0:T(8,128)(2,1)S(1)}, bf16[2048,1024]{1,0:T(8,128)(2,1)S(1)}, u32[]{:S(2)}, u32[]{:S(2)}) collective-permute-start(bf16[2048,1024]{1,0:T(8,128)(2,1)S(1)} %get-tuple-element.30), channel_id=1, source_target_pairs={{0,28},{4,0},{8,4},{12,8},{16,12},{20,16},{24,20},{28,24},{1,29},{... | collective-permute-start | bytes 12582920 | tf_op jit(solution)/shard_map/ppermute | solution.py:301
  233.5 0.2 slice_reduce_fusion.1
  233.7 2.0 collective-permute-start.8
  235.7 0.8 collective-permute-start.6
  236.5 13.6 %precondition_home.2.rest_0_ = bf16[2048,2048]{1,0:T(8,128)(2,1)} custom-call(s32[2]{0:T(128)S(1)} %get-tuple-element.52.flag_ref, bf16[2,2,2,2,1024,1024]{5,4,3,2,1,0:T(8,128)(2,1)} %right_ref.7, bf16[2048,2048]{1,0:T(8,128)(2,1)} %grad_ref.1, bf16[2,2,2,2,1024,1024]{5,4,3,2,1,0:T(8,128)(2,1)} %right_ref.7, bf16[2048,2048]{1,0:T(8,128)(2,1)} %weight_ref.3, ...), custom_call_target="tpu_custom_call" | custom-call | flops 8589934592 | bytes 20971520 | tf_op jit(solution)/shard_map/precondition_home/pallas_call | solution.py:107
  250.0 12.3 %precondition_lent.3 = (bf16[2048,1024]{1,0:T(8,128)(2,1)}, f32[8,128]{1,0:T(8,128)S(1)}) custom-call(s32[2]{0:T(128)S(1)} %get-tuple-element.50.flag_ref, bf16[2,2,2,2,1024,1024]{5,4,3,2,1,0:T(8,128)(2,1)} %right_ref.7, bf16[2048,2048]{1,0:T(8,128)(2,1)} %collective-permute-done.1.grad_ref, bf16[2,2,2,2,1024,1024]{5,4,3,2,1,0:T(8,128)(2,1)} %right_ref.7, ...), custom_call_target="tpu_custom_call" | custom-call | flops 8589934592 | bytes 16777216 | tf_op jit(solution)/shard_map/precondition_lent/pallas_call | solution.py:63
  262.4 11.1 %precondition_home.3.weight_ref = bf16[2048,2048]{1,0:T(8,128)(2,1)} custom-call(s32[2]{0:T(128)S(1)} %get-tuple-element.53.flag_ref, bf16[2,2,2,2,1024,1024]{5,4,3,2,1,0:T(8,128)(2,1)} %right_ref.7, bf16[2048,2048]{1,0:T(8,128)(2,1)} %grad_ref.1, bf16[2,2,2,2,1024,1024]{5,4,3,2,1,0:T(8,128)(2,1)} %right_ref.7, ...), custom_call_target="tpu_custom_call", output_to_operand_aliasing={{}: (5, {})} | custom-call | flops 8589934592 | bytes 20971520 | tf_op jit(solution)/shard_map/precondition_home/pallas_call | solution.py:107
  273.4 0.0 collective-permute-done.8.refs_8_
  273.4 46.5 %collective-permute-done.9.piece_ref = bf16[2048,1024]{1,0:T(8,128)(2,1)S(1)} collective-permute-done((bf16[2048,1024]{1,0:T(8,128)(2,1)S(1)}, bf16[2048,1024]{1,0:T(8,128)(2,1)S(1)}, u32[]{:S(2)}, u32[]{:S(2)}) %collective-permute-start.9) | collective-permute-done | bytes 4194336 | tf_op jit(solution)/shard_map/ppermute | solution.py:301
  320.0 1.9 copy-done.4
  321.9 2.0 collective-permute-start.10
  323.9 2.0 collective-permute-start.11
  325.9 8.3 %collective-permute-start.12 = (bf16[2048,1024]{1,0:T(8,128)(2,1)}, bf16[2048,1024]{1,0:T(8,128)(2,1)}, u32[]{:S(2)}, u32[]{:S(2)}) collective-permute-start(bf16[2048,1024]{1,0:T(8,128)(2,1)} %get-tuple-element.41), channel_id=1, source_target_pairs={{0,28},{4,0},{8,4},{12,8},{16,12},{20,16},{24,20},{28,24},{1,29},{... | collective-permute-start | bytes 12582920 | tf_op jit(solution)/shard_map/ppermute | solution.py:301
  334.2 0.1 reshape.10
  334.3 0.6 pad_add_fusion.1.place_ref
  334.9 0.6 pad_add_fusion.flag_ref
  335.6 10.7 %put_pairs.1.token_ref = bf16[2048,2048]{1,0:T(8,128)(2,1)} custom-call(s32[2]{0:T(128)} %pad_add_fusion.1.place_ref, bf16[512,2048]{1,0:T(8,128)(2,1)} %copy-done.2, bf16[512,2048]{1,0:T(8,128)(2,1)} %collective-permute-done.2.refs_1_, bf16[512,2048]{1,0:T(8,128)(2,1)} %collective-permute-done.3.refs_2_, bf16[512,2048]{1,0:T(8,128)(2,1)} %collective-permute-done.4.refs_3_, ...), custom_call_target="tpu_custom_call" | custom-call | flops 1000 | bytes 1000 | tf_op jit(solution)/shard_map/put_pairs/pallas_call | solution.py:247
  346.3 20.2 %finish_columns.3 = (bf16[2048,2048]{1,0:T(8,128)(2,1)}, bf16[2,512,1024]{2,1,0:T(8,128)(2,1)}, bf16[2,512,1024]{2,1,0:T(8,128)(2,1)}) custom-call(s32[5]{0:T(128)} %pad_add_fusion.flag_ref, bf16[2048,2048]{1,0:T(8,128)(2,1)} %precondition_home.3.weight_ref, bf16[2048,1024]{1,0:T(8,128)(2,1)} %copy-done.4, ...), custom_call_target="tpu_custom_call", output_to_operand_aliasing={{0}: (1, {})} | custom-call | flops 1000 | bytes 1000 | tf_op jit(solution)/shard_map/finish_columns/pallas_call | solution.py:176
  366.6 4.4 collective-permute-done.13
  370.9 2.5 convert_add_fusion
  373.4 1.9 copy-done
  375.4 0.2 fusion.1
  375.5 1.6 collective-permute-start.14
  377.1 47.3 %collective-permute-done.12.piece_ref = bf16[2048,1024]{1,0:T(8,128)(2,1)} collective-permute-done((bf16[2048,1024]{1,0:T(8,128)(2,1)}, bf16[2048,1024]{1,0:T(8,128)(2,1)}, u32[]{:S(2)}, u32[]{:S(2)}) %collective-permute-start.12) | collective-permute-done | bytes 4194336 | tf_op jit(solution)/shard_map/ppermute | solution.py:301
  424.4 11.9 %finish_columns.4 = (bf16[2048,2048]{1,0:T(8,128)(2,1)}, bf16[2,512,512]{2,1,0:T(8,128)(2,1)}, bf16[2,512,512]{2,1,0:T(8,128)(2,1)}) custom-call(s32[5]{0:T(128)} %pad_add_fusion.flag_ref, bf16[2048,2048]{1,0:T(8,128)(2,1)} %get-tuple-element.40.weight_ref, bf16[2048,1024]{1,0:T(8,128)(2,1)} %collective-permute-done.12.piece_ref, ...), custom_call_target="tpu_custom_call", output_to_operand_aliasing={{0}: (1, {})} | custom-call | flops 1000 | bytes 1000 | tf_op jit(solution)/shard_map/finish_columns/pallas_call | solution.py:176
  436.2 0.0 collective-permute-start.15
  436.2 0.0 collective-permute-done.14
  436.2 3.0 fusion.rest_1_
  439.2 12.0 %finish_columns.5 = (bf16[2048,2048]{1,0:T(8,128)(2,1)}, bf16[2,512,512]{2,1,0:T(8,128)(2,1)}, bf16[2,512,512]{2,1,0:T(8,128)(2,1)}) custom-call(s32[5]{0:T(128)} %pad_add_fusion.flag_ref, bf16[2048,2048]{1,0:T(8,128)(2,1)} %get-tuple-element.43.weight_ref, bf16[2048,1024]{1,0:T(8,128)(2,1)} %collective-permute-done.12.piece_ref, ...), custom_call_target="tpu_custom_call", output_to_operand_aliasing={{0}: (1, {})} | custom-call | flops 1000 | bytes 1000 | tf_op jit(solution)/shard_map/finish_columns/pallas_call | solution.py:176
  451.2 0.5 collective-permute-start.17
  451.7 0.0 collective-permute-done.15
  451.7 0.3 convert_add_fusion.2
  452.0 0.1 fusion.6
  452.1 1.3 collective-permute-start.16
  453.4 0.8 collective-permute-done.17
  454.2 0.3 convert_add_fusion.1
  454.5 0.1 fusion.7
  454.6 1.4 collective-permute-start.18
  456.0 0.2 dynamic_update_slice.9
  456.2 10.7 %collective-permute-done.16 = bf16[512,512]{1,0:T(8,128)(2,1)S(1)} collective-permute-done((bf16[512,512]{1,0:T(8,128)(2,1)S(1)}, bf16[512,512]{1,0:T(8,128)(2,1)S(1)}, u32[]{:S(2)}, u32[]{:S(2)}) %collective-permute-start.16) | collective-permute-done | bytes 524320 | tf_op jit(solution)/shard_map/ppermute | solution.py:270
  466.9 0.2 fusion.4
  467.1 10.1 %collective-permute-done.18 = bf16[512,512]{1,0:T(8,128)(2,1)S(1)} collective-permute-done((bf16[512,512]{1,0:T(8,128)(2,1)S(1)}, bf16[512,512]{1,0:T(8,128)(2,1)S(1)}, u32[]{:S(2)}, u32[]{:S(2)}) %collective-permute-start.18) | collective-permute-done | bytes 524320 | tf_op jit(solution)/shard_map/ppermute | solution.py:270
  477.2 0.2 fusion.5
  477.4 0.0 copy-start.5
  477.4 1.3 copy-done.5
  (18 shorter events, 0.0 us)
Async XLA Ops:
  0.6 26.4 %collective-permute-start = (bf16[256,2048]{1,0:T(8,128)(2,1)}, bf16[256,2048]{1,0:T(8,128)(2,1)S(1)}, u32[]{:S(2)}, u32[]{:S(2)}) collective-permute-start(bf16[256,2048]{1,0:T(8,128)(2,1)} %param.5), channel_id=1, source_target_pairs={{0,4},{4,0},{8,12},{12,8},{16,20},{20,16},{24,28},{28,24},{1,5},{5... | collective-permute-start | bytes 3145736 | tf_op jit(solution)/shard_map/ppermute | solution.py:202
  28.4 12.3 %copy-start.8 = (s32[8,16]{1,0:T(8,128)S(1)}, s32[8,16]{1,0:T(8,128)}, u32[]{:S(2)}) copy-start(s32[8,16]{1,0:T(8,128)} %param.9) | copy-start | bytes 1540
  28.5 195.2 %copy-start.2 = (bf16[512,2048]{1,0:T(8,128)(2,1)}, bf16[512,2048]{1,0:T(8,128)(2,1)S(1)}, u32[]{:S(2)}) copy-start(bf16[512,2048]{1,0:T(8,128)(2,1)S(1)} %pad_maximum_fusion.refs_0_) | copy-start | bytes 6291460
  28.5 185.8 %collective-permute-start.1 = (bf16[2048,2048]{1,0:T(8,128)(2,1)}, bf16[2048,2048]{1,0:T(8,128)(2,1)}, u32[]{:S(2)}, u32[]{:S(2)}) collective-permute-start(bf16[2048,2048]{1,0:T(8,128)(2,1)} %grad_ref.1), channel_id=1, source_target_pairs={{0,4},{4,8},{8,12},{12,16},{16,20},{20,24},{24,28},{28,0},{1,5},{5... | collective-permute-start | bytes 25165832 | tf_op jit(solution)/shard_map/ppermute | solution.py:292
  30.3 51.7 %collective-permute-start.4 = (bf16[512,2048]{1,0:T(8,128)(2,1)S(1)}, bf16[512,2048]{1,0:T(8,128)(2,1)}, u32[]{:S(2)}, u32[]{:S(2)}) collective-permute-start(bf16[512,2048]{1,0:T(8,128)(2,1)S(1)} %pad_maximum_fusion.refs_0_), channel_id=1, source_target_pairs={{0,24},{8,0},{16,8},{24,16},{1,25},{9,1},{17,9},{25,17},{2,26},{10... | collective-permute-start | bytes 6291464 | tf_op jit(solution)/shard_map/ppermute | solution.py:210
  35.8 178.5 %collective-permute-start.3 = (bf16[512,2048]{1,0:T(8,128)(2,1)S(1)}, bf16[512,2048]{1,0:T(8,128)(2,1)}, u32[]{:S(2)}, u32[]{:S(2)}) collective-permute-start(bf16[512,2048]{1,0:T(8,128)(2,1)S(1)} %pad_maximum_fusion.refs_0_), channel_id=1, source_target_pairs={{0,16},{8,24},{16,0},{24,8},{1,17},{9,25},{17,1},{25,9},{2,18},{10... | collective-permute-start | bytes 6291464 | tf_op jit(solution)/shard_map/ppermute | solution.py:210
  37.8 176.6 %collective-permute-start.2 = (bf16[512,2048]{1,0:T(8,128)(2,1)S(1)}, bf16[512,2048]{1,0:T(8,128)(2,1)}, u32[]{:S(2)}, u32[]{:S(2)}) collective-permute-start(bf16[512,2048]{1,0:T(8,128)(2,1)S(1)} %pad_maximum_fusion.refs_0_), channel_id=1, source_target_pairs={{0,8},{8,16},{16,24},{24,0},{1,9},{9,17},{17,25},{25,1},{2,10},{10... | collective-permute-start | bytes 6291464 | tf_op jit(solution)/shard_map/ppermute | solution.py:210
  214.4 19.3 %collective-permute-start.7 = (bf16[512,2048]{1,0:T(8,128)(2,1)S(1)}, bf16[512,2048]{1,0:T(8,128)(2,1)}, u32[]{:S(2)}, u32[]{:S(2)}) collective-permute-start(bf16[512,2048]{1,0:T(8,128)(2,1)S(1)} %pad_maximum_fusion.refs_0_), channel_id=1, source_target_pairs={{12,4},{20,12},{28,20},{13,5},{21,13},{29,21},{14,6},{22,14},{30,2... | collective-permute-start | bytes 6291464 | tf_op jit(solution)/shard_map/ppermute | solution.py:217
  216.4 19.3 %collective-permute-start.5 = (bf16[512,2048]{1,0:T(8,128)(2,1)S(1)}, bf16[512,2048]{1,0:T(8,128)(2,1)}, u32[]{:S(2)}, u32[]{:S(2)}) collective-permute-start(bf16[512,2048]{1,0:T(8,128)(2,1)S(1)} %pad_maximum_fusion.refs_0_), channel_id=1, source_target_pairs={{4,12},{12,20},{20,28},{5,13},{13,21},{21,29},{6,14},{14,22},{22,3... | collective-permute-start | bytes 6291464 | tf_op jit(solution)/shard_map/ppermute | solution.py:216
  223.7 96.2 %collective-permute-start.9 = (bf16[2048,1024]{1,0:T(8,128)(2,1)S(1)}, bf16[2048,1024]{1,0:T(8,128)(2,1)S(1)}, u32[]{:S(2)}, u32[]{:S(2)}) collective-permute-start(bf16[2048,1024]{1,0:T(8,128)(2,1)S(1)} %get-tuple-element.30), channel_id=1, source_target_pairs={{0,28},{4,0},{8,4},{12,8},{16,12},{20,16},{24,20},{28,24},{1,29},{... | collective-permute-start | bytes 12582920 | tf_op jit(solution)/shard_map/ppermute | solution.py:301
  233.7 39.7 %collective-permute-start.8 = (bf16[512,2048]{1,0:T(8,128)(2,1)}, bf16[512,2048]{1,0:T(8,128)(2,1)}, u32[]{:S(2)}, u32[]{:S(2)}) collective-permute-start(bf16[512,2048]{1,0:T(8,128)(2,1)} %collective-permute-done.7.refs_7_), channel_id=1, source_target_pairs={{12,4},{20,12},{28,20},{13,5},{21,13},{29,21},{14,6},{22,14},{30,2... | collective-permute-start | bytes 6291464 | tf_op jit(solution)/shard_map/ppermute | solution.py:217
  235.7 37.7 %collective-permute-start.6 = (bf16[512,2048]{1,0:T(8,128)(2,1)}, bf16[512,2048]{1,0:T(8,128)(2,1)S(1)}, u32[]{:S(2)}, u32[]{:S(2)}) collective-permute-start(bf16[512,2048]{1,0:T(8,128)(2,1)} %collective-permute-done.5.refs_4_), channel_id=1, source_target_pairs={{4,12},{12,20},{20,28},{5,13},{13,21},{21,29},{6,14},{14,22},{22,3... | collective-permute-start | bytes 6291464 | tf_op jit(solution)/shard_map/ppermute | solution.py:216
  273.4 62.2 %copy-start.6 = (bf16[512,2048]{1,0:T(8,128)(2,1)}, bf16[512,2048]{1,0:T(8,128)(2,1)S(1)}, u32[]{:S(2)}) copy-start(bf16[512,2048]{1,0:T(8,128)(2,1)S(1)} %collective-permute-done.6.refs_5_) | copy-start | bytes 6291460
  320.0 1.9 copy-start.4
  321.9 13.7 %collective-permute-start.10 = (bf16[512,2048]{1,0:T(8,128)(2,1)S(1)}, bf16[512,2048]{1,0:T(8,128)(2,1)}, u32[]{:S(2)}, u32[]{:S(2)}) collective-permute-start(bf16[512,2048]{1,0:T(8,128)(2,1)S(1)} %collective-permute-done.6.refs_5_), channel_id=1, source_target_pairs={{4,12},{12,20},{20,28},{5,13},{13,21},{21,29},{6,14},{14,22},{22,3... | collective-permute-start | bytes 6291464 | tf_op jit(solution)/shard_map/ppermute | solution.py:216
  323.9 11.6 %collective-permute-start.11 = (bf16[512,2048]{1,0:T(8,128)(2,1)}, bf16[512,2048]{1,0:T(8,128)(2,1)}, u32[]{:S(2)}, u32[]{:S(2)}) collective-permute-start(bf16[512,2048]{1,0:T(8,128)(2,1)} %collective-permute-done.8.refs_8_), channel_id=1, source_target_pairs={{12,4},{20,12},{28,20},{13,5},{21,13},{29,21},{14,6},{22,14},{30,2... | collective-permute-start | bytes 6291464 | tf_op jit(solution)/shard_map/ppermute | solution.py:217
  325.9 98.5 %collective-permute-start.12 = (bf16[2048,1024]{1,0:T(8,128)(2,1)}, bf16[2048,1024]{1,0:T(8,128)(2,1)}, u32[]{:S(2)}, u32[]{:S(2)}) collective-permute-start(bf16[2048,1024]{1,0:T(8,128)(2,1)} %get-tuple-element.41), channel_id=1, source_target_pairs={{0,28},{4,0},{8,4},{12,8},{16,12},{20,16},{24,20},{28,24},{1,29},{... | collective-permute-start | bytes 12582920 | tf_op jit(solution)/shard_map/ppermute | solution.py:301
  366.5 4.4 collective-permute-start.13
  373.4 1.9 copy-start
  375.5 60.7 %collective-permute-start.14 = (bf16[512,1024]{1,0:T(8,128)(2,1)S(1)}, bf16[512,1024]{1,0:T(8,128)(2,1)S(1)}, u32[]{:S(2)}, u32[]{:S(2)}) collective-permute-start(bf16[512,1024]{1,0:T(8,128)(2,1)S(1)} %fusion.1), channel_id=1, source_target_pairs={{0,2},{1,3},{2,0},{3,1},{4,6},{5,7},{6,4},{7,5},{8,10},{9,11},{10,... | collective-permute-start | bytes 3145736 | tf_op jit(solution)/shard_map/ppermute | solution.py:270
  436.2 15.5 %collective-permute-start.15 = (bf16[2,512,512]{2,1,0:T(8,128)(2,1)}, bf16[2,512,512]{2,1,0:T(8,128)(2,1)S(1)}, u32[]{:S(2)}, u32[]{:S(2)}) collective-permute-start(bf16[2,512,512]{2,1,0:T(8,128)(2,1)} %get-tuple-element.47), channel_id=1, source_target_pairs={{0,1},{1,0},{2,3},{3,2},{4,5},{5,4},{6,7},{7,6},{8,9},{9,8},{10,11... | collective-permute-start | bytes 3145736 | tf_op jit(solution)/shard_map/ppermute | solution.py:328
  439.2 12.5 %copy-start.3 = (bf16[2,512,512]{2,1,0:T(8,128)(2,1)S(1)}, bf16[2,512,512]{2,1,0:T(8,128)(2,1)}, u32[]{:S(2)}) copy-start(bf16[2,512,512]{2,1,0:T(8,128)(2,1)} %get-tuple-element.44.rest_0_) | copy-start | bytes 3145732
  451.2 3.0 copy-start.7
  451.2 3.0 collective-permute-start.17
  452.1 14.8 %collective-permute-start.16 = (bf16[512,512]{1,0:T(8,128)(2,1)S(1)}, bf16[512,512]{1,0:T(8,128)(2,1)S(1)}, u32[]{:S(2)}, u32[]{:S(2)}) collective-permute-start(bf16[512,512]{1,0:T(8,128)(2,1)S(1)} %fusion.6), channel_id=1, source_target_pairs={{0,2},{1,3},{2,0},{3,1},{4,6},{5,7},{6,4},{7,5},{8,10},{9,11},{10,... | collective-permute-start | bytes 1572872 | tf_op jit(solution)/shard_map/ppermute | solution.py:270
  454.2 1.8 copy-start.1
  454.6 22.6 %collective-permute-start.18 = (bf16[512,512]{1,0:T(8,128)(2,1)S(1)}, bf16[512,512]{1,0:T(8,128)(2,1)S(1)}, u32[]{:S(2)}, u32[]{:S(2)}) collective-permute-start(bf16[512,512]{1,0:T(8,128)(2,1)S(1)} %fusion.7), channel_id=1, source_target_pairs={{0,2},{1,3},{2,0},{3,1},{4,6},{5,7},{6,4},{7,5},{8,10},{9,11},{10,... | collective-permute-start | bytes 1572872 | tf_op jit(solution)/shard_map/ppermute | solution.py:270
  477.4 1.3 copy-start.5

commit v3 on v2

--- a/solution.py
+++ b/solution.py
@@ -76,7 +76,7 @@
             out_specs=[pl.BlockSpec((width, stop - start), lambda p, f: (p, 0)) for start, stop in pieces]
             + [pl.BlockSpec((8, 128), lambda p, f: (0, 0))],
         ),
-        compiler_params=pltpu.CompilerParams(vmem_limit_bytes=40 << 20),
+        compiler_params=pltpu.CompilerParams(vmem_limit_bytes=60 << 20),
         cost_estimate=cost(down, width, 4),
         name="precondition_lent",
     )(flags, roots, came, roots, *later_than)
@@ -120,8 +120,8 @@
             out_specs=tiles,
         ),
         input_output_aliases={} if new_weight is None else {5: 0},
-        compiler_params=pltpu.CompilerParams(vmem_limit_bytes=48 << 20),
-        cost_estimate=cost(down, width, 5),
+        compiler_params=pltpu.CompilerParams(vmem_limit_bytes=60 << 20),
+        cost_estimate=cost(2 * down, width, 5),
         name="precondition_home",
     )(kept_column, roots, grad, roots, weight, *extra)
 
@@ -291,25 +291,26 @@
     swapped, grad = together(swapped, grad)
     came = lax.ppermute(grad, "row", forth)
     early = ring_direct(swapped, row_count, 0)
-    came, late_pair, *early = together(came, swapped, *early)
+    new_weight = precondition_home(kept[:, 0], roots, grad, weight, 0, None, ())
+    came, late_pair, new_weight, *early = together(came, swapped, new_weight, *early)
 
     returned = []
-    new_weight = None
+    up, down_piece = line_step(late_pair, late_pair, row_count, 1)
+    late = [(up, down_piece)]
+    returned = []
+    later_than = ()
     for q in range(across):
-        later_than = () if new_weight is None else (new_weight,)
         lent, mark = precondition_lent(taken[:, q], roots, q, came, (0, width), later_than)
         returned.append(lax.ppermute(lent, "row", back))
-        new_weight = precondition_home(kept[:, q], roots, grad, weight, q, new_weight, (mark,))
-
-    late = []
-    up = down_piece = late_pair
-    first_piece = returned[0]
-    for step in range(1, row_count // 2):
+        later_than = (mark,)
+        if q > 0:
+            new_weight = precondition_home(kept[:, q], roots, grad, weight, q, new_weight, later_than)
+
+    for step in range(2, row_count // 2):
         if step == row_count // 2 - 1:
-            up, down_piece, first_piece, new_weight = together(up, down_piece, first_piece, new_weight)
+            up, down_piece, new_weight = together(up, down_piece, new_weight)
         up, down_piece = line_step(up, down_piece, row_count, 1)
         late.append((up, down_piece))
-    returned[0] = first_piece
     all_tokens = put_pairs(swapped, early, late, row_place)
     output = jnp.zeros((all_tokens.shape[0] // col_count, weight.shape[1]), jnp.bfloat16)
 

time: 485 us -> 469 us (0.967)
  waiting for transfers between devices: 316 us -> 258 us
  starting transfers between devices: 48.9 us -> 90.3 us
  Pallas kernels: 97.1 us -> 104 us
    ppermute x2, waiting for transfers between devices: 93.8 us -> 49.7 us  [on_device(): returned.append(lax.ppermute(lent, 'row', back))]
    ppermute x2, starting transfers between devices: 18.1 us -> 61.1 us  [on_device(): returned.append(lax.ppermute(lent, 'row', back))]
    ppermute x3, waiting for transfers between devices: 173 us -> 157 us  [ring_direct(): lax.ppermute(pair, 'row', [(i, (i + 2 * step) % row_count) for i in sides])]
  transfers between devices with their start and end apart: 19 -> 19, of which waited for: 9 -> 8; matrix products, arithmetic and copies ran while one was open for 2% -> 2% of each run, Pallas kernels for 20% -> 22%
where the time goes in v3:
time: 469 us; the launch traced here: 467 us
  waiting for transfers between devices  258 us (55%)
  Pallas kernels  104 us (22%)
  starting transfers between devices  90.3 us (19%)
  other arithmetic  9.15 us (2%)
  local copies, waits for them, and re-layouts  5.1 us (1%)
    ppermute x3, waiting for transfers between devices, ring_direct(): lax.ppermute(pair, 'row', [(i, (i + 2 * step) % row_count) for i in sides])  157 us
    ppermute x2, starting transfers between devices, on_device(): returned.append(lax.ppermute(lent, 'row', back))  61.1 us
    ppermute x2, waiting for transfers between devices, on_device(): returned.append(lax.ppermute(lent, 'row', back))  49.7 us
    pallas_call x3, Pallas kernels, finish_columns(): pl.pallas_call(kernel, out_shape=(jax.ShapeDtypeStruct(new_weight.shape,...  43.6 us
    pallas_call x2, Pallas kernels, precondition_home(): pl.pallas_call(kernel, out_shape=jax.ShapeDtypeStruct(weight.shape, jnp.b...  26.8 us
    ppermute x1, waiting for transfers between devices, swap_tokens(): other = lax.ppermute(tokens, 'row', pair_route(row_count))  23.4 us
    pallas_call x2, Pallas kernels, precondition_lent(): pl.pallas_call(kernel, out_shape=[jax.ShapeDtypeStruct((down * width, sto...  22.5 us
    ppermute x3, waiting for transfers between devices, far_sum(): lax.ppermute(piece, 'col', shift_route(col_count, 2 * step))  21.5 us
  transfers between devices with their start and end apart: 19, of which 8 were waited for; matrix products, arithmetic and copies ran while one was open for 2% of the time, Pallas kernels for 22%

profile of v3, /device:TPU:0, one launch (start us, length us, event | category | flops | bytes accessed | tf_op | source)
XLA Modules:
  0.0 466.9 jit_solution(14086646998915898020)
XLA Ops:
  0.6 3.0 collective-permute-start
  3.6 23.4 %collective-permute-done = bf16[256,2048]{1,0:T(8,128)(2,1)S(1)} collective-permute-done((bf16[256,2048]{1,0:T(8,128)(2,1)}, bf16[256,2048]{1,0:T(8,128)(2,1)S(1)}, u32[]{:S(2)}, u32[]{:S(2)}) %collective-permute-start) | collective-permute-done | bytes 1048608 | tf_op jit(solution)/shard_map/ppermute | solution.py:202
  27.0 1.4 broadcast_select_fusion.1
  28.4 0.0 copy-start.7
  28.4 0.1 pad_maximum_fusion.refs_0_
  28.5 0.0 copy-start.2
  28.5 1.8 collective-permute-start.1
  30.3 5.5 %collective-permute-start.4 = (bf16[512,2048]{1,0:T(8,128)(2,1)S(1)}, bf16[512,2048]{1,0:T(8,128)(2,1)}, u32[]{:S(2)}, u32[]{:S(2)}) collective-permute-start(bf16[512,2048]{1,0:T(8,128)(2,1)S(1)} %pad_maximum_fusion.refs_0_), channel_id=1, source_target_pairs={{0,24},{8,0},{16,8},{24,16},{1,25},{9,1},{17,9},{25,17},{2,26},{10... | collective-permute-start | bytes 6291464 | tf_op jit(solution)/shard_map/ppermute | solution.py:210
  35.8 1.9 collective-permute-start.3
  37.8 2.9 collective-permute-start.2
  40.7 0.1 compare_convert_fusion
  40.8 0.8 slice_reduce_fusion
  41.6 15.6 %precondition_home.2.rest_0_ = bf16[2048,2048]{1,0:T(8,128)(2,1)} custom-call(s32[2]{0:T(128)} %get-tuple-element.58.flag_ref, bf16[2,2,2,2,1024,1024]{5,4,3,2,1,0:T(8,128)(2,1)} %right_ref.7, bf16[2048,2048]{1,0:T(8,128)(2,1)} %grad_ref.1, bf16[2,2,2,2,1024,1024]{5,4,3,2,1,0:T(8,128)(2,1)} %right_ref.7, bf16[2048,2048]{1,0:T(8,128)(2,1)} %weight_ref.3), custom_call_target="tpu_custom_call" | custom-call | flops 17179869184 | bytes 41943040 | tf_op jit(solution)/shard_map/precondition_home/pallas_call | solution.py:107
  57.2 24.8 %collective-permute-done.4.refs_3_ = bf16[512,2048]{1,0:T(8,128)(2,1)} collective-permute-done((bf16[512,2048]{1,0:T(8,128)(2,1)S(1)}, bf16[512,2048]{1,0:T(8,128)(2,1)}, u32[]{:S(2)}, u32[]{:S(2)}) %collective-permute-start.4) | collective-permute-done | bytes 2097184 | tf_op jit(solution)/shard_map/ppermute | solution.py:210
  82.0 132.4 %collective-permute-done.3.refs_2_ = bf16[512,2048]{1,0:T(8,128)(2,1)} collective-permute-done((bf16[512,2048]{1,0:T(8,128)(2,1)S(1)}, bf16[512,2048]{1,0:T(8,128)(2,1)}, u32[]{:S(2)}, u32[]{:S(2)}) %collective-permute-start.3) | collective-permute-done | bytes 2097184 | tf_op jit(solution)/shard_map/ppermute | solution.py:210
  214.4 0.0 collective-permute-done.2.refs_1_
  214.4 2.0 collective-permute-start.7
  216.3 2.0 collective-permute-start.5
  218.3 14.9 %precondition_lent.2 = (bf16[2048,1024]{1,0:T(8,128)(2,1)}, f32[8,128]{1,0:T(8,128)}) custom-call(s32[2]{0:T(128)} %get-tuple-element.50.flag_ref, bf16[2,2,2,2,1024,1024]{5,4,3,2,1,0:T(8,128)(2,1)} %right_ref.7, bf16[2048,2048]{1,0:T(8,128)(2,1)} %collective-permute-done.1.grad_ref, bf16[2,2,2,2,1024,1024]{5,4,3,2,1,0:T(8,128)(2,1)} %right_ref.7), custom_call_target="tpu_custom_call" | custom-call | flops 8589934592 | bytes 16777216 | tf_op jit(solution)/shard_map/precondition_lent/pallas_call | solution.py:63
  233.2 0.0 collective-permute-start.9
  233.3 0.0 collective-permute-done.7.refs_7_
  233.3 2.1 collective-permute-start.8
  235.3 0.8 collective-permute-start.6
  236.1 7.5 %precondition_lent.3 = (bf16[2048,1024]{1,0:T(8,128)(2,1)}, f32[8,128]{1,0:T(8,128)}) custom-call(s32[2]{0:T(128)} %get-tuple-element.51.flag_ref, bf16[2,2,2,2,1024,1024]{5,4,3,2,1,0:T(8,128)(2,1)} %right_ref.7, bf16[2048,2048]{1,0:T(8,128)(2,1)} %collective-permute-done.1.grad_ref, bf16[2,2,2,2,1024,1024]{5,4,3,2,1,0:T(8,128)(2,1)} %right_ref.7, ...), custom_call_target="tpu_custom_call" | custom-call | flops 8589934592 | bytes 16777216 | tf_op jit(solution)/shard_map/precondition_lent/pallas_call | solution.py:63
  243.7 11.2 %precondition_home.3.weight_ref = bf16[2048,2048]{1,0:T(8,128)(2,1)} custom-call(s32[2]{0:T(128)} %get-tuple-element.59.flag_ref, bf16[2,2,2,2,1024,1024]{5,4,3,2,1,0:T(8,128)(2,1)} %right_ref.7, bf16[2048,2048]{1,0:T(8,128)(2,1)} %grad_ref.1, bf16[2,2,2,2,1024,1024]{5,4,3,2,1,0:T(8,128)(2,1)} %right_ref.7, ...), custom_call_target="tpu_custom_call", output_to_operand_aliasing={{}: (5, {})} | custom-call | flops 17179869184 | bytes 41943040 | tf_op jit(solution)/shard_map/precondition_home/pallas_call | solution.py:107
  254.9 2.0 collective-permute-start.10
  256.9 2.0 collective-permute-start.11
  258.9 61.1 %collective-permute-start.12 = (bf16[2048,1024]{1,0:T(8,128)(2,1)}, bf16[2048,1024]{1,0:T(8,128)(2,1)}, u32[]{:S(2)}, u32[]{:S(2)}) collective-permute-start(bf16[2048,1024]{1,0:T(8,128)(2,1)} %get-tuple-element.41), channel_id=1, source_target_pairs={{0,28},{4,0},{8,4},{12,8},{16,12},{20,16},{24,20},{28,24},{1,29},{... | collective-permute-start | bytes 12582920 | tf_op jit(solution)/shard_map/ppermute | solution.py:304
  320.0 0.1 reshape.10
  320.1 0.6 pad_add_fusion.1.place_ref
  320.7 0.6 pad_add_fusion.flag_ref
  321.3 0.0 collective-permute-done.10.refs_6_
  321.3 0.0 collective-permute-done.11.refs_9_
  321.3 10.7 %put_pairs.1.token_ref = bf16[2048,2048]{1,0:T(8,128)(2,1)} custom-call(s32[2]{0:T(128)} %pad_add_fusion.1.place_ref, bf16[512,2048]{1,0:T(8,128)(2,1)} %copy-done.2, bf16[512,2048]{1,0:T(8,128)(2,1)} %collective-permute-done.2.refs_1_, bf16[512,2048]{1,0:T(8,128)(2,1)} %collective-permute-done.3.refs_2_, bf16[512,2048]{1,0:T(8,128)(2,1)} %collective-permute-done.4.refs_3_, ...), custom_call_target="tpu_custom_call" | custom-call | flops 1000 | bytes 1000 | tf_op jit(solution)/shard_map/put_pairs/pallas_call | solution.py:247
  332.0 19.8 %finish_columns.3 = (bf16[2048,2048]{1,0:T(8,128)(2,1)}, bf16[2,512,1024]{2,1,0:T(8,128)(2,1)}, bf16[2,512,1024]{2,1,0:T(8,128)(2,1)}) custom-call(s32[5]{0:T(128)} %pad_add_fusion.flag_ref, bf16[2048,2048]{1,0:T(8,128)(2,1)} %precondition_home.3.weight_ref, bf16[2048,1024]{1,0:T(8,128)(2,1)} %collective-permute-done.9.piece_ref, ...), custom_call_target="tpu_custom_call", output_to_operand_aliasing={{0}: (1, {})} | custom-call | flops 1000 | bytes 1000 | tf_op jit(solution)/shard_map/finish_columns/pallas_call | solution.py:176
  351.8 0.0 collective-permute-start.13
  351.8 4.4 collective-permute-done.13
  356.1 2.5 convert_add_fusion
  358.6 2.0 copy-done
  360.6 0.2 fusion.1
  360.8 2.0 collective-permute-start.14
  362.8 49.7 %collective-permute-done.12.piece_ref = bf16[2048,1024]{1,0:T(8,128)(2,1)} collective-permute-done((bf16[2048,1024]{1,0:T(8,128)(2,1)}, bf16[2048,1024]{1,0:T(8,128)(2,1)}, u32[]{:S(2)}, u32[]{:S(2)}) %collective-permute-start.12) | collective-permute-done | bytes 4194336 | tf_op jit(solution)/shard_map/ppermute | solution.py:304
  412.5 11.9 %finish_columns.4 = (bf16[2048,2048]{1,0:T(8,128)(2,1)}, bf16[2,512,512]{2,1,0:T(8,128)(2,1)}, bf16[2,512,512]{2,1,0:T(8,128)(2,1)}) custom-call(s32[5]{0:T(128)} %pad_add_fusion.flag_ref, bf16[2048,2048]{1,0:T(8,128)(2,1)} %get-tuple-element.40.weight_ref, bf16[2048,1024]{1,0:T(8,128)(2,1)} %collective-permute-done.12.piece_ref, ...), custom_call_target="tpu_custom_call", output_to_operand_aliasing={{0}: (1, {})} | custom-call | flops 1000 | bytes 1000 | tf_op jit(solution)/shard_map/finish_columns/pallas_call | solution.py:176
  424.4 0.0 collective-permute-start.15
  424.4 0.0 collective-permute-done.14
  424.4 3.0 fusion.rest_1_
  427.4 12.0 %finish_columns.5 = (bf16[2048,2048]{1,0:T(8,128)(2,1)}, bf16[2,512,512]{2,1,0:T(8,128)(2,1)}, bf16[2,512,512]{2,1,0:T(8,128)(2,1)}) custom-call(s32[5]{0:T(128)} %pad_add_fusion.flag_ref, bf16[2048,2048]{1,0:T(8,128)(2,1)} %get-tuple-element.43.weight_ref, bf16[2048,1024]{1,0:T(8,128)(2,1)} %collective-permute-done.12.piece_ref, ...), custom_call_target="tpu_custom_call", output_to_operand_aliasing={{0}: (1, {})} | custom-call | flops 1000 | bytes 1000 | tf_op jit(solution)/shard_map/finish_columns/pallas_call | solution.py:176
  439.4 0.3 collective-permute-start.17
  439.6 0.0 collective-permute-done.15
  439.6 0.3 convert_add_fusion.2
  439.9 0.1 fusion.6
  440.0 0.5 collective-permute-start.16
  440.5 1.7 collective-permute-done.17
  442.2 0.3 convert_add_fusion.1
  442.5 0.1 fusion.7
  442.6 0.4 collective-permute-start.18
  443.0 0.4 copy-done.1
  443.5 0.2 dynamic_update_slice.9
  443.7 11.1 %collective-permute-done.16 = bf16[512,512]{1,0:T(8,128)(2,1)S(1)} collective-permute-done((bf16[512,512]{1,0:T(8,128)(2,1)S(1)}, bf16[512,512]{1,0:T(8,128)(2,1)S(1)}, u32[]{:S(2)}, u32[]{:S(2)}) %collective-permute-start.16) | collective-permute-done | bytes 524320 | tf_op jit(solution)/shard_map/ppermute | solution.py:270
  454.8 0.2 fusion.4
  455.0 10.4 %collective-permute-done.18 = bf16[512,512]{1,0:T(8,128)(2,1)S(1)} collective-permute-done((bf16[512,512]{1,0:T(8,128)(2,1)S(1)}, bf16[512,512]{1,0:T(8,128)(2,1)S(1)}, u32[]{:S(2)}, u32[]{:S(2)}) %collective-permute-start.18) | collective-permute-done | bytes 524320 | tf_op jit(solution)/shard_map/ppermute | solution.py:270
  465.4 0.2 fusion.5
  465.6 0.0 copy-start.4
  465.6 1.3 copy-done.4
  (15 shorter events, 0.0 us)
Async XLA Ops:
  0.6 26.4 %collective-permute-start = (bf16[256,2048]{1,0:T(8,128)(2,1)}, bf16[256,2048]{1,0:T(8,128)(2,1)S(1)}, u32[]{:S(2)}, u32[]{:S(2)}) collective-permute-start(bf16[256,2048]{1,0:T(8,128)(2,1)} %param.5), channel_id=1, source_target_pairs={{0,4},{4,0},{8,12},{12,8},{16,20},{20,16},{24,28},{28,24},{1,5},{5... | collective-permute-start | bytes 3145736 | tf_op jit(solution)/shard_map/ppermute | solution.py:202
  28.4 12.3 %copy-start.7 = (s32[8,16]{1,0:T(8,128)S(1)}, s32[8,16]{1,0:T(8,128)}, u32[]{:S(2)}) copy-start(s32[8,16]{1,0:T(8,128)} %param.9) | copy-start | bytes 1540
  28.5 187.8 %copy-start.2 = (bf16[512,2048]{1,0:T(8,128)(2,1)}, bf16[512,2048]{1,0:T(8,128)(2,1)S(1)}, u32[]{:S(2)}) copy-start(bf16[512,2048]{1,0:T(8,128)(2,1)S(1)} %pad_maximum_fusion.refs_0_) | copy-start | bytes 6291460
  28.5 185.8 %collective-permute-start.1 = (bf16[2048,2048]{1,0:T(8,128)(2,1)}, bf16[2048,2048]{1,0:T(8,128)(2,1)}, u32[]{:S(2)}, u32[]{:S(2)}) collective-permute-start(bf16[2048,2048]{1,0:T(8,128)(2,1)} %grad_ref.1), channel_id=1, source_target_pairs={{0,4},{4,8},{8,12},{12,16},{16,20},{20,24},{24,28},{28,0},{1,5},{5... | collective-permute-start | bytes 25165832 | tf_op jit(solution)/shard_map/ppermute | solution.py:292
  30.3 51.7 %collective-permute-start.4 = (bf16[512,2048]{1,0:T(8,128)(2,1)S(1)}, bf16[512,2048]{1,0:T(8,128)(2,1)}, u32[]{:S(2)}, u32[]{:S(2)}) collective-permute-start(bf16[512,2048]{1,0:T(8,128)(2,1)S(1)} %pad_maximum_fusion.refs_0_), channel_id=1, source_target_pairs={{0,24},{8,0},{16,8},{24,16},{1,25},{9,1},{17,9},{25,17},{2,26},{10... | collective-permute-start | bytes 6291464 | tf_op jit(solution)/shard_map/ppermute | solution.py:210
  35.8 178.5 %collective-permute-start.3 = (bf16[512,2048]{1,0:T(8,128)(2,1)S(1)}, bf16[512,2048]{1,0:T(8,128)(2,1)}, u32[]{:S(2)}, u32[]{:S(2)}) collective-permute-start(bf16[512,2048]{1,0:T(8,128)(2,1)S(1)} %pad_maximum_fusion.refs_0_), channel_id=1, source_target_pairs={{0,16},{8,24},{16,0},{24,8},{1,17},{9,25},{17,1},{25,9},{2,18},{10... | collective-permute-start | bytes 6291464 | tf_op jit(solution)/shard_map/ppermute | solution.py:210
  37.8 176.6 %collective-permute-start.2 = (bf16[512,2048]{1,0:T(8,128)(2,1)S(1)}, bf16[512,2048]{1,0:T(8,128)(2,1)}, u32[]{:S(2)}, u32[]{:S(2)}) collective-permute-start(bf16[512,2048]{1,0:T(8,128)(2,1)S(1)} %pad_maximum_fusion.refs_0_), channel_id=1, source_target_pairs={{0,8},{8,16},{16,24},{24,0},{1,9},{9,17},{17,25},{25,1},{2,10},{10... | collective-permute-start | bytes 6291464 | tf_op jit(solution)/shard_map/ppermute | solution.py:210
  214.4 18.9 %collective-permute-start.7 = (bf16[512,2048]{1,0:T(8,128)(2,1)S(1)}, bf16[512,2048]{1,0:T(8,128)(2,1)}, u32[]{:S(2)}, u32[]{:S(2)}) collective-permute-start(bf16[512,2048]{1,0:T(8,128)(2,1)S(1)} %pad_maximum_fusion.refs_0_), channel_id=1, source_target_pairs={{12,4},{20,12},{28,20},{13,5},{21,13},{29,21},{14,6},{22,14},{30,2... | collective-permute-start | bytes 6291464 | tf_op jit(solution)/shard_map/ppermute | solution.py:217
  216.3 19.0 %collective-permute-start.5 = (bf16[512,2048]{1,0:T(8,128)(2,1)S(1)}, bf16[512,2048]{1,0:T(8,128)(2,1)}, u32[]{:S(2)}, u32[]{:S(2)}) collective-permute-start(bf16[512,2048]{1,0:T(8,128)(2,1)S(1)} %pad_maximum_fusion.refs_0_), channel_id=1, source_target_pairs={{4,12},{12,20},{20,28},{5,13},{13,21},{21,29},{6,14},{14,22},{22,3... | collective-permute-start | bytes 6291464 | tf_op jit(solution)/shard_map/ppermute | solution.py:216
  233.2 98.7 %collective-permute-start.9 = (bf16[2048,1024]{1,0:T(8,128)(2,1)}, bf16[2048,1024]{1,0:T(8,128)(2,1)}, u32[]{:S(2)}, u32[]{:S(2)}) collective-permute-start(bf16[2048,1024]{1,0:T(8,128)(2,1)} %get-tuple-element.34), channel_id=1, source_target_pairs={{0,28},{4,0},{8,4},{12,8},{16,12},{20,16},{24,20},{28,24},{1,29},{... | collective-permute-start | bytes 12582920 | tf_op jit(solution)/shard_map/ppermute | solution.py:304
  233.3 21.6 %collective-permute-start.8 = (bf16[512,2048]{1,0:T(8,128)(2,1)}, bf16[512,2048]{1,0:T(8,128)(2,1)}, u32[]{:S(2)}, u32[]{:S(2)}) collective-permute-start(bf16[512,2048]{1,0:T(8,128)(2,1)} %collective-permute-done.7.refs_7_), channel_id=1, source_target_pairs={{12,4},{20,12},{28,20},{13,5},{21,13},{29,21},{14,6},{22,14},{30,2... | collective-permute-start | bytes 6291464 | tf_op jit(solution)/shard_map/ppermute | solution.py:217
  235.3 19.5 %collective-permute-start.6 = (bf16[512,2048]{1,0:T(8,128)(2,1)}, bf16[512,2048]{1,0:T(8,128)(2,1)S(1)}, u32[]{:S(2)}, u32[]{:S(2)}) collective-permute-start(bf16[512,2048]{1,0:T(8,128)(2,1)} %collective-permute-done.5.refs_4_), channel_id=1, source_target_pairs={{4,12},{12,20},{20,28},{5,13},{13,21},{21,29},{6,14},{14,22},{22,3... | collective-permute-start | bytes 6291464 | tf_op jit(solution)/shard_map/ppermute | solution.py:216
  254.9 66.4 %copy-start.5 = (bf16[512,2048]{1,0:T(8,128)(2,1)}, bf16[512,2048]{1,0:T(8,128)(2,1)S(1)}, u32[]{:S(2)}) copy-start(bf16[512,2048]{1,0:T(8,128)(2,1)S(1)} %collective-permute-done.6.refs_5_) | copy-start | bytes 6291460
  254.9 66.4 %collective-permute-start.10 = (bf16[512,2048]{1,0:T(8,128)(2,1)S(1)}, bf16[512,2048]{1,0:T(8,128)(2,1)}, u32[]{:S(2)}, u32[]{:S(2)}) collective-permute-start(bf16[512,2048]{1,0:T(8,128)(2,1)S(1)} %collective-permute-done.6.refs_5_), channel_id=1, source_target_pairs={{4,12},{12,20},{20,28},{5,13},{13,21},{21,29},{6,14},{14,22},{22,3... | collective-permute-start | bytes 6291464 | tf_op jit(solution)/shard_map/ppermute | solution.py:216
  256.9 64.3 %collective-permute-start.11 = (bf16[512,2048]{1,0:T(8,128)(2,1)}, bf16[512,2048]{1,0:T(8,128)(2,1)}, u32[]{:S(2)}, u32[]{:S(2)}) collective-permute-start(bf16[512,2048]{1,0:T(8,128)(2,1)} %collective-permute-done.8.refs_8_), channel_id=1, source_target_pairs={{12,4},{20,12},{28,20},{13,5},{21,13},{29,21},{14,6},{22,14},{30,2... | collective-permute-start | bytes 6291464 | tf_op jit(solution)/shard_map/ppermute | solution.py:217
  258.9 153.6 %collective-permute-start.12 = (bf16[2048,1024]{1,0:T(8,128)(2,1)}, bf16[2048,1024]{1,0:T(8,128)(2,1)}, u32[]{:S(2)}, u32[]{:S(2)}) collective-permute-start(bf16[2048,1024]{1,0:T(8,128)(2,1)} %get-tuple-element.41), channel_id=1, source_target_pairs={{0,28},{4,0},{8,4},{12,8},{16,12},{20,16},{24,20},{28,24},{1,29},{... | collective-permute-start | bytes 12582920 | tf_op jit(solution)/shard_map/ppermute | solution.py:304
  351.8 4.4 collective-permute-start.13
  358.6 2.0 copy-start
  360.8 63.6 %collective-permute-start.14 = (bf16[512,1024]{1,0:T(8,128)(2,1)S(1)}, bf16[512,1024]{1,0:T(8,128)(2,1)S(1)}, u32[]{:S(2)}, u32[]{:S(2)}) collective-permute-start(bf16[512,1024]{1,0:T(8,128)(2,1)S(1)} %fusion.1), channel_id=1, source_target_pairs={{0,2},{1,3},{2,0},{3,1},{4,6},{5,7},{6,4},{7,5},{8,10},{9,11},{10,... | collective-permute-start | bytes 3145736 | tf_op jit(solution)/shard_map/ppermute | solution.py:270
  424.4 15.3 %collective-permute-start.15 = (bf16[2,512,512]{2,1,0:T(8,128)(2,1)}, bf16[2,512,512]{2,1,0:T(8,128)(2,1)S(1)}, u32[]{:S(2)}, u32[]{:S(2)}) collective-permute-start(bf16[2,512,512]{2,1,0:T(8,128)(2,1)} %get-tuple-element.47), channel_id=1, source_target_pairs={{0,1},{1,0},{2,3},{3,2},{4,5},{5,4},{6,7},{7,6},{8,9},{9,8},{10,11... | collective-permute-start | bytes 3145736 | tf_op jit(solution)/shard_map/ppermute | solution.py:329
  427.4 12.3 %copy-start.3 = (bf16[2,512,512]{2,1,0:T(8,128)(2,1)S(1)}, bf16[2,512,512]{2,1,0:T(8,128)(2,1)}, u32[]{:S(2)}) copy-start(bf16[2,512,512]{2,1,0:T(8,128)(2,1)} %get-tuple-element.44.rest_0_) | copy-start | bytes 3145732
  439.4 2.9 copy-start.6
  439.4 2.9 collective-permute-start.17
  440.0 14.8 %collective-permute-start.16 = (bf16[512,512]{1,0:T(8,128)(2,1)S(1)}, bf16[512,512]{1,0:T(8,128)(2,1)S(1)}, u32[]{:S(2)}, u32[]{:S(2)}) collective-permute-start(bf16[512,512]{1,0:T(8,128)(2,1)S(1)} %fusion.6), channel_id=1, source_target_pairs={{0,2},{1,3},{2,0},{3,1},{4,6},{5,7},{6,4},{7,5},{8,10},{9,11},{10,... | collective-permute-start | bytes 1572872 | tf_op jit(solution)/shard_map/ppermute | solution.py:270
  442.2 1.2 copy-start.1
  442.6 22.8 %collective-permute-start.18 = (bf16[512,512]{1,0:T(8,128)(2,1)S(1)}, bf16[512,512]{1,0:T(8,128)(2,1)S(1)}, u32[]{:S(2)}, u32[]{:S(2)}) collective-permute-start(bf16[512,512]{1,0:T(8,128)(2,1)S(1)} %fusion.7), channel_id=1, source_target_pairs={{0,2},{1,3},{2,0},{3,1},{4,6},{5,7},{6,4},{7,5},{8,10},{9,11},{10,... | collective-permute-start | bytes 1572872 | tf_op jit(solution)/shard_map/ppermute | solution.py:270
  465.6 1.3 copy-start.4

commit v4 on v3

--- a/solution.py
+++ b/solution.py
@@ -69,7 +69,7 @@
             grid=(down,),
             in_specs=[
                 root_spec(roots, 0, 1, lambda p, f: (p, q)),
-                pl.BlockSpec((width, width), lambda p, f: (p, q)),
+                pl.BlockSpec((width, width), lambda p, f: (p, 0)),
                 root_spec(roots, 1, 1, lambda p, f: (p, q)),
             ]
             + [pl.BlockSpec(memory_space=pl.ANY)] * len(later_than),
@@ -121,7 +121,7 @@
         ),
         input_output_aliases={} if new_weight is None else {5: 0},
         compiler_params=pltpu.CompilerParams(vmem_limit_bytes=60 << 20),
-        cost_estimate=cost(2 * down, width, 5),
+        cost_estimate=cost(4 * down, width, 5),
         name="precondition_home",
     )(kept_column, roots, grad, roots, weight, *extra)
 
@@ -288,23 +288,27 @@
     back = shift_route(row_count, -1)
 
     swapped = swap_tokens(tokens, row_count, row_place)
-    swapped, grad = together(swapped, grad)
-    came = lax.ppermute(grad, "row", forth)
+    columns = [grad[:, q * width:(q + 1) * width] for q in range(across)]
+    swapped, *columns = together(swapped, *columns)
+    came = [lax.ppermute(column, "row", forth) for column in columns]
     early = ring_direct(swapped, row_count, 0)
-    new_weight = precondition_home(kept[:, 0], roots, grad, weight, 0, None, ())
-    came, late_pair, new_weight, *early = together(came, swapped, new_weight, *early)
-
-    returned = []
+    lents = []
+    later_than = ()
+    for q in range(across - 1):
+        lent, mark = precondition_lent(taken[:, q], roots, q, came[q], (0, width), later_than)
+        lents.append(lent)
+        later_than = (mark,)
+    new_weight = precondition_home(kept[:, 0], roots, grad, weight, 0, None, later_than)
+    last, late_pair, new_weight, *rest = together(came[-1], swapped, new_weight, *lents, *early)
+    lents, early = rest[:across - 1], rest[across - 1:]
+
+    returned = [lax.ppermute(lent, "row", back) for lent in lents]
     up, down_piece = line_step(late_pair, late_pair, row_count, 1)
     late = [(up, down_piece)]
-    returned = []
-    later_than = ()
-    for q in range(across):
-        lent, mark = precondition_lent(taken[:, q], roots, q, came, (0, width), later_than)
-        returned.append(lax.ppermute(lent, "row", back))
-        later_than = (mark,)
-        if q > 0:
-            new_weight = precondition_home(kept[:, q], roots, grad, weight, q, new_weight, later_than)
+    lent, mark = precondition_lent(taken[:, across - 1], roots, across - 1, last, (0, width), ())
+    returned.append(lax.ppermute(lent, "row", back))
+    for q in range(1, across):
+        new_weight = precondition_home(kept[:, q], roots, grad, weight, q, new_weight, (mark,))
 
     for step in range(2, row_count // 2):
         if step == row_count // 2 - 1:

time: 469 us -> 464 us (0.989)
  waiting for transfers between devices: 258 us -> 229 us
  Pallas kernels: 104 us -> 115 us
  local copies, waits for them, and re-layouts: 5.1 us -> 10.8 us
    ppermute x3, waiting for transfers between devices: 157 us -> 60.8 us  [ring_direct(): lax.ppermute(pair, 'row', [(i, (i + 2 * step) % row_count) for i in sides])]
    ppermute x1 -> x3, waiting for transfers between devices: 0.01 us -> 82.1 us  [the longest x2 82.1 us: on_device(): came = [lax.ppermute(column, 'row', forth) for column in columns]]
    pallas_call x2, Pallas kernels: 22.5 us -> 29.8 us  [precondition_lent(): pl.pallas_call(kernel, out_shape=[jax.ShapeDtypeStruct((down * width, sto...]
    ppermute x2 -> x1, waiting for transfers between devices: 49.7 us -> 43.3 us  [on_device(): returned.append(lax.ppermute(lent, 'row', back))]
    slice x1 -> x2, local copies, waits for them, and re-layouts: 0.76 us -> 6.9 us  [the longest x1 6.11 us: on_device(): columns = [grad[:, q * width:(q + 1) * width] for q in range(across)]]
    ppermute x1, waiting for transfers between devices: 23.4 us -> 17.3 us  [swap_tokens(): other = lax.ppermute(tokens, 'row', pair_route(row_count))]
    ppermute x2 -> x1, starting transfers between devices: 61.1 us -> 62.1 us  [on_device(): returned.append(lax.ppermute(lent, 'row', back))]
  transfers between devices with their start and end apart: 19 -> 20, of which waited for: 8 -> 8; matrix products, arithmetic and copies ran while one was open for 2% -> 3% of each run, Pallas kernels for 22% -> 25%
where the time goes in v4:
time: 464 us; the launch traced here: 459 us
  waiting for transfers between devices  229 us (49%)
  Pallas kernels  115 us (25%)
  starting transfers between devices  94.9 us (20%)
  local copies, waits for them, and re-layouts  10.8 us (2%)
  other arithmetic  8.08 us (2%)
    ppermute x2, waiting for transfers between devices, on_device(): came = [lax.ppermute(column, 'row', forth) for column in columns]  82.1 us
    ppermute x1, starting transfers between devices, on_device(): returned.append(lax.ppermute(lent, 'row', back))  62.1 us
    ppermute x3, waiting for transfers between devices, ring_direct(): lax.ppermute(pair, 'row', [(i, (i + 2 * step) % row_count) for i in sides])  60.8 us
    ppermute x1, waiting for transfers between devices, on_device(): returned.append(lax.ppermute(lent, 'row', back))  43.3 us
    pallas_call x3, Pallas kernels, finish_columns(): pl.pallas_call(kernel, out_shape=(jax.ShapeDtypeStruct(new_weight.shape,...  43.2 us
    pallas_call x2, Pallas kernels, precondition_home(): pl.pallas_call(kernel, out_shape=jax.ShapeDtypeStruct(weight.shape, jnp.b...  31.2 us
    pallas_call x2, Pallas kernels, precondition_lent(): pl.pallas_call(kernel, out_shape=[jax.ShapeDtypeStruct((down * width, sto...  29.8 us
    ppermute x3, waiting for transfers between devices, far_sum(): lax.ppermute(piece, 'col', shift_route(col_count, 2 * step))  20.6 us
  transfers between devices with their start and end apart: 20, of which 8 were waited for; matrix products, arithmetic and copies ran while one was open for 3% of the time, Pallas kernels for 25%

profile of v4, /device:TPU:0, one launch (start us, length us, event | category | flops | bytes accessed | tf_op | source)
XLA Modules:
  0.0 458.6 jit_solution(14901345395511407945)
XLA Ops:
  0.6 3.0 collective-permute-start
  3.6 6.1 %fusion.8 = (bf16[2048,1024]{1,0:T(8,128)(2,1)}, bf16[2048,1024]{1,0:T(8,128)(2,1)}) fusion(bf16[2048,2048]{1,0:T(8,128)(2,1)} %grad_ref.3), kind=kLoop, calls=%fused_computation.28 | loop fusion | bytes 16777216 | tf_op jit(solution)/shard_map/slice | solution.py:291
  9.7 17.3 %collective-permute-done = bf16[256,2048]{1,0:T(8,128)(2,1)S(1)} collective-permute-done((bf16[256,2048]{1,0:T(8,128)(2,1)}, bf16[256,2048]{1,0:T(8,128)(2,1)S(1)}, u32[]{:S(2)}, u32[]{:S(2)}) %collective-permute-start) | collective-permute-done | bytes 1048608 | tf_op jit(solution)/shard_map/ppermute | solution.py:202
  27.0 0.3 broadcast_select_fusion.1
  27.3 0.0 copy-start.8
  27.3 0.1 pad_maximum_fusion.refs_0_
  27.4 0.0 copy-start.2
  27.4 1.8 collective-permute-start.2
  29.2 1.5 collective-permute-start.1
  30.8 0.1 compare_convert_fusion
  30.9 0.8 slice_reduce_fusion
  31.7 4.0 collective-permute-start.5
  35.7 2.8 collective-permute-start.4
  38.5 3.5 collective-permute-start.3
  42.0 82.1 %collective-permute-done.2.grad_ref = bf16[2048,1024]{1,0:T(8,128)(2,1)} collective-permute-done((bf16[2048,1024]{1,0:T(8,128)(2,1)}, bf16[2048,1024]{1,0:T(8,128)(2,1)}, u32[]{:S(2)}, u32[]{:S(2)}) %collective-permute-start.2) | collective-permute-done | bytes 4194336 | tf_op jit(solution)/shard_map/ppermute | solution.py:293
  124.1 14.9 %precondition_lent.2 = (bf16[2048,1024]{1,0:T(8,128)(2,1)}, f32[8,128]{1,0:T(8,128)}) custom-call(s32[2]{0:T(128)} %get-tuple-element.55.flag_ref, bf16[2,2,2,2,1024,1024]{5,4,3,2,1,0:T(8,128)(2,1)} %right_ref.7, bf16[2048,1024]{1,0:T(8,128)(2,1)} %collective-permute-done.2.grad_ref, bf16[2,2,2,2,1024,1024]{5,4,3,2,1,0:T(8,128)(2,1)} %right_ref.7), custom_call_target="tpu_custom_call" | custom-call | flops 8589934592 | bytes 16777216 | tf_op jit(solution)/shard_map/precondition_lent/pallas_call | solution.py:63
  139.0 15.6 %precondition_home.2.rest_0_ = bf16[2048,2048]{1,0:T(8,128)(2,1)} custom-call(s32[2]{0:T(128)} %get-tuple-element.64.flag_ref, bf16[2,2,2,2,1024,1024]{5,4,3,2,1,0:T(8,128)(2,1)} %right_ref.7, bf16[2048,2048]{1,0:T(8,128)(2,1)} %grad_ref.3, bf16[2,2,2,2,1024,1024]{5,4,3,2,1,0:T(8,128)(2,1)} %right_ref.7, bf16[2048,2048]{1,0:T(8,128)(2,1)} %weight_ref.3, ...), custom_call_target="tpu_custom_call" | custom-call | flops 34359738368 | bytes 83886080 | tf_op jit(solution)/shard_map/precondition_home/pallas_call | solution.py:107
  154.6 0.0 collective-permute-done.5.refs_3_
  154.6 60.8 %collective-permute-done.4.refs_2_ = bf16[512,2048]{1,0:T(8,128)(2,1)} collective-permute-done((bf16[512,2048]{1,0:T(8,128)(2,1)S(1)}, bf16[512,2048]{1,0:T(8,128)(2,1)}, u32[]{:S(2)}, u32[]{:S(2)}) %collective-permute-start.4) | collective-permute-done | bytes 2097184 | tf_op jit(solution)/shard_map/ppermute | solution.py:210
  215.4 0.0 collective-permute-done.1.grad_ref
  215.4 2.0 collective-permute-start.8
  217.4 2.0 collective-permute-start.6
  219.4 0.0 collective-permute-start.10
  219.4 14.9 %precondition_lent.3 = (bf16[2048,1024]{1,0:T(8,128)(2,1)}, f32[8,128]{1,0:T(8,128)}) custom-call(s32[2]{0:T(128)} %get-tuple-element.54.flag_ref, bf16[2,2,2,2,1024,1024]{5,4,3,2,1,0:T(8,128)(2,1)} %right_ref.7, bf16[2048,1024]{1,0:T(8,128)(2,1)} %collective-permute-done.1.grad_ref, bf16[2,2,2,2,1024,1024]{5,4,3,2,1,0:T(8,128)(2,1)} %right_ref.7), custom_call_target="tpu_custom_call" | custom-call | flops 8589934592 | bytes 16777216 | tf_op jit(solution)/shard_map/precondition_lent/pallas_call | solution.py:63
  234.3 2.0 collective-permute-start.9
  236.3 0.0 collective-permute-done.6.refs_4_
  236.3 0.8 collective-permute-start.7
  237.1 15.6 %precondition_home.3.weight_ref = bf16[2048,2048]{1,0:T(8,128)(2,1)} custom-call(s32[2]{0:T(128)} %get-tuple-element.65.flag_ref, bf16[2,2,2,2,1024,1024]{5,4,3,2,1,0:T(8,128)(2,1)} %right_ref.7, bf16[2048,2048]{1,0:T(8,128)(2,1)} %grad_ref.3, bf16[2,2,2,2,1024,1024]{5,4,3,2,1,0:T(8,128)(2,1)} %right_ref.7, ...), custom_call_target="tpu_custom_call", output_to_operand_aliasing={{}: (5, {})} | custom-call | flops 34359738368 | bytes 83886080 | tf_op jit(solution)/shard_map/precondition_home/pallas_call | solution.py:107
  252.7 0.0 collective-permute-done.9.refs_8_
  252.7 0.0 collective-permute-done.7.refs_5_
  252.8 2.0 collective-permute-start.11
  254.8 2.0 collective-permute-start.12
  256.8 62.1 %collective-permute-start.13 = (bf16[2048,1024]{1,0:T(8,128)(2,1)}, bf16[2048,1024]{1,0:T(8,128)(2,1)}, u32[]{:S(2)}, u32[]{:S(2)}) collective-permute-start(bf16[2048,1024]{1,0:T(8,128)(2,1)} %get-tuple-element.45), channel_id=1, source_target_pairs={{0,28},{4,0},{8,4},{12,8},{16,12},{20,16},{24,20},{28,24},{1,29},{... | collective-permute-start | bytes 12582920 | tf_op jit(solution)/shard_map/ppermute | solution.py:309
  318.9 0.1 reshape.10
  319.0 0.6 pad_add_fusion.1.place_ref
  319.6 0.6 pad_add_fusion.flag_ref
  320.2 0.0 collective-permute-done.11.refs_6_
  320.2 0.0 collective-permute-done.12.refs_9_
  320.2 10.7 %put_pairs.1.token_ref = bf16[2048,2048]{1,0:T(8,128)(2,1)} custom-call(s32[2]{0:T(128)} %pad_add_fusion.1.place_ref, bf16[512,2048]{1,0:T(8,128)(2,1)} %copy-done.2, bf16[512,2048]{1,0:T(8,128)(2,1)} %collective-permute-done.3.refs_1_, bf16[512,2048]{1,0:T(8,128)(2,1)} %collective-permute-done.4.refs_2_, bf16[512,2048]{1,0:T(8,128)(2,1)} %collective-permute-done.5.refs_3_, ...), custom_call_target="tpu_custom_call" | custom-call | flops 1000 | bytes 1000 | tf_op jit(solution)/shard_map/put_pairs/pallas_call | solution.py:247
  330.9 19.8 %finish_columns.3 = (bf16[2048,2048]{1,0:T(8,128)(2,1)}, bf16[2,512,1024]{2,1,0:T(8,128)(2,1)}, bf16[2,512,1024]{2,1,0:T(8,128)(2,1)}) custom-call(s32[5]{0:T(128)} %pad_add_fusion.flag_ref, bf16[2048,2048]{1,0:T(8,128)(2,1)} %precondition_home.3.weight_ref, bf16[2048,1024]{1,0:T(8,128)(2,1)} %collective-permute-done.10.piece_ref, ...), custom_call_target="tpu_custom_call", output_to_operand_aliasing={{0}: (1, {})} | custom-call | flops 1000 | bytes 1000 | tf_op jit(solution)/shard_map/finish_columns/pallas_call | solution.py:176
  350.7 4.4 collective-permute-done.14
  355.1 2.5 convert_add_fusion
  357.6 2.0 copy-done
  359.6 0.2 fusion.1
  359.7 1.6 collective-permute-start.15
  361.3 43.3 %collective-permute-done.13.piece_ref = bf16[2048,1024]{1,0:T(8,128)(2,1)} collective-permute-done((bf16[2048,1024]{1,0:T(8,128)(2,1)}, bf16[2048,1024]{1,0:T(8,128)(2,1)}, u32[]{:S(2)}, u32[]{:S(2)}) %collective-permute-start.13) | collective-permute-done | bytes 4194336 | tf_op jit(solution)/shard_map/ppermute | solution.py:309
  404.7 11.6 %finish_columns.4 = (bf16[2048,2048]{1,0:T(8,128)(2,1)}, bf16[2,512,512]{2,1,0:T(8,128)(2,1)}, bf16[2,512,512]{2,1,0:T(8,128)(2,1)}) custom-call(s32[5]{0:T(128)} %pad_add_fusion.flag_ref, bf16[2048,2048]{1,0:T(8,128)(2,1)} %get-tuple-element.44.weight_ref, bf16[2048,1024]{1,0:T(8,128)(2,1)} %collective-permute-done.13.piece_ref, ...), custom_call_target="tpu_custom_call", output_to_operand_aliasing={{0}: (1, {})} | custom-call | flops 1000 | bytes 1000 | tf_op jit(solution)/shard_map/finish_columns/pallas_call | solution.py:176
  416.3 3.0 fusion.rest_1_
  419.3 11.8 %finish_columns.5 = (bf16[2048,2048]{1,0:T(8,128)(2,1)}, bf16[2,512,512]{2,1,0:T(8,128)(2,1)}, bf16[2,512,512]{2,1,0:T(8,128)(2,1)}) custom-call(s32[5]{0:T(128)} %pad_add_fusion.flag_ref, bf16[2048,2048]{1,0:T(8,128)(2,1)} %get-tuple-element.47.weight_ref, bf16[2048,1024]{1,0:T(8,128)(2,1)} %collective-permute-done.13.piece_ref, ...), custom_call_target="tpu_custom_call", output_to_operand_aliasing={{0}: (1, {})} | custom-call | flops 1000 | bytes 1000 | tf_op jit(solution)/shard_map/finish_columns/pallas_call | solution.py:176
  431.0 0.5 collective-permute-start.18
  431.5 0.3 convert_add_fusion.2
  431.8 0.1 fusion.6
  431.9 1.6 collective-permute-start.17
  433.5 0.5 collective-permute-done.18
  434.0 0.3 convert_add_fusion.1
  434.3 0.1 fusion.7
  434.4 1.6 collective-permute-start.19
  436.0 0.2 dynamic_update_slice.9
  436.3 10.5 %collective-permute-done.17 = bf16[512,512]{1,0:T(8,128)(2,1)S(1)} collective-permute-done((bf16[512,512]{1,0:T(8,128)(2,1)S(1)}, bf16[512,512]{1,0:T(8,128)(2,1)S(1)}, u32[]{:S(2)}, u32[]{:S(2)}) %collective-permute-start.17) | collective-permute-done | bytes 524320 | tf_op jit(solution)/shard_map/ppermute | solution.py:270
  446.8 0.2 fusion.4
  446.9 10.1 %collective-permute-done.19 = bf16[512,512]{1,0:T(8,128)(2,1)S(1)} collective-permute-done((bf16[512,512]{1,0:T(8,128)(2,1)S(1)}, bf16[512,512]{1,0:T(8,128)(2,1)S(1)}, u32[]{:S(2)}, u32[]{:S(2)}) %collective-permute-start.19) | collective-permute-done | bytes 524320 | tf_op jit(solution)/shard_map/ppermute | solution.py:270
  457.1 0.2 fusion.5
  457.3 0.0 copy-start.4
  457.3 1.3 copy-done.4
  (20 shorter events, 0.0 us)
Async XLA Ops:
  0.6 26.4 %collective-permute-start = (bf16[256,2048]{1,0:T(8,128)(2,1)}, bf16[256,2048]{1,0:T(8,128)(2,1)S(1)}, u32[]{:S(2)}, u32[]{:S(2)}) collective-permute-start(bf16[256,2048]{1,0:T(8,128)(2,1)} %param.5), channel_id=1, source_target_pairs={{0,4},{4,0},{8,12},{12,8},{16,20},{20,16},{24,28},{28,24},{1,5},{5... | collective-permute-start | bytes 3145736 | tf_op jit(solution)/shard_map/ppermute | solution.py:202
  3.6 23.4 %copy-start.6 = (bf16[256,2048]{1,0:T(8,128)(2,1)S(1)}, bf16[256,2048]{1,0:T(8,128)(2,1)}, u32[]{:S(2)}) copy-start(bf16[256,2048]{1,0:T(8,128)(2,1)} %param.5) | copy-start | bytes 3145732
  27.3 3.5 copy-start.8
  27.4 190.0 %copy-start.2 = (bf16[512,2048]{1,0:T(8,128)(2,1)}, bf16[512,2048]{1,0:T(8,128)(2,1)S(1)}, u32[]{:S(2)}) copy-start(bf16[512,2048]{1,0:T(8,128)(2,1)S(1)} %pad_maximum_fusion.refs_0_) | copy-start | bytes 6291460
  27.4 96.6 %collective-permute-start.2 = (bf16[2048,1024]{1,0:T(8,128)(2,1)}, bf16[2048,1024]{1,0:T(8,128)(2,1)}, u32[]{:S(2)}, u32[]{:S(2)}) collective-permute-start(bf16[2048,1024]{1,0:T(8,128)(2,1)} %get-tuple-element.30), channel_id=1, source_target_pairs={{0,4},{4,8},{8,12},{12,16},{16,20},{20,24},{24,28},{28,0},{1,5},{5... | collective-permute-start | bytes 12582920 | tf_op jit(solution)/shard_map/ppermute | solution.py:293
  29.2 186.2 %collective-permute-start.1 = (bf16[2048,1024]{1,0:T(8,128)(2,1)}, bf16[2048,1024]{1,0:T(8,128)(2,1)}, u32[]{:S(2)}, u32[]{:S(2)}) collective-permute-start(bf16[2048,1024]{1,0:T(8,128)(2,1)} %get-tuple-element.28), channel_id=1, source_target_pairs={{0,4},{4,8},{8,12},{12,16},{16,20},{20,24},{24,28},{28,0},{1,5},{5... | collective-permute-start | bytes 12582920 | tf_op jit(solution)/shard_map/ppermute | solution.py:293
  31.7 123.0 %collective-permute-start.5 = (bf16[512,2048]{1,0:T(8,128)(2,1)S(1)}, bf16[512,2048]{1,0:T(8,128)(2,1)}, u32[]{:S(2)}, u32[]{:S(2)}) collective-permute-start(bf16[512,2048]{1,0:T(8,128)(2,1)S(1)} %pad_maximum_fusion.refs_0_), channel_id=1, source_target_pairs={{0,24},{8,0},{16,8},{24,16},{1,25},{9,1},{17,9},{25,17},{2,26},{10... | collective-permute-start | bytes 6291464 | tf_op jit(solution)/shard_map/ppermute | solution.py:210
  35.7 179.7 %collective-permute-start.4 = (bf16[512,2048]{1,0:T(8,128)(2,1)S(1)}, bf16[512,2048]{1,0:T(8,128)(2,1)}, u32[]{:S(2)}, u32[]{:S(2)}) collective-permute-start(bf16[512,2048]{1,0:T(8,128)(2,1)S(1)} %pad_maximum_fusion.refs_0_), channel_id=1, source_target_pairs={{0,16},{8,24},{16,0},{24,8},{1,17},{9,25},{17,1},{25,9},{2,18},{10... | collective-permute-start | bytes 6291464 | tf_op jit(solution)/shard_map/ppermute | solution.py:210
  38.5 176.9 %collective-permute-start.3 = (bf16[512,2048]{1,0:T(8,128)(2,1)S(1)}, bf16[512,2048]{1,0:T(8,128)(2,1)}, u32[]{:S(2)}, u32[]{:S(2)}) collective-permute-start(bf16[512,2048]{1,0:T(8,128)(2,1)S(1)} %pad_maximum_fusion.refs_0_), channel_id=1, source_target_pairs={{0,8},{8,16},{16,24},{24,0},{1,9},{9,17},{17,25},{25,1},{2,10},{10... | collective-permute-start | bytes 6291464 | tf_op jit(solution)/shard_map/ppermute | solution.py:210
  215.4 18.9 %collective-permute-start.8 = (bf16[512,2048]{1,0:T(8,128)(2,1)S(1)}, bf16[512,2048]{1,0:T(8,128)(2,1)}, u32[]{:S(2)}, u32[]{:S(2)}) collective-permute-start(bf16[512,2048]{1,0:T(8,128)(2,1)S(1)} %pad_maximum_fusion.refs_0_), channel_id=1, source_target_pairs={{12,4},{20,12},{28,20},{13,5},{21,13},{29,21},{14,6},{22,14},{30,2... | collective-permute-start | bytes 6291464 | tf_op jit(solution)/shard_map/ppermute | solution.py:217
  217.4 18.9 %collective-permute-start.6 = (bf16[512,2048]{1,0:T(8,128)(2,1)S(1)}, bf16[512,2048]{1,0:T(8,128)(2,1)}, u32[]{:S(2)}, u32[]{:S(2)}) collective-permute-start(bf16[512,2048]{1,0:T(8,128)(2,1)S(1)} %pad_maximum_fusion.refs_0_), channel_id=1, source_target_pairs={{4,12},{12,20},{20,28},{5,13},{13,21},{21,29},{6,14},{14,22},{22,3... | collective-permute-start | bytes 6291464 | tf_op jit(solution)/shard_map/ppermute | solution.py:216
  219.4 111.5 %collective-permute-start.10 = (bf16[2048,1024]{1,0:T(8,128)(2,1)}, bf16[2048,1024]{1,0:T(8,128)(2,1)}, u32[]{:S(2)}, u32[]{:S(2)}) collective-permute-start(bf16[2048,1024]{1,0:T(8,128)(2,1)} %get-tuple-element.38), channel_id=1, source_target_pairs={{0,28},{4,0},{8,4},{12,8},{16,12},{20,16},{24,20},{28,24},{1,29},{... | collective-permute-start | bytes 12582920 | tf_op jit(solution)/shard_map/ppermute | solution.py:305
  234.3 18.4 %collective-permute-start.9 = (bf16[512,2048]{1,0:T(8,128)(2,1)}, bf16[512,2048]{1,0:T(8,128)(2,1)}, u32[]{:S(2)}, u32[]{:S(2)}) collective-permute-start(bf16[512,2048]{1,0:T(8,128)(2,1)} %collective-permute-done.8.refs_7_), channel_id=1, source_target_pairs={{12,4},{20,12},{28,20},{13,5},{21,13},{29,21},{14,6},{22,14},{30,2... | collective-permute-start | bytes 6291464 | tf_op jit(solution)/shard_map/ppermute | solution.py:217
  236.3 16.4 %collective-permute-start.7 = (bf16[512,2048]{1,0:T(8,128)(2,1)}, bf16[512,2048]{1,0:T(8,128)(2,1)S(1)}, u32[]{:S(2)}, u32[]{:S(2)}) collective-permute-start(bf16[512,2048]{1,0:T(8,128)(2,1)} %collective-permute-done.6.refs_4_), channel_id=1, source_target_pairs={{4,12},{12,20},{20,28},{5,13},{13,21},{21,29},{6,14},{14,22},{22,3... | collective-permute-start | bytes 6291464 | tf_op jit(solution)/shard_map/ppermute | solution.py:216
  252.7 67.4 %copy-start.5 = (bf16[512,2048]{1,0:T(8,128)(2,1)}, bf16[512,2048]{1,0:T(8,128)(2,1)S(1)}, u32[]{:S(2)}) copy-start(bf16[512,2048]{1,0:T(8,128)(2,1)S(1)} %collective-permute-done.7.refs_5_) | copy-start | bytes 6291460
  252.8 67.4 %collective-permute-start.11 = (bf16[512,2048]{1,0:T(8,128)(2,1)S(1)}, bf16[512,2048]{1,0:T(8,128)(2,1)}, u32[]{:S(2)}, u32[]{:S(2)}) collective-permute-start(bf16[512,2048]{1,0:T(8,128)(2,1)S(1)} %collective-permute-done.7.refs_5_), channel_id=1, source_target_pairs={{4,12},{12,20},{20,28},{5,13},{13,21},{21,29},{6,14},{14,22},{22,3... | collective-permute-start | bytes 6291464 | tf_op jit(solution)/shard_map/ppermute | solution.py:216
  254.8 65.4 %collective-permute-start.12 = (bf16[512,2048]{1,0:T(8,128)(2,1)}, bf16[512,2048]{1,0:T(8,128)(2,1)}, u32[]{:S(2)}, u32[]{:S(2)}) collective-permute-start(bf16[512,2048]{1,0:T(8,128)(2,1)} %collective-permute-done.9.refs_8_), channel_id=1, source_target_pairs={{12,4},{20,12},{28,20},{13,5},{21,13},{29,21},{14,6},{22,14},{30,2... | collective-permute-start | bytes 6291464 | tf_op jit(solution)/shard_map/ppermute | solution.py:217
  256.8 147.8 %collective-permute-start.13 = (bf16[2048,1024]{1,0:T(8,128)(2,1)}, bf16[2048,1024]{1,0:T(8,128)(2,1)}, u32[]{:S(2)}, u32[]{:S(2)}) collective-permute-start(bf16[2048,1024]{1,0:T(8,128)(2,1)} %get-tuple-element.45), channel_id=1, source_target_pairs={{0,28},{4,0},{8,4},{12,8},{16,12},{20,16},{24,20},{28,24},{1,29},{... | collective-permute-start | bytes 12582920 | tf_op jit(solution)/shard_map/ppermute | solution.py:309
  350.7 4.4 collective-permute-start.14
  357.6 2.0 copy-start
  359.7 56.6 %collective-permute-start.15 = (bf16[512,1024]{1,0:T(8,128)(2,1)S(1)}, bf16[512,1024]{1,0:T(8,128)(2,1)S(1)}, u32[]{:S(2)}, u32[]{:S(2)}) collective-permute-start(bf16[512,1024]{1,0:T(8,128)(2,1)S(1)} %fusion.1), channel_id=1, source_target_pairs={{0,2},{1,3},{2,0},{3,1},{4,6},{5,7},{6,4},{7,5},{8,10},{9,11},{10,... | collective-permute-start | bytes 3145736 | tf_op jit(solution)/shard_map/ppermute | solution.py:270
  416.3 15.3 %collective-permute-start.16 = (bf16[2,512,512]{2,1,0:T(8,128)(2,1)}, bf16[2,512,512]{2,1,0:T(8,128)(2,1)S(1)}, u32[]{:S(2)}, u32[]{:S(2)}) collective-permute-start(bf16[2,512,512]{2,1,0:T(8,128)(2,1)} %get-tuple-element.51), channel_id=1, source_target_pairs={{0,1},{1,0},{2,3},{3,2},{4,5},{5,4},{6,7},{7,6},{8,9},{9,8},{10,11... | collective-permute-start | bytes 3145736 | tf_op jit(solution)/shard_map/ppermute | solution.py:333
  419.3 12.3 %copy-start.3 = (bf16[2,512,512]{2,1,0:T(8,128)(2,1)S(1)}, bf16[2,512,512]{2,1,0:T(8,128)(2,1)}, u32[]{:S(2)}) copy-start(bf16[2,512,512]{2,1,0:T(8,128)(2,1)} %get-tuple-element.48.rest_0_) | copy-start | bytes 3145732
  431.0 3.0 copy-start.7
  431.0 3.0 collective-permute-start.18
  431.9 14.8 %collective-permute-start.17 = (bf16[512,512]{1,0:T(8,128)(2,1)S(1)}, bf16[512,512]{1,0:T(8,128)(2,1)S(1)}, u32[]{:S(2)}, u32[]{:S(2)}) collective-permute-start(bf16[512,512]{1,0:T(8,128)(2,1)S(1)} %fusion.6), channel_id=1, source_target_pairs={{0,2},{1,3},{2,0},{3,1},{4,6},{5,7},{6,4},{7,5},{8,10},{9,11},{10,... | collective-permute-start | bytes 1572872 | tf_op jit(solution)/shard_map/ppermute | solution.py:270
  434.0 2.0 copy-start.1
  434.4 22.6 %collective-permute-start.19 = (bf16[512,512]{1,0:T(8,128)(2,1)S(1)}, bf16[512,512]{1,0:T(8,128)(2,1)S(1)}, u32[]{:S(2)}, u32[]{:S(2)}) collective-permute-start(bf16[512,512]{1,0:T(8,128)(2,1)S(1)} %fusion.7), channel_id=1, source_target_pairs={{0,2},{1,3},{2,0},{3,1},{4,6},{5,7},{6,4},{7,5},{8,10},{9,11},{10,... | collective-permute-start | bytes 1572872 | tf_op jit(solution)/shard_map/ppermute | solution.py:270
  457.3 1.3 copy-start.4

commit v5 on v4

--- a/solution.py
+++ b/solution.py
@@ -260,15 +260,21 @@
 
 
 def far_sum(mine, came, col_count, col_place):
-    halves = mine.astype(jnp.float32) + came.astype(jnp.float32)
     groups = col_count // 2
     place = col_place // 2
-    total = lax.dynamic_index_in_dim(halves, place, 0, keepdims=False)
-    sent = halves.astype(jnp.bfloat16)
+
+    def half(index):
+        both = [lax.dynamic_index_in_dim(x, index, 0, keepdims=False).astype(jnp.float32) for x in (mine, came)]
+        return both[0] + both[1]
+
+    arrived = []
     for step in range(1, groups):
-        piece = lax.dynamic_index_in_dim(sent, jnp.mod(place + step, groups), 0, keepdims=False)
-        total = total + lax.ppermute(piece, "col", shift_route(col_count, 2 * step)).astype(jnp.float32)
-    return total.astype(jnp.bfloat16)
+        piece = half(jnp.mod(place + step, groups)).astype(jnp.bfloat16)
+        arrived.append(lax.ppermute(piece, "col", shift_route(col_count, 2 * step)))
+    total = half(place)
+    for piece in arrived:
+        total = total + piece.astype(jnp.float32)
+    return total.astype(jnp.bfloat16), arrived
 
 
 def on_device(tokens, weight, grad, roots, owner):
@@ -331,11 +337,11 @@
             flags, down, across, q, col_count, new_weight, returned[q], all_tokens, start, size, later_than
         )
         other = lax.ppermute(others, "col", pair_route(col_count))
-        total = far_sum(mine, other, col_count, col_place)
+        total, arrived = far_sum(mine, other, col_count, col_place)
         output = lax.dynamic_update_slice(output, total, (0, q * width + start))
         later_than = (mine,)
         if q < across - 1:
-            ahead = ahead + (total,)
+            ahead = ahead + tuple(arrived)
     return new_weight, output
 
 

time: 464 us -> 462 us (level)
  Pallas kernels: 115 us -> 94.3 us
  starting transfers between devices: 94.9 us -> 108 us
  waiting for transfers between devices: 229 us -> 236 us
    pallas_call x2, Pallas kernels: 29.8 us -> 15.2 us  [precondition_lent(): pl.pallas_call(kernel, out_shape=[jax.ShapeDtypeStruct((down * width, sto...]
    ppermute x1, starting transfers between devices: 62.1 us -> 76.3 us  [on_device(): returned.append(lax.ppermute(lent, 'row', back))]
    ppermute x3, waiting for transfers between devices: 60.8 us -> 68.2 us  [ring_direct(): lax.ppermute(pair, 'row', [(i, (i + 2 * step) % row_count) for i in sides])]
    pallas_call x2, Pallas kernels: 31.2 us -> 24.4 us  [precondition_home(): pl.pallas_call(kernel, out_shape=jax.ShapeDtypeStruct(weight.shape, jnp.b...]
  transfers between devices with their start and end apart: 20 -> 20, of which waited for: 8 -> 8; matrix products, arithmetic and copies ran while one was open for 3% -> 4% of each run, Pallas kernels for 25% -> 21%
where the time goes in v5:
time: 462 us; the launch traced here: 460 us
  waiting for transfers between devices  236 us (51%)
  starting transfers between devices  108 us (23%)
  Pallas kernels  94.3 us (20%)
  other arithmetic  10.7 us (2%)
  local copies, waits for them, and re-layouts  9.78 us (2%)
    ppermute x2, waiting for transfers between devices, on_device(): came = [lax.ppermute(column, 'row', forth) for column in columns]  82.1 us
    ppermute x1, starting transfers between devices, on_device(): returned.append(lax.ppermute(lent, 'row', back))  76.3 us
    ppermute x3, waiting for transfers between devices, ring_direct(): lax.ppermute(pair, 'row', [(i, (i + 2 * step) % row_count) for i in sides])  68.2 us
    ppermute x1, waiting for transfers between devices, on_device(): returned.append(lax.ppermute(lent, 'row', back))  45.1 us
    pallas_call x3, Pallas kernels, finish_columns(): pl.pallas_call(kernel, out_shape=(jax.ShapeDtypeStruct(new_weight.shape,...  44.1 us
    pallas_call x2, Pallas kernels, precondition_home(): pl.pallas_call(kernel, out_shape=jax.ShapeDtypeStruct(weight.shape, jnp.b...  24.4 us
    ppermute x3, waiting for transfers between devices, far_sum(): arrived.append(lax.ppermute(piece, 'col', shift_route(col_count, 2 * step)))  18.1 us
    ppermute x1, waiting for transfers between devices, swap_tokens(): other = lax.ppermute(tokens, 'row', pair_route(row_count))  17.3 us
  transfers between devices with their start and end apart: 20, of which 8 were waited for; matrix products, arithmetic and copies ran while one was open for 4% of the time, Pallas kernels for 21%

profile of v5, /device:TPU:0, one launch (start us, length us, event | category | flops | bytes accessed | tf_op | source)
XLA Modules:
  0.0 459.5 jit_solution(7865303193104467827)
XLA Ops:
  0.6 3.0 collective-permute-start
  3.6 6.1 %fusion.8 = (bf16[2048,1024]{1,0:T(8,128)(2,1)}, bf16[2048,1024]{1,0:T(8,128)(2,1)}) fusion(bf16[2048,2048]{1,0:T(8,128)(2,1)} %grad_ref.3), kind=kLoop, calls=%fused_computation.25 | loop fusion | bytes 16777216 | tf_op jit(solution)/shard_map/slice | solution.py:297
  9.7 17.3 %collective-permute-done = bf16[256,2048]{1,0:T(8,128)(2,1)S(1)} collective-permute-done((bf16[256,2048]{1,0:T(8,128)(2,1)}, bf16[256,2048]{1,0:T(8,128)(2,1)S(1)}, u32[]{:S(2)}, u32[]{:S(2)}) %collective-permute-start) | collective-permute-done | bytes 1048608 | tf_op jit(solution)/shard_map/ppermute | solution.py:202
  27.0 0.3 broadcast_select_fusion.1
  27.3 0.0 copy-start.13
  27.3 0.1 pad_maximum_fusion.refs_0_
  27.4 0.0 copy-start.1
  27.4 1.8 collective-permute-start.2
  29.2 1.5 collective-permute-start.1
  30.8 0.1 compare_convert_fusion
  30.9 0.8 slice_reduce_fusion
  31.7 4.0 collective-permute-start.5
  35.7 2.8 collective-permute-start.4
  38.5 3.5 collective-permute-start.3
  42.0 82.1 %collective-permute-done.2.grad_ref = bf16[2048,1024]{1,0:T(8,128)(2,1)} collective-permute-done((bf16[2048,1024]{1,0:T(8,128)(2,1)}, bf16[2048,1024]{1,0:T(8,128)(2,1)}, u32[]{:S(2)}, u32[]{:S(2)}) %collective-permute-start.2) | collective-permute-done | bytes 4194336 | tf_op jit(solution)/shard_map/ppermute | solution.py:299
  124.1 7.6 %precondition_lent.2 = (bf16[2048,1024]{1,0:T(8,128)(2,1)}, f32[8,128]{1,0:T(8,128)}) custom-call(s32[2]{0:T(128)} %get-tuple-element.55.flag_ref, bf16[2,2,2,2,1024,1024]{5,4,3,2,1,0:T(8,128)(2,1)} %right_ref.7, bf16[2048,1024]{1,0:T(8,128)(2,1)} %collective-permute-done.2.grad_ref, bf16[2,2,2,2,1024,1024]{5,4,3,2,1,0:T(8,128)(2,1)} %right_ref.7), custom_call_target="tpu_custom_call" | custom-call | flops 8589934592 | bytes 16777216 | tf_op jit(solution)/shard_map/precondition_lent/pallas_call | solution.py:63
  131.7 15.6 %precondition_home.2.rest_0_ = bf16[2048,2048]{1,0:T(8,128)(2,1)} custom-call(s32[2]{0:T(128)} %get-tuple-element.64.flag_ref, bf16[2,2,2,2,1024,1024]{5,4,3,2,1,0:T(8,128)(2,1)} %right_ref.7, bf16[2048,2048]{1,0:T(8,128)(2,1)} %grad_ref.3, bf16[2,2,2,2,1024,1024]{5,4,3,2,1,0:T(8,128)(2,1)} %right_ref.7, bf16[2048,2048]{1,0:T(8,128)(2,1)} %weight_ref.3, ...), custom_call_target="tpu_custom_call" | custom-call | flops 34359738368 | bytes 83886080 | tf_op jit(solution)/shard_map/precondition_home/pallas_call | solution.py:107
  147.3 0.0 collective-permute-done.5.refs_3_
  147.3 68.2 %collective-permute-done.4.refs_2_ = bf16[512,2048]{1,0:T(8,128)(2,1)} collective-permute-done((bf16[512,2048]{1,0:T(8,128)(2,1)S(1)}, bf16[512,2048]{1,0:T(8,128)(2,1)}, u32[]{:S(2)}, u32[]{:S(2)}) %collective-permute-start.4) | collective-permute-done | bytes 2097184 | tf_op jit(solution)/shard_map/ppermute | solution.py:210
  215.4 0.0 collective-permute-done.3.refs_1_
  215.4 0.0 collective-permute-done.1.grad_ref
  215.4 2.0 collective-permute-start.8
  217.4 2.0 collective-permute-start.6
  219.4 0.0 collective-permute-start.10
  219.4 7.6 %precondition_lent.3 = (bf16[2048,1024]{1,0:T(8,128)(2,1)}, f32[8,128]{1,0:T(8,128)}) custom-call(s32[2]{0:T(128)} %get-tuple-element.54.flag_ref, bf16[2,2,2,2,1024,1024]{5,4,3,2,1,0:T(8,128)(2,1)} %right_ref.7, bf16[2048,1024]{1,0:T(8,128)(2,1)} %collective-permute-done.1.grad_ref, bf16[2,2,2,2,1024,1024]{5,4,3,2,1,0:T(8,128)(2,1)} %right_ref.7), custom_call_target="tpu_custom_call" | custom-call | flops 8589934592 | bytes 16777216 | tf_op jit(solution)/shard_map/precondition_lent/pallas_call | solution.py:63
  226.9 0.0 collective-permute-done.8.refs_7_
  226.9 2.0 collective-permute-start.9
  229.0 0.0 collective-permute-done.6.refs_4_
  229.0 0.8 collective-permute-start.7
  229.8 8.8 %precondition_home.3.weight_ref = bf16[2048,2048]{1,0:T(8,128)(2,1)} custom-call(s32[2]{0:T(128)} %get-tuple-element.65.flag_ref, bf16[2,2,2,2,1024,1024]{5,4,3,2,1,0:T(8,128)(2,1)} %right_ref.7, bf16[2048,2048]{1,0:T(8,128)(2,1)} %grad_ref.3, bf16[2,2,2,2,1024,1024]{5,4,3,2,1,0:T(8,128)(2,1)} %right_ref.7, ...), custom_call_target="tpu_custom_call", output_to_operand_aliasing={{}: (5, {})} | custom-call | flops 34359738368 | bytes 83886080 | tf_op jit(solution)/shard_map/precondition_home/pallas_call | solution.py:107
  238.5 0.0 collective-permute-done.9.refs_8_
  238.5 0.0 collective-permute-done.7.refs_5_
  238.5 2.0 collective-permute-start.11
  240.6 2.0 collective-permute-start.12
  242.6 76.3 %collective-permute-start.13 = (bf16[2048,1024]{1,0:T(8,128)(2,1)}, bf16[2048,1024]{1,0:T(8,128)(2,1)}, u32[]{:S(2)}, u32[]{:S(2)}) collective-permute-start(bf16[2048,1024]{1,0:T(8,128)(2,1)} %get-tuple-element.45), channel_id=1, source_target_pairs={{0,28},{4,0},{8,4},{12,8},{16,12},{20,16},{24,20},{28,24},{1,29},{... | collective-permute-start | bytes 12582920 | tf_op jit(solution)/shard_map/ppermute | solution.py:315
  318.9 0.1 reshape.31
  318.9 0.6 pad_add_fusion.1.place_ref
  319.6 0.6 pad_add_fusion.flag_ref
  320.2 10.7 %put_pairs.1.token_ref = bf16[2048,2048]{1,0:T(8,128)(2,1)} custom-call(s32[2]{0:T(128)} %pad_add_fusion.1.place_ref, bf16[512,2048]{1,0:T(8,128)(2,1)} %copy-done.1, bf16[512,2048]{1,0:T(8,128)(2,1)} %collective-permute-done.3.refs_1_, bf16[512,2048]{1,0:T(8,128)(2,1)} %collective-permute-done.4.refs_2_, bf16[512,2048]{1,0:T(8,128)(2,1)} %collective-permute-done.5.refs_3_, ...), custom_call_target="tpu_custom_call" | custom-call | flops 1000 | bytes 1000 | tf_op jit(solution)/shard_map/put_pairs/pallas_call | solution.py:247
  330.9 0.0 collective-permute-done.10.piece_ref
  331.0 19.8 %finish_columns.3 = (bf16[2048,2048]{1,0:T(8,128)(2,1)}, bf16[2,512,1024]{2,1,0:T(8,128)(2,1)}, bf16[2,512,1024]{2,1,0:T(8,128)(2,1)}) custom-call(s32[5]{0:T(128)} %pad_add_fusion.flag_ref, bf16[2048,2048]{1,0:T(8,128)(2,1)} %precondition_home.3.weight_ref, bf16[2048,1024]{1,0:T(8,128)(2,1)} %collective-permute-done.10.piece_ref, ...), custom_call_target="tpu_custom_call", output_to_operand_aliasing={{0}: (1, {})} | custom-call | flops 1000 | bytes 1000 | tf_op jit(solution)/shard_map/finish_columns/pallas_call | solution.py:176
  350.7 0.0 collective-permute-start.14
  350.7 4.4 collective-permute-done.14
  355.1 2.4 fusion.1
  357.5 2.1 collective-permute-start.15
  359.6 45.1 %collective-permute-done.13.piece_ref = bf16[2048,1024]{1,0:T(8,128)(2,1)} collective-permute-done((bf16[2048,1024]{1,0:T(8,128)(2,1)}, bf16[2048,1024]{1,0:T(8,128)(2,1)}, u32[]{:S(2)}, u32[]{:S(2)}) %collective-permute-start.13) | collective-permute-done | bytes 4194336 | tf_op jit(solution)/shard_map/ppermute | solution.py:315
  404.6 12.1 %finish_columns.4 = (bf16[2048,2048]{1,0:T(8,128)(2,1)}, bf16[2,512,512]{2,1,0:T(8,128)(2,1)}, bf16[2,512,512]{2,1,0:T(8,128)(2,1)}) custom-call(s32[5]{0:T(128)} %pad_add_fusion.flag_ref, bf16[2048,2048]{1,0:T(8,128)(2,1)} %get-tuple-element.44.weight_ref, bf16[2048,1024]{1,0:T(8,128)(2,1)} %collective-permute-done.13.piece_ref, ...), custom_call_target="tpu_custom_call", output_to_operand_aliasing={{0}: (1, {})} | custom-call | flops 1000 | bytes 1000 | tf_op jit(solution)/shard_map/finish_columns/pallas_call | solution.py:176
  416.7 1.0 copy-done.2
  417.7 12.2 %finish_columns.5 = (bf16[2048,2048]{1,0:T(8,128)(2,1)}, bf16[2,512,512]{2,1,0:T(8,128)(2,1)}, bf16[2,512,512]{2,1,0:T(8,128)(2,1)}) custom-call(s32[5]{0:T(128)} %pad_add_fusion.flag_ref, bf16[2048,2048]{1,0:T(8,128)(2,1)} %get-tuple-element.47.weight_ref, bf16[2048,1024]{1,0:T(8,128)(2,1)} %collective-permute-done.13.piece_ref, ...), custom_call_target="tpu_custom_call", output_to_operand_aliasing={{0}: (1, {})} | custom-call | flops 1000 | bytes 1000 | tf_op jit(solution)/shard_map/finish_columns/pallas_call | solution.py:176
  430.0 0.3 collective-permute-start.18
  430.3 0.9 fusion.4
  431.2 0.2 copy-done.11
  431.4 1.1 collective-permute-start.17
  432.5 0.5 collective-permute-done.18
  433.0 1.3 fusion.5
  434.4 1.1 collective-permute-start.19
  435.5 1.8 fusion
  437.4 0.2 dynamic_update_slice.9
  437.6 8.9 %collective-permute-done.17 = bf16[512,512]{1,0:T(8,128)(2,1)} collective-permute-done((bf16[512,512]{1,0:T(8,128)(2,1)}, bf16[512,512]{1,0:T(8,128)(2,1)}, u32[]{:S(2)}, u32[]{:S(2)}) %collective-permute-start.17) | collective-permute-done | bytes 524320 | tf_op jit(solution)/shard_map/ppermute | solution.py:273
  446.5 1.2 fusion.6
  447.8 9.2 %collective-permute-done.19 = bf16[512,512]{1,0:T(8,128)(2,1)S(1)} collective-permute-done((bf16[512,512]{1,0:T(8,128)(2,1)S(1)}, bf16[512,512]{1,0:T(8,128)(2,1)S(1)}, u32[]{:S(2)}, u32[]{:S(2)}) %collective-permute-start.19) | collective-permute-done | bytes 524320 | tf_op jit(solution)/shard_map/ppermute | solution.py:273
  457.0 1.2 fusion.7
  458.2 0.0 copy-start.7
  458.2 1.3 copy-done.7
  (27 shorter events, 0.1 us)
Async XLA Ops:
  0.6 26.4 %collective-permute-start = (bf16[256,2048]{1,0:T(8,128)(2,1)}, bf16[256,2048]{1,0:T(8,128)(2,1)S(1)}, u32[]{:S(2)}, u32[]{:S(2)}) collective-permute-start(bf16[256,2048]{1,0:T(8,128)(2,1)} %param.5), channel_id=1, source_target_pairs={{0,4},{4,0},{8,12},{12,8},{16,20},{20,16},{24,28},{28,24},{1,5},{5... | collective-permute-start | bytes 3145736 | tf_op jit(solution)/shard_map/ppermute | solution.py:202
  3.6 23.4 %copy-start.9 = (bf16[256,2048]{1,0:T(8,128)(2,1)S(1)}, bf16[256,2048]{1,0:T(8,128)(2,1)}, u32[]{:S(2)}) copy-start(bf16[256,2048]{1,0:T(8,128)(2,1)} %param.5) | copy-start | bytes 3145732
  27.3 3.5 copy-start.13
  27.4 190.0 %copy-start.1 = (bf16[512,2048]{1,0:T(8,128)(2,1)}, bf16[512,2048]{1,0:T(8,128)(2,1)S(1)}, u32[]{:S(2)}) copy-start(bf16[512,2048]{1,0:T(8,128)(2,1)S(1)} %pad_maximum_fusion.refs_0_) | copy-start | bytes 6291460
  27.4 96.6 %collective-permute-start.2 = (bf16[2048,1024]{1,0:T(8,128)(2,1)}, bf16[2048,1024]{1,0:T(8,128)(2,1)}, u32[]{:S(2)}, u32[]{:S(2)}) collective-permute-start(bf16[2048,1024]{1,0:T(8,128)(2,1)} %get-tuple-element.30), channel_id=1, source_target_pairs={{0,4},{4,8},{8,12},{12,16},{16,20},{20,24},{24,28},{28,0},{1,5},{5... | collective-permute-start | bytes 12582920 | tf_op jit(solution)/shard_map/ppermute | solution.py:299
  29.2 186.2 %collective-permute-start.1 = (bf16[2048,1024]{1,0:T(8,128)(2,1)}, bf16[2048,1024]{1,0:T(8,128)(2,1)}, u32[]{:S(2)}, u32[]{:S(2)}) collective-permute-start(bf16[2048,1024]{1,0:T(8,128)(2,1)} %get-tuple-element.28), channel_id=1, source_target_pairs={{0,4},{4,8},{8,12},{12,16},{16,20},{20,24},{24,28},{28,0},{1,5},{5... | collective-permute-start | bytes 12582920 | tf_op jit(solution)/shard_map/ppermute | solution.py:299
  31.7 115.6 %collective-permute-start.5 = (bf16[512,2048]{1,0:T(8,128)(2,1)S(1)}, bf16[512,2048]{1,0:T(8,128)(2,1)}, u32[]{:S(2)}, u32[]{:S(2)}) collective-permute-start(bf16[512,2048]{1,0:T(8,128)(2,1)S(1)} %pad_maximum_fusion.refs_0_), channel_id=1, source_target_pairs={{0,24},{8,0},{16,8},{24,16},{1,25},{9,1},{17,9},{25,17},{2,26},{10... | collective-permute-start | bytes 6291464 | tf_op jit(solution)/shard_map/ppermute | solution.py:210
  35.7 179.7 %collective-permute-start.4 = (bf16[512,2048]{1,0:T(8,128)(2,1)S(1)}, bf16[512,2048]{1,0:T(8,128)(2,1)}, u32[]{:S(2)}, u32[]{:S(2)}) collective-permute-start(bf16[512,2048]{1,0:T(8,128)(2,1)S(1)} %pad_maximum_fusion.refs_0_), channel_id=1, source_target_pairs={{0,16},{8,24},{16,0},{24,8},{1,17},{9,25},{17,1},{25,9},{2,18},{10... | collective-permute-start | bytes 6291464 | tf_op jit(solution)/shard_map/ppermute | solution.py:210
  38.5 176.9 %collective-permute-start.3 = (bf16[512,2048]{1,0:T(8,128)(2,1)S(1)}, bf16[512,2048]{1,0:T(8,128)(2,1)}, u32[]{:S(2)}, u32[]{:S(2)}) collective-permute-start(bf16[512,2048]{1,0:T(8,128)(2,1)S(1)} %pad_maximum_fusion.refs_0_), channel_id=1, source_target_pairs={{0,8},{8,16},{16,24},{24,0},{1,9},{9,17},{17,25},{25,1},{2,10},{10... | collective-permute-start | bytes 6291464 | tf_op jit(solution)/shard_map/ppermute | solution.py:210
  215.4 11.5 %collective-permute-start.8 = (bf16[512,2048]{1,0:T(8,128)(2,1)S(1)}, bf16[512,2048]{1,0:T(8,128)(2,1)}, u32[]{:S(2)}, u32[]{:S(2)}) collective-permute-start(bf16[512,2048]{1,0:T(8,128)(2,1)S(1)} %pad_maximum_fusion.refs_0_), channel_id=1, source_target_pairs={{12,4},{20,12},{28,20},{13,5},{21,13},{29,21},{14,6},{22,14},{30,2... | collective-permute-start | bytes 6291464 | tf_op jit(solution)/shard_map/ppermute | solution.py:217
  217.4 11.6 %collective-permute-start.6 = (bf16[512,2048]{1,0:T(8,128)(2,1)S(1)}, bf16[512,2048]{1,0:T(8,128)(2,1)}, u32[]{:S(2)}, u32[]{:S(2)}) collective-permute-start(bf16[512,2048]{1,0:T(8,128)(2,1)S(1)} %pad_maximum_fusion.refs_0_), channel_id=1, source_target_pairs={{4,12},{12,20},{20,28},{5,13},{13,21},{21,29},{6,14},{14,22},{22,3... | collective-permute-start | bytes 6291464 | tf_op jit(solution)/shard_map/ppermute | solution.py:216
  219.4 111.6 %collective-permute-start.10 = (bf16[2048,1024]{1,0:T(8,128)(2,1)}, bf16[2048,1024]{1,0:T(8,128)(2,1)}, u32[]{:S(2)}, u32[]{:S(2)}) collective-permute-start(bf16[2048,1024]{1,0:T(8,128)(2,1)} %get-tuple-element.38), channel_id=1, source_target_pairs={{0,28},{4,0},{8,4},{12,8},{16,12},{20,16},{24,20},{28,24},{1,29},{... | collective-permute-start | bytes 12582920 | tf_op jit(solution)/shard_map/ppermute | solution.py:311
  226.9 11.6 %collective-permute-start.9 = (bf16[512,2048]{1,0:T(8,128)(2,1)}, bf16[512,2048]{1,0:T(8,128)(2,1)}, u32[]{:S(2)}, u32[]{:S(2)}) collective-permute-start(bf16[512,2048]{1,0:T(8,128)(2,1)} %collective-permute-done.8.refs_7_), channel_id=1, source_target_pairs={{12,4},{20,12},{28,20},{13,5},{21,13},{29,21},{14,6},{22,14},{30,2... | collective-permute-start | bytes 6291464 | tf_op jit(solution)/shard_map/ppermute | solution.py:217
  229.0 9.6 %collective-permute-start.7 = (bf16[512,2048]{1,0:T(8,128)(2,1)}, bf16[512,2048]{1,0:T(8,128)(2,1)S(1)}, u32[]{:S(2)}, u32[]{:S(2)}) collective-permute-start(bf16[512,2048]{1,0:T(8,128)(2,1)} %collective-permute-done.6.refs_4_), channel_id=1, source_target_pairs={{4,12},{12,20},{20,28},{5,13},{13,21},{21,29},{6,14},{14,22},{22,3... | collective-permute-start | bytes 6291464 | tf_op jit(solution)/shard_map/ppermute | solution.py:216
  238.5 81.7 %copy-start.8 = (bf16[512,2048]{1,0:T(8,128)(2,1)}, bf16[512,2048]{1,0:T(8,128)(2,1)S(1)}, u32[]{:S(2)}) copy-start(bf16[512,2048]{1,0:T(8,128)(2,1)S(1)} %collective-permute-done.7.refs_5_) | copy-start | bytes 6291460
  238.5 81.7 %collective-permute-start.11 = (bf16[512,2048]{1,0:T(8,128)(2,1)S(1)}, bf16[512,2048]{1,0:T(8,128)(2,1)}, u32[]{:S(2)}, u32[]{:S(2)}) collective-permute-start(bf16[512,2048]{1,0:T(8,128)(2,1)S(1)} %collective-permute-done.7.refs_5_), channel_id=1, source_target_pairs={{4,12},{12,20},{20,28},{5,13},{13,21},{21,29},{6,14},{14,22},{22,3... | collective-permute-start | bytes 6291464 | tf_op jit(solution)/shard_map/ppermute | solution.py:216
  240.6 79.6 %collective-permute-start.12 = (bf16[512,2048]{1,0:T(8,128)(2,1)}, bf16[512,2048]{1,0:T(8,128)(2,1)}, u32[]{:S(2)}, u32[]{:S(2)}) collective-permute-start(bf16[512,2048]{1,0:T(8,128)(2,1)} %collective-permute-done.9.refs_8_), channel_id=1, source_target_pairs={{12,4},{20,12},{28,20},{13,5},{21,13},{29,21},{14,6},{22,14},{30,2... | collective-permute-start | bytes 6291464 | tf_op jit(solution)/shard_map/ppermute | solution.py:217
  242.6 162.0 %collective-permute-start.13 = (bf16[2048,1024]{1,0:T(8,128)(2,1)}, bf16[2048,1024]{1,0:T(8,128)(2,1)}, u32[]{:S(2)}, u32[]{:S(2)}) collective-permute-start(bf16[2048,1024]{1,0:T(8,128)(2,1)} %get-tuple-element.45), channel_id=1, source_target_pairs={{0,28},{4,0},{8,4},{12,8},{16,12},{20,16},{24,20},{28,24},{1,29},{... | collective-permute-start | bytes 12582920 | tf_op jit(solution)/shard_map/ppermute | solution.py:315
  350.7 4.4 collective-permute-start.14
  355.1 61.6 %copy-start.6 = (bf16[2,512,1024]{2,1,0:T(8,128)(2,1)}, bf16[2,512,1024]{2,1,0:T(8,128)(2,1)S(1)}, u32[]{:S(2)}) copy-start(bf16[2,512,1024]{2,1,0:T(8,128)(2,1)S(1)} %collective-permute-done.14) | copy-start | bytes 6291460
  357.5 59.2 %collective-permute-start.15 = (bf16[512,1024]{1,0:T(8,128)(2,1)S(1)}, bf16[512,1024]{1,0:T(8,128)(2,1)S(1)}, u32[]{:S(2)}, u32[]{:S(2)}) collective-permute-start(bf16[512,1024]{1,0:T(8,128)(2,1)S(1)} %fusion.1), channel_id=1, source_target_pairs={{0,2},{1,3},{2,0},{3,1},{4,6},{5,7},{6,4},{7,5},{8,10},{9,11},{10,... | collective-permute-start | bytes 3145736 | tf_op jit(solution)/shard_map/ppermute | solution.py:273
  416.7 13.6 %collective-permute-start.16 = (bf16[2,512,512]{2,1,0:T(8,128)(2,1)}, bf16[2,512,512]{2,1,0:T(8,128)(2,1)S(1)}, u32[]{:S(2)}, u32[]{:S(2)}) collective-permute-start(bf16[2,512,512]{2,1,0:T(8,128)(2,1)} %get-tuple-element.51), channel_id=1, source_target_pairs={{0,1},{1,0},{2,3},{3,2},{4,5},{5,4},{6,7},{7,6},{8,9},{9,8},{10,11... | collective-permute-start | bytes 3145736 | tf_op jit(solution)/shard_map/ppermute | solution.py:339
  416.7 1.0 copy-start.2
  417.7 12.6 %copy-start.4 = (bf16[2,512,512]{2,1,0:T(8,128)(2,1)S(1)}, bf16[2,512,512]{2,1,0:T(8,128)(2,1)}, u32[]{:S(2)}) copy-start(bf16[2,512,512]{2,1,0:T(8,128)(2,1)} %get-tuple-element.48.rest_0_) | copy-start | bytes 3145732
  430.0 5.5 %copy-start = (bf16[2,512,1024]{2,1,0:T(8,128)(2,1)S(1)}, bf16[2,512,1024]{2,1,0:T(8,128)(2,1)}, u32[]{:S(2)}) copy-start(bf16[2,512,1024]{2,1,0:T(8,128)(2,1)} %get-tuple-element.46.rest_0_) | copy-start | bytes 6291460
  430.0 5.5 %copy-start.3 = (bf16[512,1024]{1,0:T(8,128)(2,1)S(1)}, bf16[512,1024]{1,0:T(8,128)(2,1)}, u32[]{:S(2)}) copy-start(bf16[512,1024]{1,0:T(8,128)(2,1)} %copy-done.2) | copy-start | bytes 3145732
  430.0 3.1 collective-permute-start.18
  430.3 1.1 copy-start.11
  431.4 15.1 %collective-permute-start.17 = (bf16[512,512]{1,0:T(8,128)(2,1)}, bf16[512,512]{1,0:T(8,128)(2,1)}, u32[]{:S(2)}, u32[]{:S(2)}) collective-permute-start(bf16[512,512]{1,0:T(8,128)(2,1)} %fusion.4), channel_id=1, source_target_pairs={{0,2},{1,3},{2,0},{3,1},{4,6},{5,7},{6,4},{7,5},{8,10},{9,11},{10,... | collective-permute-start | bytes 1572872 | tf_op jit(solution)/shard_map/ppermute | solution.py:273
  434.4 22.6 %collective-permute-start.19 = (bf16[512,512]{1,0:T(8,128)(2,1)S(1)}, bf16[512,512]{1,0:T(8,128)(2,1)S(1)}, u32[]{:S(2)}, u32[]{:S(2)}) collective-permute-start(bf16[512,512]{1,0:T(8,128)(2,1)S(1)} %fusion.5), channel_id=1, source_target_pairs={{0,2},{1,3},{2,0},{3,1},{4,6},{5,7},{6,4},{7,5},{8,10},{9,11},{10,... | collective-permute-start | bytes 1572872 | tf_op jit(solution)/shard_map/ppermute | solution.py:273
  437.3 9.2 %copy-start.5 = (bf16[2,512,512]{2,1,0:T(8,128)(2,1)S(1)}, bf16[2,512,512]{2,1,0:T(8,128)(2,1)}, u32[]{:S(2)}) copy-start(bf16[2,512,512]{2,1,0:T(8,128)(2,1)} %get-tuple-element.48.rest_0_) | copy-start | bytes 3145732
  437.4 9.2 %copy-start.12 = (bf16[2,512,512]{2,1,0:T(8,128)(2,1)S(1)}, bf16[2,512,512]{2,1,0:T(8,128)(2,1)}, u32[]{:S(2)}) copy-start(bf16[2,512,512]{2,1,0:T(8,128)(2,1)} %copy-done.11) | copy-start | bytes 3145732
  437.4 19.6 %copy-start.10 = (bf16[2,512,512]{2,1,0:T(8,128)(2,1)S(1)}, bf16[2,512,512]{2,1,0:T(8,128)(2,1)}, u32[]{:S(2)}) copy-start(bf16[2,512,512]{2,1,0:T(8,128)(2,1)} %get-tuple-element.52) | copy-start | bytes 3145732
  458.2 1.3 copy-start.7

commit v6 on v5

--- a/solution.py
+++ b/solution.py
@@ -225,23 +225,24 @@
     downs = [below for _, below in late]
 
     def kernel(place_ref, *refs):
-        pair_ref, *others, out_ref, sem = refs
+        pair_ref, *others, out_ref, sems = refs
         early_refs, up_refs, down_refs = (others[i * (pairs - 1):(i + 1) * (pairs - 1)] for i in range(3))
-        t = pl.program_id(0)
-        apart = place_ref[0] - t
         odd = place_ref[1] == 1
-        cases = [(apart == 0, pair_ref)]
-        for step in range(1, pairs):
-            cases.append((jnp.logical_and(odd, apart == step), up_refs[step - 1]))
-            cases.append((jnp.logical_and(odd, apart == -step), down_refs[step - 1]))
-            around = jnp.logical_or(apart == step, apart == step - pairs)
-            cases.append((jnp.logical_and(jnp.logical_not(odd), around), early_refs[step - 1]))
-        for case, source in cases:
-            @pl.when(case)
-            def _():
-                copy = pltpu.make_async_copy(source, out_ref, sem)
-                copy.start()
-                copy.wait()
+        copies = []
+        for t in range(pairs):
+            apart = place_ref[0] - t
+            cases = [(apart == 0, pair_ref)]
+            for step in range(1, pairs):
+                cases.append((jnp.logical_and(odd, apart == step), up_refs[step - 1]))
+                cases.append((jnp.logical_and(odd, apart == -step), down_refs[step - 1]))
+                around = jnp.logical_or(apart == step, apart == step - pairs)
+                cases.append((jnp.logical_and(jnp.logical_not(odd), around), early_refs[step - 1]))
+            for case, source in cases:
+                copies.append((case, source, out_ref.at[pl.ds(t * rows, rows), :], sems.at[t]))
+        for case, *copy in copies:
+            pl.when(case)(lambda copy=copy: pltpu.make_async_copy(*copy).start())
+        for case, *copy in copies:
+            pl.when(case)(lambda copy=copy: pltpu.make_async_copy(*copy).wait())
 
     count = 1 + 3 * (pairs - 1)
     return pl.pallas_call(
@@ -249,11 +250,12 @@
         out_shape=jax.ShapeDtypeStruct((rows * pairs, depth), pair.dtype),
         grid_spec=pltpu.PrefetchScalarGridSpec(
             num_scalar_prefetch=1,
-            grid=(pairs,),
+            grid=(1,),
             in_specs=[pl.BlockSpec(memory_space=pl.ANY)] * count,
-            out_specs=pl.BlockSpec((rows, depth), lambda t, f: (t, 0)),
-            scratch_shapes=[pltpu.SemaphoreType.DMA],
+            out_specs=pl.BlockSpec((rows * pairs, depth), lambda t, f: (0, 0)),
+            scratch_shapes=[pltpu.SemaphoreType.DMA((pairs,))],
         ),
+        compiler_params=pltpu.CompilerParams(vmem_limit_bytes=40 << 20),
         cost_estimate=pl.CostEstimate(flops=1000, bytes_accessed=1000, transcendentals=0),
         name="put_pairs",
     )(jnp.stack([row_place // 2, row_place % 2]), pair, *early, *ups, *downs)

time: 462 us -> 460 us (level)
  starting transfers between devices: 108 us -> 98.8 us
  waiting for transfers between devices: 236 us -> 243 us
    ppermute x1, starting transfers between devices: 76.3 us -> 65.4 us  [on_device(): returned.append(lax.ppermute(lent, 'row', back))]
    pallas_call x2, Pallas kernels: 15.2 us -> 25.4 us  [precondition_lent(): pl.pallas_call(kernel, out_shape=[jax.ShapeDtypeStruct((down * width, sto...]
  transfers between devices with their start and end apart: 20 -> 20, of which waited for: 8 -> 7; matrix products, arithmetic and copies ran while one was open for 4% -> 3% of each run, Pallas kernels for 21% -> 21%
where the time goes in v6:
time: 460 us; the launch traced here: 459 us
  waiting for transfers between devices  243 us (53%)
  starting transfers between devices  98.8 us (21%)
  Pallas kernels  96.9 us (21%)
  other arithmetic  10.2 us (2%)
  local copies, waits for them, and re-layouts  9.77 us (2%)
    ppermute x2, waiting for transfers between devices, on_device(): came = [lax.ppermute(column, 'row', forth) for column in columns]  82.1 us
    ppermute x3, waiting for transfers between devices, ring_direct(): lax.ppermute(pair, 'row', [(i, (i + 2 * step) % row_count) for i in sides])  72.1 us
    ppermute x1, starting transfers between devices, on_device(): returned.append(lax.ppermute(lent, 'row', back))  65.4 us
    ppermute x1, waiting for transfers between devices, on_device(): returned.append(lax.ppermute(lent, 'row', back))  49.3 us
    pallas_call x3, Pallas kernels, finish_columns(): pl.pallas_call(kernel, out_shape=(jax.ShapeDtypeStruct(new_weight.shape,...  44.6 us
    pallas_call x2, Pallas kernels, precondition_lent(): pl.pallas_call(kernel, out_shape=[jax.ShapeDtypeStruct((down * width, sto...  25.4 us
    pallas_call x2, Pallas kernels, precondition_home(): pl.pallas_call(kernel, out_shape=jax.ShapeDtypeStruct(weight.shape, jnp.b...  19.9 us
    ppermute x3, waiting for transfers between devices, far_sum(): arrived.append(lax.ppermute(piece, 'col', shift_route(col_count, 2 * step)))  17.5 us
  transfers between devices with their start and end apart: 20, of which 7 were waited for; matrix products, arithmetic and copies ran while one was open for 3% of the time, Pallas kernels for 21%

profile of v6, /device:TPU:0, one launch (start us, length us, event | category | flops | bytes accessed | tf_op | source)
XLA Modules:
  0.0 459.0 jit_solution(1867174780501671319)
XLA Ops:
  0.6 3.0 collective-permute-start
  3.6 6.1 %fusion.8 = (bf16[2048,1024]{1,0:T(8,128)(2,1)}, bf16[2048,1024]{1,0:T(8,128)(2,1)}) fusion(bf16[2048,2048]{1,0:T(8,128)(2,1)} %grad_ref.3), kind=kLoop, calls=%fused_computation.25 | loop fusion | bytes 16777216 | tf_op jit(solution)/shard_map/slice | solution.py:299
  9.7 17.3 %collective-permute-done = bf16[256,2048]{1,0:T(8,128)(2,1)S(1)} collective-permute-done((bf16[256,2048]{1,0:T(8,128)(2,1)}, bf16[256,2048]{1,0:T(8,128)(2,1)S(1)}, u32[]{:S(2)}, u32[]{:S(2)}) %collective-permute-start) | collective-permute-done | bytes 1048608 | tf_op jit(solution)/shard_map/ppermute | solution.py:202
  27.0 0.3 broadcast_select_fusion.1
  27.3 0.0 copy-start.11
  27.3 0.1 pad_maximum_fusion.refs_0_
  27.4 1.8 collective-permute-start.2
  29.2 1.5 collective-permute-start.1
  30.8 0.1 compare_convert_fusion
  30.9 0.8 slice_reduce_fusion
  31.6 4.0 collective-permute-start.5
  35.7 2.8 collective-permute-start.4
  38.5 3.5 collective-permute-start.3
  42.0 82.1 %collective-permute-done.2.grad_ref = bf16[2048,1024]{1,0:T(8,128)(2,1)} collective-permute-done((bf16[2048,1024]{1,0:T(8,128)(2,1)}, bf16[2048,1024]{1,0:T(8,128)(2,1)}, u32[]{:S(2)}, u32[]{:S(2)}) %collective-permute-start.2) | collective-permute-done | bytes 4194336 | tf_op jit(solution)/shard_map/ppermute | solution.py:301
  124.1 10.5 %precondition_lent.2 = (bf16[2048,1024]{1,0:T(8,128)(2,1)}, f32[8,128]{1,0:T(8,128)}) custom-call(s32[2]{0:T(128)} %get-tuple-element.55.flag_ref, bf16[2,2,2,2,1024,1024]{5,4,3,2,1,0:T(8,128)(2,1)} %right_ref.7, bf16[2048,1024]{1,0:T(8,128)(2,1)} %collective-permute-done.2.grad_ref, bf16[2,2,2,2,1024,1024]{5,4,3,2,1,0:T(8,128)(2,1)} %right_ref.7), custom_call_target="tpu_custom_call" | custom-call | flops 8589934592 | bytes 16777216 | tf_op jit(solution)/shard_map/precondition_lent/pallas_call | solution.py:63
  134.6 8.7 %precondition_home.2.rest_0_ = bf16[2048,2048]{1,0:T(8,128)(2,1)} custom-call(s32[2]{0:T(128)} %get-tuple-element.64.flag_ref, bf16[2,2,2,2,1024,1024]{5,4,3,2,1,0:T(8,128)(2,1)} %right_ref.7, bf16[2048,2048]{1,0:T(8,128)(2,1)} %grad_ref.3, bf16[2,2,2,2,1024,1024]{5,4,3,2,1,0:T(8,128)(2,1)} %right_ref.7, bf16[2048,2048]{1,0:T(8,128)(2,1)} %weight_ref.3, ...), custom_call_target="tpu_custom_call" | custom-call | flops 34359738368 | bytes 83886080 | tf_op jit(solution)/shard_map/precondition_home/pallas_call | solution.py:107
  143.3 0.0 collective-permute-done.5.refs_3_
  143.4 72.1 %collective-permute-done.4.refs_2_ = bf16[512,2048]{1,0:T(8,128)(2,1)} collective-permute-done((bf16[512,2048]{1,0:T(8,128)(2,1)S(1)}, bf16[512,2048]{1,0:T(8,128)(2,1)}, u32[]{:S(2)}, u32[]{:S(2)}) %collective-permute-start.4) | collective-permute-done | bytes 2097184 | tf_op jit(solution)/shard_map/ppermute | solution.py:210
  215.4 0.0 collective-permute-done.3.refs_1_
  215.4 0.0 collective-permute-done.1.grad_ref
  215.4 1.9 collective-permute-start.8
  217.4 2.0 collective-permute-start.6
  219.3 0.0 collective-permute-start.10
  219.3 14.9 %precondition_lent.3 = (bf16[2048,1024]{1,0:T(8,128)(2,1)}, f32[8,128]{1,0:T(8,128)}) custom-call(s32[2]{0:T(128)} %get-tuple-element.54.flag_ref, bf16[2,2,2,2,1024,1024]{5,4,3,2,1,0:T(8,128)(2,1)} %right_ref.7, bf16[2048,1024]{1,0:T(8,128)(2,1)} %collective-permute-done.1.grad_ref, bf16[2,2,2,2,1024,1024]{5,4,3,2,1,0:T(8,128)(2,1)} %right_ref.7), custom_call_target="tpu_custom_call" | custom-call | flops 8589934592 | bytes 16777216 | tf_op jit(solution)/shard_map/precondition_lent/pallas_call | solution.py:63
  234.3 0.0 collective-permute-done.8.refs_7_
  234.3 2.0 collective-permute-start.9
  236.2 0.0 collective-permute-done.6.refs_4_
  236.2 2.0 collective-permute-start.7
  238.2 11.2 %precondition_home.3.weight_ref = bf16[2048,2048]{1,0:T(8,128)(2,1)} custom-call(s32[2]{0:T(128)} %get-tuple-element.65.flag_ref, bf16[2,2,2,2,1024,1024]{5,4,3,2,1,0:T(8,128)(2,1)} %right_ref.7, bf16[2048,2048]{1,0:T(8,128)(2,1)} %grad_ref.3, bf16[2,2,2,2,1024,1024]{5,4,3,2,1,0:T(8,128)(2,1)} %right_ref.7, ...), custom_call_target="tpu_custom_call", output_to_operand_aliasing={{}: (5, {})} | custom-call | flops 34359738368 | bytes 83886080 | tf_op jit(solution)/shard_map/precondition_home/pallas_call | solution.py:107
  249.4 0.0 collective-permute-done.9.refs_8_
  249.4 0.0 collective-permute-done.7.refs_5_
  249.4 2.0 collective-permute-start.11
  251.5 2.0 collective-permute-start.12
  253.5 65.4 %collective-permute-start.13 = (bf16[2048,1024]{1,0:T(8,128)(2,1)}, bf16[2048,1024]{1,0:T(8,128)(2,1)}, u32[]{:S(2)}, u32[]{:S(2)}) collective-permute-start(bf16[2048,1024]{1,0:T(8,128)(2,1)} %get-tuple-element.45), channel_id=1, source_target_pairs={{0,28},{4,0},{8,4},{12,8},{16,12},{20,16},{24,20},{28,24},{1,29},{... | collective-permute-start | bytes 12582920 | tf_op jit(solution)/shard_map/ppermute | solution.py:317
  318.9 0.1 reshape.31
  319.0 0.1 pad_add_fusion.1.place_ref
  319.1 0.6 pad_add_fusion.flag_ref
  319.7 0.0 collective-permute-done.11.refs_6_
  319.7 0.0 collective-permute-done.12.refs_9_
  319.7 7.0 %put_pairs.1.token_ref = bf16[2048,2048]{1,0:T(8,128)(2,1)} custom-call(s32[2]{0:T(128)S(1)} %pad_add_fusion.1.place_ref, bf16[512,2048]{1,0:T(8,128)(2,1)S(1)} %pad_maximum_fusion.refs_0_, bf16[512,2048]{1,0:T(8,128)(2,1)} %collective-permute-done.3.refs_1_, bf16[512,2048]{1,0:T(8,128)(2,1)} %collective-permute-done.4.refs_2_, ...), custom_call_target="tpu_custom_call" | custom-call | flops 1000 | bytes 1000 | tf_op jit(solution)/shard_map/put_pairs/pallas_call | solution.py:248
  326.7 0.0 collective-permute-done.10.piece_ref
  326.7 20.7 %finish_columns.3 = (bf16[2048,2048]{1,0:T(8,128)(2,1)}, bf16[2,512,1024]{2,1,0:T(8,128)(2,1)}, bf16[2,512,1024]{2,1,0:T(8,128)(2,1)}) custom-call(s32[5]{0:T(128)} %pad_add_fusion.flag_ref, bf16[2048,2048]{1,0:T(8,128)(2,1)} %precondition_home.3.weight_ref, bf16[2048,1024]{1,0:T(8,128)(2,1)} %collective-permute-done.10.piece_ref, ...), custom_call_target="tpu_custom_call", output_to_operand_aliasing={{0}: (1, {})} | custom-call | flops 1000 | bytes 1000 | tf_op jit(solution)/shard_map/finish_columns/pallas_call | solution.py:176
  347.4 4.4 collective-permute-done.14
  351.8 2.4 fusion.1
  354.2 1.1 collective-permute-start.15
  355.3 49.3 %collective-permute-done.13.piece_ref = bf16[2048,1024]{1,0:T(8,128)(2,1)} collective-permute-done((bf16[2048,1024]{1,0:T(8,128)(2,1)}, bf16[2048,1024]{1,0:T(8,128)(2,1)}, u32[]{:S(2)}, u32[]{:S(2)}) %collective-permute-start.13) | collective-permute-done | bytes 4194336 | tf_op jit(solution)/shard_map/ppermute | solution.py:317
  404.6 11.8 %finish_columns.4 = (bf16[2048,2048]{1,0:T(8,128)(2,1)}, bf16[2,512,512]{2,1,0:T(8,128)(2,1)}, bf16[2,512,512]{2,1,0:T(8,128)(2,1)}) custom-call(s32[5]{0:T(128)} %pad_add_fusion.flag_ref, bf16[2048,2048]{1,0:T(8,128)(2,1)} %get-tuple-element.44.weight_ref, bf16[2048,1024]{1,0:T(8,128)(2,1)} %collective-permute-done.13.piece_ref, ...), custom_call_target="tpu_custom_call", output_to_operand_aliasing={{0}: (1, {})} | custom-call | flops 1000 | bytes 1000 | tf_op jit(solution)/shard_map/finish_columns/pallas_call | solution.py:176
  416.4 1.0 copy-done.1
  417.4 12.0 %finish_columns.5 = (bf16[2048,2048]{1,0:T(8,128)(2,1)}, bf16[2,512,512]{2,1,0:T(8,128)(2,1)}, bf16[2,512,512]{2,1,0:T(8,128)(2,1)}) custom-call(s32[5]{0:T(128)} %pad_add_fusion.flag_ref, bf16[2048,2048]{1,0:T(8,128)(2,1)} %get-tuple-element.47.weight_ref, bf16[2048,1024]{1,0:T(8,128)(2,1)} %collective-permute-done.13.piece_ref, ...), custom_call_target="tpu_custom_call", output_to_operand_aliasing={{0}: (1, {})} | custom-call | flops 1000 | bytes 1000 | tf_op jit(solution)/shard_map/finish_columns/pallas_call | solution.py:176
  429.5 0.6 collective-permute-start.18
  430.0 0.9 fusion.4
  431.0 0.2 copy-done.9
  431.1 1.5 collective-permute-start.17
  432.7 0.0 collective-permute-done.18
  432.7 1.3 fusion.5
  434.0 1.6 collective-permute-start.19
  435.6 1.8 fusion
  437.5 0.2 dynamic_update_slice.9
  437.7 8.6 %collective-permute-done.17 = bf16[512,512]{1,0:T(8,128)(2,1)} collective-permute-done((bf16[512,512]{1,0:T(8,128)(2,1)}, bf16[512,512]{1,0:T(8,128)(2,1)}, u32[]{:S(2)}, u32[]{:S(2)}) %collective-permute-start.17) | collective-permute-done | bytes 524320 | tf_op jit(solution)/shard_map/ppermute | solution.py:275
  446.3 1.2 fusion.6
  447.5 8.9 %collective-permute-done.19 = bf16[512,512]{1,0:T(8,128)(2,1)S(1)} collective-permute-done((bf16[512,512]{1,0:T(8,128)(2,1)S(1)}, bf16[512,512]{1,0:T(8,128)(2,1)S(1)}, u32[]{:S(2)}, u32[]{:S(2)}) %collective-permute-start.19) | collective-permute-done | bytes 524320 | tf_op jit(solution)/shard_map/ppermute | solution.py:275
  456.5 1.2 fusion.7
  457.7 0.0 copy-start.6
  457.7 1.3 copy-done.6
  (23 shorter events, 0.0 us)
Async XLA Ops:
  0.6 26.4 %collective-permute-start = (bf16[256,2048]{1,0:T(8,128)(2,1)}, bf16[256,2048]{1,0:T(8,128)(2,1)S(1)}, u32[]{:S(2)}, u32[]{:S(2)}) collective-permute-start(bf16[256,2048]{1,0:T(8,128)(2,1)} %param.5), channel_id=1, source_target_pairs={{0,4},{4,0},{8,12},{12,8},{16,20},{20,16},{24,28},{28,24},{1,5},{5... | collective-permute-start | bytes 3145736 | tf_op jit(solution)/shard_map/ppermute | solution.py:202
  3.6 23.4 %copy-start.7 = (bf16[256,2048]{1,0:T(8,128)(2,1)S(1)}, bf16[256,2048]{1,0:T(8,128)(2,1)}, u32[]{:S(2)}) copy-start(bf16[256,2048]{1,0:T(8,128)(2,1)} %param.5) | copy-start | bytes 3145732
  27.3 3.5 copy-start.11
  27.4 96.6 %collective-permute-start.2 = (bf16[2048,1024]{1,0:T(8,128)(2,1)}, bf16[2048,1024]{1,0:T(8,128)(2,1)}, u32[]{:S(2)}, u32[]{:S(2)}) collective-permute-start(bf16[2048,1024]{1,0:T(8,128)(2,1)} %get-tuple-element.30), channel_id=1, source_target_pairs={{0,4},{4,8},{8,12},{12,16},{16,20},{20,24},{24,28},{28,0},{1,5},{5... | collective-permute-start | bytes 12582920 | tf_op jit(solution)/shard_map/ppermute | solution.py:301
  29.2 186.2 %collective-permute-start.1 = (bf16[2048,1024]{1,0:T(8,128)(2,1)}, bf16[2048,1024]{1,0:T(8,128)(2,1)}, u32[]{:S(2)}, u32[]{:S(2)}) collective-permute-start(bf16[2048,1024]{1,0:T(8,128)(2,1)} %get-tuple-element.28), channel_id=1, source_target_pairs={{0,4},{4,8},{8,12},{12,16},{16,20},{20,24},{24,28},{28,0},{1,5},{5... | collective-permute-start | bytes 12582920 | tf_op jit(solution)/shard_map/ppermute | solution.py:301
  31.6 111.7 %collective-permute-start.5 = (bf16[512,2048]{1,0:T(8,128)(2,1)S(1)}, bf16[512,2048]{1,0:T(8,128)(2,1)}, u32[]{:S(2)}, u32[]{:S(2)}) collective-permute-start(bf16[512,2048]{1,0:T(8,128)(2,1)S(1)} %pad_maximum_fusion.refs_0_), channel_id=1, source_target_pairs={{0,24},{8,0},{16,8},{24,16},{1,25},{9,1},{17,9},{25,17},{2,26},{10... | collective-permute-start | bytes 6291464 | tf_op jit(solution)/shard_map/ppermute | solution.py:210
  35.7 179.7 %collective-permute-start.4 = (bf16[512,2048]{1,0:T(8,128)(2,1)S(1)}, bf16[512,2048]{1,0:T(8,128)(2,1)}, u32[]{:S(2)}, u32[]{:S(2)}) collective-permute-start(bf16[512,2048]{1,0:T(8,128)(2,1)S(1)} %pad_maximum_fusion.refs_0_), channel_id=1, source_target_pairs={{0,16},{8,24},{16,0},{24,8},{1,17},{9,25},{17,1},{25,9},{2,18},{10... | collective-permute-start | bytes 6291464 | tf_op jit(solution)/shard_map/ppermute | solution.py:210
  38.5 176.9 %collective-permute-start.3 = (bf16[512,2048]{1,0:T(8,128)(2,1)S(1)}, bf16[512,2048]{1,0:T(8,128)(2,1)}, u32[]{:S(2)}, u32[]{:S(2)}) collective-permute-start(bf16[512,2048]{1,0:T(8,128)(2,1)S(1)} %pad_maximum_fusion.refs_0_), channel_id=1, source_target_pairs={{0,8},{8,16},{16,24},{24,0},{1,9},{9,17},{17,25},{25,1},{2,10},{10... | collective-permute-start | bytes 6291464 | tf_op jit(solution)/shard_map/ppermute | solution.py:210
  215.4 18.8 %collective-permute-start.8 = (bf16[512,2048]{1,0:T(8,128)(2,1)S(1)}, bf16[512,2048]{1,0:T(8,128)(2,1)}, u32[]{:S(2)}, u32[]{:S(2)}) collective-permute-start(bf16[512,2048]{1,0:T(8,128)(2,1)S(1)} %pad_maximum_fusion.refs_0_), channel_id=1, source_target_pairs={{12,4},{20,12},{28,20},{13,5},{21,13},{29,21},{14,6},{22,14},{30,2... | collective-permute-start | bytes 6291464 | tf_op jit(solution)/shard_map/ppermute | solution.py:217
  217.4 18.9 %collective-permute-start.6 = (bf16[512,2048]{1,0:T(8,128)(2,1)S(1)}, bf16[512,2048]{1,0:T(8,128)(2,1)}, u32[]{:S(2)}, u32[]{:S(2)}) collective-permute-start(bf16[512,2048]{1,0:T(8,128)(2,1)S(1)} %pad_maximum_fusion.refs_0_), channel_id=1, source_target_pairs={{4,12},{12,20},{20,28},{5,13},{13,21},{21,29},{6,14},{14,22},{22,3... | collective-permute-start | bytes 6291464 | tf_op jit(solution)/shard_map/ppermute | solution.py:216
  219.3 107.4 %collective-permute-start.10 = (bf16[2048,1024]{1,0:T(8,128)(2,1)}, bf16[2048,1024]{1,0:T(8,128)(2,1)}, u32[]{:S(2)}, u32[]{:S(2)}) collective-permute-start(bf16[2048,1024]{1,0:T(8,128)(2,1)} %get-tuple-element.38), channel_id=1, source_target_pairs={{0,28},{4,0},{8,4},{12,8},{16,12},{20,16},{24,20},{28,24},{1,29},{... | collective-permute-start | bytes 12582920 | tf_op jit(solution)/shard_map/ppermute | solution.py:313
  234.3 15.2 %collective-permute-start.9 = (bf16[512,2048]{1,0:T(8,128)(2,1)}, bf16[512,2048]{1,0:T(8,128)(2,1)}, u32[]{:S(2)}, u32[]{:S(2)}) collective-permute-start(bf16[512,2048]{1,0:T(8,128)(2,1)} %collective-permute-done.8.refs_7_), channel_id=1, source_target_pairs={{12,4},{20,12},{28,20},{13,5},{21,13},{29,21},{14,6},{22,14},{30,2... | collective-permute-start | bytes 6291464 | tf_op jit(solution)/shard_map/ppermute | solution.py:217
  236.2 13.2 %collective-permute-start.7 = (bf16[512,2048]{1,0:T(8,128)(2,1)}, bf16[512,2048]{1,0:T(8,128)(2,1)}, u32[]{:S(2)}, u32[]{:S(2)}) collective-permute-start(bf16[512,2048]{1,0:T(8,128)(2,1)} %collective-permute-done.6.refs_4_), channel_id=1, source_target_pairs={{4,12},{12,20},{20,28},{5,13},{13,21},{21,29},{6,14},{14,22},{22,3... | collective-permute-start | bytes 6291464 | tf_op jit(solution)/shard_map/ppermute | solution.py:216
  249.4 70.3 %collective-permute-start.11 = (bf16[512,2048]{1,0:T(8,128)(2,1)}, bf16[512,2048]{1,0:T(8,128)(2,1)}, u32[]{:S(2)}, u32[]{:S(2)}) collective-permute-start(bf16[512,2048]{1,0:T(8,128)(2,1)} %collective-permute-done.7.refs_5_), channel_id=1, source_target_pairs={{4,12},{12,20},{20,28},{5,13},{13,21},{21,29},{6,14},{14,22},{22,3... | collective-permute-start | bytes 6291464 | tf_op jit(solution)/shard_map/ppermute | solution.py:216
  251.5 68.2 %collective-permute-start.12 = (bf16[512,2048]{1,0:T(8,128)(2,1)}, bf16[512,2048]{1,0:T(8,128)(2,1)}, u32[]{:S(2)}, u32[]{:S(2)}) collective-permute-start(bf16[512,2048]{1,0:T(8,128)(2,1)} %collective-permute-done.9.refs_8_), channel_id=1, source_target_pairs={{12,4},{20,12},{28,20},{13,5},{21,13},{29,21},{14,6},{22,14},{30,2... | collective-permute-start | bytes 6291464 | tf_op jit(solution)/shard_map/ppermute | solution.py:217
  253.5 151.1 %collective-permute-start.13 = (bf16[2048,1024]{1,0:T(8,128)(2,1)}, bf16[2048,1024]{1,0:T(8,128)(2,1)}, u32[]{:S(2)}, u32[]{:S(2)}) collective-permute-start(bf16[2048,1024]{1,0:T(8,128)(2,1)} %get-tuple-element.45), channel_id=1, source_target_pairs={{0,28},{4,0},{8,4},{12,8},{16,12},{20,16},{24,20},{28,24},{1,29},{... | collective-permute-start | bytes 12582920 | tf_op jit(solution)/shard_map/ppermute | solution.py:317
  347.4 4.4 collective-permute-start.14
  351.8 64.6 %copy-start.5 = (bf16[2,512,1024]{2,1,0:T(8,128)(2,1)}, bf16[2,512,1024]{2,1,0:T(8,128)(2,1)S(1)}, u32[]{:S(2)}) copy-start(bf16[2,512,1024]{2,1,0:T(8,128)(2,1)S(1)} %collective-permute-done.14) | copy-start | bytes 6291460
  354.2 62.2 %collective-permute-start.15 = (bf16[512,1024]{1,0:T(8,128)(2,1)S(1)}, bf16[512,1024]{1,0:T(8,128)(2,1)S(1)}, u32[]{:S(2)}, u32[]{:S(2)}) collective-permute-start(bf16[512,1024]{1,0:T(8,128)(2,1)S(1)} %fusion.1), channel_id=1, source_target_pairs={{0,2},{1,3},{2,0},{3,1},{4,6},{5,7},{6,4},{7,5},{8,10},{9,11},{10,... | collective-permute-start | bytes 3145736 | tf_op jit(solution)/shard_map/ppermute | solution.py:275
  416.4 13.6 %collective-permute-start.16 = (bf16[2,512,512]{2,1,0:T(8,128)(2,1)}, bf16[2,512,512]{2,1,0:T(8,128)(2,1)S(1)}, u32[]{:S(2)}, u32[]{:S(2)}) collective-permute-start(bf16[2,512,512]{2,1,0:T(8,128)(2,1)} %get-tuple-element.51), channel_id=1, source_target_pairs={{0,1},{1,0},{2,3},{3,2},{4,5},{5,4},{6,7},{7,6},{8,9},{9,8},{10,11... | collective-permute-start | bytes 3145736 | tf_op jit(solution)/shard_map/ppermute | solution.py:341
  416.4 1.0 copy-start.1
  417.4 12.6 %copy-start.3 = (bf16[2,512,512]{2,1,0:T(8,128)(2,1)S(1)}, bf16[2,512,512]{2,1,0:T(8,128)(2,1)}, u32[]{:S(2)}) copy-start(bf16[2,512,512]{2,1,0:T(8,128)(2,1)} %get-tuple-element.48.rest_0_) | copy-start | bytes 3145732
  429.4 6.1 %copy-start = (bf16[2,512,1024]{2,1,0:T(8,128)(2,1)S(1)}, bf16[2,512,1024]{2,1,0:T(8,128)(2,1)}, u32[]{:S(2)}) copy-start(bf16[2,512,1024]{2,1,0:T(8,128)(2,1)} %get-tuple-element.46.rest_0_) | copy-start | bytes 6291460
  429.4 6.1 %copy-start.2 = (bf16[512,1024]{1,0:T(8,128)(2,1)S(1)}, bf16[512,1024]{1,0:T(8,128)(2,1)}, u32[]{:S(2)}) copy-start(bf16[512,1024]{1,0:T(8,128)(2,1)} %copy-done.1) | copy-start | bytes 3145732
  429.5 3.2 collective-permute-start.18
  430.0 1.1 copy-start.9
  431.1 15.1 %collective-permute-start.17 = (bf16[512,512]{1,0:T(8,128)(2,1)}, bf16[512,512]{1,0:T(8,128)(2,1)}, u32[]{:S(2)}, u32[]{:S(2)}) collective-permute-start(bf16[512,512]{1,0:T(8,128)(2,1)} %fusion.4), channel_id=1, source_target_pairs={{0,2},{1,3},{2,0},{3,1},{4,6},{5,7},{6,4},{7,5},{8,10},{9,11},{10,... | collective-permute-start | bytes 1572872 | tf_op jit(solution)/shard_map/ppermute | solution.py:275
  434.0 22.4 %collective-permute-start.19 = (bf16[512,512]{1,0:T(8,128)(2,1)S(1)}, bf16[512,512]{1,0:T(8,128)(2,1)S(1)}, u32[]{:S(2)}, u32[]{:S(2)}) collective-permute-start(bf16[512,512]{1,0:T(8,128)(2,1)S(1)} %fusion.5), channel_id=1, source_target_pairs={{0,2},{1,3},{2,0},{3,1},{4,6},{5,7},{6,4},{7,5},{8,10},{9,11},{10,... | collective-permute-start | bytes 1572872 | tf_op jit(solution)/shard_map/ppermute | solution.py:275
  437.4 8.8 %copy-start.4 = (bf16[2,512,512]{2,1,0:T(8,128)(2,1)S(1)}, bf16[2,512,512]{2,1,0:T(8,128)(2,1)}, u32[]{:S(2)}) copy-start(bf16[2,512,512]{2,1,0:T(8,128)(2,1)} %get-tuple-element.48.rest_0_) | copy-start | bytes 3145732
  437.4 8.8 %copy-start.10 = (bf16[2,512,512]{2,1,0:T(8,128)(2,1)S(1)}, bf16[2,512,512]{2,1,0:T(8,128)(2,1)}, u32[]{:S(2)}) copy-start(bf16[2,512,512]{2,1,0:T(8,128)(2,1)} %copy-done.9) | copy-start | bytes 3145732
  437.4 19.0 %copy-start.8 = (bf16[2,512,512]{2,1,0:T(8,128)(2,1)S(1)}, bf16[2,512,512]{2,1,0:T(8,128)(2,1)}, u32[]{:S(2)}) copy-start(bf16[2,512,512]{2,1,0:T(8,128)(2,1)} %get-tuple-element.52) | copy-start | bytes 3145732
  457.7 1.3 copy-start.6
